TPU v7x, 128 devices: a whole 4x4x4 slice. The times are simulated.
128 devices in a mesh: dp: 2 (over core), row: 8 (over y, x_hi), col: 8 (over z, x_lo).
Axes of the slice: x: 4 (x_hi: 2, x_lo: 2; x = x_hi * 2 + x_lo), y: 4, z: 4, core: 2. Of those that a mesh axis runs over, the one named last changes fastest.
Arguments:
- context: bfloat16 [2048, 8192], P(('dp', 'col'), 'row'), may hold values from -6 to 6
- out_weight: bfloat16 [8192, 8192], P('row', 'col'), may hold values from -0.0625 to 0.0625
- up_weight: bfloat16 [8192, 14336], P('col', 'row'), may hold values from -0.0625 to 0.0625
- down_weight: bfloat16 [14336, 8192], P('row', 'col'), may hold values from -0.046875 to 0.046875
- cotangent: bfloat16 [2048, 8192], P(('dp', 'row'), 'col'), may hold values from -6 to 6
- masked_pos: int32 [16, 20], P(('dp', 'row')), may hold values from 0 to 127, as said below
Outputs:
- block_out: bfloat16 [2048, 8192], P(('dp', 'row'), 'col')
- context_grad: bfloat16 [2048, 8192], P(('dp', 'col'), 'row')
- out_grad: bfloat16 [8192, 8192], P('row', 'col')
- up_grad: bfloat16 [8192, 14336], P('col', 'row')
- down_grad: bfloat16 [14336, 8192], P('row', 'col')
Inputs may be any that keep to these rules, and one draw needn't show every extreme that they name: `masked_pos`: each row names 20 different token positions of one sequence.
All inputs are finite; a program needn't handle non-finite values.
Results may differ from a plain program's by a relative error of at most 0.035.
Values may be sent and summed in bfloat16 or wider, within the bound.
No kernel may reach another device: no remote copies, remote signals or barrier semaphores. Data moves between devices by JAX's collectives and lax.ppermute only.
A program may use at most 192 MiB of HBM per device.

v0:
```python
import jax
import jax.numpy as jnp
from jax import lax
from jax.sharding import PartitionSpec as P

SEQ = 128


coef = 0.7978845608
cubic = 0.044715


def gelu(value):
    inner = jnp.tanh(coef * (value + cubic * value * value * value))
    return 0.5 * value * (1.0 + inner)


def gelu_slope(value):
    inner = jnp.tanh(coef * (value + cubic * value * value * value))
    return 0.5 * (1.0 + inner) + 0.5 * value * (1.0 - inner * inner) * coef * (
        1.0 + 3.0 * cubic * value * value
    )


def col_gather(values):
    return lax.all_gather(values, "col", axis=0, tiled=True)


def row_gather(values):
    return lax.all_gather(values, "row", axis=0, tiled=True)


def row_total(left, weight, contract):
    return lax.psum_scatter(
        lax.dot_general(
            left, weight, (((1,), (contract,)), ((), ())), preferred_element_type=jnp.float32
        ).astype(jnp.bfloat16),
        "row",
        scatter_dimension=0,
        tiled=True,
    ).astype(jnp.float32)


def col_total(left, weight, contract):
    return lax.psum_scatter(
        lax.dot_general(
            left, weight, (((1,), (contract,)), ((), ())), preferred_element_type=jnp.float32
        ).astype(jnp.bfloat16),
        "col",
        scatter_dimension=0,
        tiled=True,
    ).astype(jnp.float32)


def token_product(left, right):
    return lax.dot_general(
        left, right, (((0,), (0,)), ((), ())), preferred_element_type=jnp.float32
    )


def body(context, out_weight, up_weight, down_weight, cotangent, masked_pos):
    ctx_full = col_gather(context)
    projected = row_total(ctx_full, out_weight, 0).astype(jnp.bfloat16)
    proj_full = row_gather(projected)
    pre_act = col_total(proj_full, up_weight, 0).astype(jnp.bfloat16)
    pre_float = pre_act.astype(jnp.float32)
    act = gelu(pre_float).astype(jnp.bfloat16)
    act_full = col_gather(act)
    block_out = row_total(act_full, down_weight, 0).astype(jnp.bfloat16)
    places = jnp.arange(SEQ, dtype=jnp.int32)
    keep = (
        jnp.any(masked_pos[:, :, None] == places[None, None, :], axis=1)
        .astype(jnp.float32)
        .reshape(-1)
    )
    grad_out = (cotangent.astype(jnp.float32) * keep[:, None]).astype(jnp.bfloat16)
    grad_full = row_gather(grad_out)
    grad_act = col_total(grad_full, down_weight, 1)
    grad_hidden = (grad_act * gelu_slope(pre_float)).astype(jnp.bfloat16)
    hidden_full = col_gather(grad_hidden)
    grad_proj = row_total(hidden_full, up_weight, 1).astype(jnp.bfloat16)
    gproj_full = row_gather(grad_proj)
    context_grad = col_total(gproj_full, out_weight, 1).astype(jnp.bfloat16)
    sums = (
        lax.psum(token_product(ctx_full, gproj_full).astype(jnp.bfloat16), "dp").astype(
            jnp.float32
        ),
        lax.psum(token_product(proj_full, hidden_full).astype(jnp.bfloat16), "dp").astype(
            jnp.float32
        ),
        lax.psum(token_product(act_full, grad_full).astype(jnp.bfloat16), "dp").astype(jnp.float32),
    )
    out_grad = sums[0].astype(jnp.bfloat16)
    up_grad = sums[1].astype(jnp.bfloat16)
    down_grad = sums[2].astype(jnp.bfloat16)
    return (block_out, context_grad, out_grad, up_grad, down_grad)


def solution(mesh):
    placed = (
        P(("dp", "col"), "row"),
        P("row", "col"),
        P("col", "row"),
        P("row", "col"),
        P(("dp", "row"), "col"),
        P(("dp", "row"), None),
    )
    return jax.shard_map(
        body,
        mesh=mesh,
        in_specs=placed,
        out_specs=(
            P(("dp", "row"), "col"),
            P(("dp", "col"), "row"),
            P("row", "col"),
            P("col", "row"),
            P("row", "col"),
        ),
        check_vma=False,
    )
```

profile of v0, /device:TPU:0, one launch (start us, length us, event | category | flops | bytes accessed | tf_op | source)
XLA Modules:
  0.0 923.8 jit_solution(9392140225219248487)
XLA Ops:
  8.0 56.5 %all-gather.7.cloned.1.call-done = bf16[1024,1024]{1,0:T(8,128)(2,1)} async-done(((bf16[128,1024]{1,0:T(8,128)(2,1)}), bf16[1024,1024]{1,0:T(8,128)(2,1)}) %all-gather.7.cloned.1.call-update) | async-done | bytes 2097168 | tf_op jit(solution)/shard_map/all_gather | solution.py:26
  64.5 5.2 convolution_convert_fusion.7
  70.8 73.2 %reduce-scatter.7.cloned.1.call-done = bf16[128,1024]{1,0:T(8,128)(2,1)} async-done(((bf16[1024,1024]{1,0:T(8,128)(2,1)}), bf16[128,1024]{1,0:T(8,128)(2,1)}) %reduce-scatter.7.cloned.1.call-update) | async-done | bytes 262160 | tf_op jit(solution)/shard_map/reduce_scatter | solution.py:34
  144.0 55.6 %all-gather.13.cloned.1.call-done = bf16[1024,1024]{1,0:T(8,128)(2,1)} async-done(((bf16[128,1024]{1,0:T(8,128)(2,1)}), bf16[1024,1024]{1,0:T(8,128)(2,1)}) %all-gather.13.cloned.1.call-update) | async-done | bytes 2097168 | tf_op jit(solution)/shard_map/all_gather | solution.py:30
  199.6 8.5 convolution_convert_fusion.2
  208.2 45.4 %all-gather.9.cloned.1.call-done = bf16[1024,1024]{1,0:T(8,128)(2,1)} async-done(((bf16[128,1024]{1,0:T(8,128)(2,1)}), bf16[1024,1024]{1,0:T(8,128)(2,1)}) %all-gather.9.cloned.1.call-update) | async-done | bytes 2097168 | tf_op jit(solution)/shard_map/all_gather | solution.py:30
  253.6 8.5 convolution_convert_fusion.3
  262.2 73.9 %reduce-scatter.13.cloned.1.call-done = bf16[128,1792]{1,0:T(8,128)(2,1)} async-done(((bf16[1024,1792]{1,0:T(8,128)(2,1)}), bf16[128,1792]{1,0:T(8,128)(2,1)}) %reduce-scatter.13.cloned.1.call-update) | async-done | bytes 458768 | tf_op jit(solution)/shard_map/reduce_scatter | solution.py:45
  336.1 84.3 %reduce-scatter.9.cloned.1.call-done = bf16[128,1792]{1,0:T(8,128)(2,1)} async-done(((bf16[1024,1792]{1,0:T(8,128)(2,1)}), bf16[128,1792]{1,0:T(8,128)(2,1)}) %reduce-scatter.9.cloned.1.call-update) | async-done | bytes 458768 | tf_op jit(solution)/shard_map/reduce_scatter | solution.py:45
  423.2 81.1 %all-gather.15.cloned.1.call-done = bf16[1024,1792]{1,0:T(8,128)(2,1)} async-done(((bf16[128,1792]{1,0:T(8,128)(2,1)}), bf16[1024,1792]{1,0:T(8,128)(2,1)}) %all-gather.15.cloned.1.call-update) | async-done | bytes 3670032 | tf_op jit(solution)/shard_map/all_gather | solution.py:26
  504.3 8.5 convolution_convert_fusion.5
  513.6 74.0 %reduce-scatter.15.cloned.1.call-done = bf16[128,1024]{1,0:T(8,128)(2,1)} async-done(((bf16[1024,1024]{1,0:T(8,128)(2,1)}), bf16[128,1024]{1,0:T(8,128)(2,1)}) %reduce-scatter.15.cloned.1.call-update) | async-done | bytes 262160 | tf_op jit(solution)/shard_map/reduce_scatter | solution.py:34
  587.8 8.5 convolution_convert_fusion.1
  596.3 73.6 %all-gather.11.cloned.1.call-done = bf16[1024,1792]{1,0:T(8,128)(2,1)} async-done(((bf16[128,1792]{1,0:T(8,128)(2,1)}), bf16[1024,1792]{1,0:T(8,128)(2,1)}) %all-gather.11.cloned.1.call-update) | async-done | bytes 3670032 | tf_op jit(solution)/shard_map/all_gather | solution.py:26
  669.9 8.6 convolution_convert_fusion
  678.4 47.2 %all-gather.17.cloned.1.call-done = bf16[1024,1024]{1,0:T(8,128)(2,1)} async-done(((bf16[128,1024]{1,0:T(8,128)(2,1)}), bf16[1024,1024]{1,0:T(8,128)(2,1)}) %all-gather.17.cloned.1.call-update) | async-done | bytes 2097168 | tf_op jit(solution)/shard_map/all_gather | solution.py:30
  725.6 5.9 convert_bitcast_fusion
  731.8 8.4 convolution_convert_fusion.6
  740.4 5.8 convolution_convert_fusion.4
  746.2 30.0 %all-reduce.3.cloned.1.call-done = (bf16[1024,1024]{0,1:T(8,128)(2,1)}, bf16[1024,1792]{1,0:T(8,128)(2,1)}, bf16[1792,1024]{1,0:T(8,128)(2,1)}) async-done(((bf16[1024,1024]{0,1:T(8,128)(2,1)}, bf16[1024,1792]{1,0:T(8,128)(2,1)}, bf16[1792,1024]{1,0:T(8,128)(2,1)}), (bf16[1024,1024]{0,1:T(8,128)(2,1)}, bf16[1024,1792]{1,0:T(8,128)(2,1)}, bf16[1792,1024]{1,0:T(8,128)(2,1)})) %all-reduce.3.cloned.1.call-update) | async-done | bytes 9437200 | tf_op jit(solution)/shard_map/psum | solution.py:85
  776.2 3.9 copy.12
  780.1 76.5 %reduce-scatter.11.cloned.1.call-done = bf16[128,1024]{1,0:T(8,128)(2,1)} async-done(((bf16[1024,1024]{1,0:T(8,128)(2,1)}), bf16[128,1024]{1,0:T(8,128)(2,1)}) %reduce-scatter.11.cloned.1.call-update) | async-done | bytes 262160 | tf_op jit(solution)/shard_map/reduce_scatter | solution.py:34
  856.7 54.5 %reduce-scatter.17.cloned.1.call-done = bf16[128,1024]{1,0:T(8,128)(2,1)} async-done(((bf16[1024,1024]{1,0:T(8,128)(2,1)}), bf16[128,1024]{1,0:T(8,128)(2,1)}) %reduce-scatter.17.cloned.1.call-update) | async-done | bytes 262160 | tf_op jit(solution)/shard_map/reduce_scatter | solution.py:45
  911.2 4.3 copy.16
  (39 shorter events, 8.0 us)
Async XLA Ops:
  7.2 57.3 %copy-start = (bf16[1024,1024]{1,0:T(8,128)(2,1)S(1)}, bf16[1024,1024]{1,0:T(8,128)(2,1)}, u32[]{:S(2)}) copy-start(bf16[1024,1024]{1,0:T(8,128)(2,1)} %param.7) | copy-start | bytes 6291460
  7.2 57.3 %all-gather.7.cloned.1.call-start = ((), (), s32[]{:S(2)}) async-start(), calls=%async_computation.6 | async-start | bytes 2359296 | tf_op jit(solution)/shard_map/all_gather | solution.py:26
  7.9 61.9 %copy-start.3 = (s32[1,20]{1,0:T(1,128)S(1)}, s32[1,20]{1,0:T(1,128)}, u32[]{:S(2)}) copy-start(s32[1,20]{1,0:T(1,128)} %param.11) | copy-start | bytes 244
  7.9 62.0 %copy-start.2 = (bf16[128,1024]{1,0:T(8,128)(2,1)S(1)}, bf16[128,1024]{1,0:T(8,128)(2,1)}, u32[]{:S(2)}) copy-start(bf16[128,1024]{1,0:T(8,128)(2,1)} %param.10) | copy-start | bytes 786436
  7.9 136.0 %reduce-scatter.7.cloned.1.call-start = ((), (), s32[]{:S(2)}) async-start(), calls=%async_computation.7 | async-start | bytes 2359296 | tf_op jit(solution)/shard_map/reduce_scatter | solution.py:34
  69.7 129.9 %all-gather.13.cloned.1.call-start = ((), (), s32[]{:S(2)}) async-start(), calls=%async_computation.12 | async-start | bytes 2359296 | tf_op jit(solution)/shard_map/all_gather | solution.py:30
  70.7 182.9 %all-gather.9.cloned.1.call-start = ((), (), s32[]{:S(2)}) async-start(), calls=%async_computation.8 | async-start | bytes 2359296 | tf_op jit(solution)/shard_map/all_gather | solution.py:30
  144.0 192.1 %reduce-scatter.13.cloned.1.call-start = ((), (), s32[]{:S(2)}) async-start(), calls=%async_computation.13 | async-start | bytes 4128768 | tf_op jit(solution)/shard_map/reduce_scatter | solution.py:45
  208.1 212.3 %reduce-scatter.9.cloned.1.call-start = ((), (), s32[]{:S(2)}) async-start(), calls=%async_computation.9 | async-start | bytes 4128768 | tf_op jit(solution)/shard_map/reduce_scatter | solution.py:45
  262.1 242.2 %all-gather.15.cloned.1.call-start = ((), (), s32[]{:S(2)}) async-start(), calls=%async_computation.14 | async-start | bytes 4128768 | tf_op jit(solution)/shard_map/all_gather | solution.py:26
  423.2 164.4 %reduce-scatter.15.cloned.1.call-start = ((), (), s32[]{:S(2)}) async-start(), calls=%async_computation.15 | async-start | bytes 2359296 | tf_op jit(solution)/shard_map/reduce_scatter | solution.py:34
  512.8 157.1 %all-gather.11.cloned.1.call-start = ((), (), s32[]{:S(2)}) async-start(), calls=%async_computation.10 | async-start | bytes 4128768 | tf_op jit(solution)/shard_map/all_gather | solution.py:26
  513.5 212.1 %all-gather.17.cloned.1.call-start = ((), (), s32[]{:S(2)}) async-start(), calls=%async_computation.16 | async-start | bytes 2359296 | tf_op jit(solution)/shard_map/all_gather | solution.py:30
  587.6 188.7 %all-reduce.3.cloned.1.call-start = ((), (), s32[]{:S(2)}) async-start(), calls=%async_computation.18 | async-start | bytes 18874368 | tf_op jit(solution)/shard_map/psum | solution.py:85
  731.6 125.1 %reduce-scatter.11.cloned.1.call-start = ((), (), s32[]{:S(2)}) async-start(), calls=%async_computation.11 | async-start | bytes 2359296 | tf_op jit(solution)/shard_map/reduce_scatter | solution.py:34
  740.3 170.9 %reduce-scatter.17.cloned.1.call-start = ((), (), s32[]{:S(2)}) async-start(), calls=%async_computation.17 | async-start | bytes 2359296 | tf_op jit(solution)/shard_map/reduce_scatter | solution.py:45
  911.2 4.3 copy-start.1
Sparse Core Ops, SparseCore 0:
  9.7 54.7 all-gather.6
  69.9 74.0 reduce-scatter.6
  146.9 52.6 all-gather.12
  201.8 51.7 all-gather.8
  256.5 79.6 reduce-scatter.12
  338.9 81.3 reduce-scatter.8
  423.3 80.9 all-gather.14
  512.9 74.5 reduce-scatter.14
  589.8 80.0 all-gather.10
  672.1 53.5 all-gather.16
  731.7 44.4 all-reduce.2
  780.4 76.2 reduce-scatter.10
  859.6 51.4 reduce-scatter.16
where the time goes:
time: 925 us; the launch traced here: 924 us
  waiting for transfers between devices  827 us (89%)
  matrix products  67.9 us (7%)
  between operations  14 us (2%)
  local copies, waits for them, and re-layouts  10 us (1%)
    reduce_scatter x3, waiting for transfers between devices, row_total(): lax.psum_scatter(lax.dot_general(left, weight, (((1,), (contract,)), ((),...  224 us
    reduce_scatter x3, waiting for transfers between devices, col_total(): lax.psum_scatter(lax.dot_general(left, weight, (((1,), (contract,)), ((),...  213 us
    all_gather x3, waiting for transfers between devices, col_gather(): return lax.all_gather(values, 'col', axis=0, tiled=True)  211 us
    all_gather x3, waiting for transfers between devices, row_gather(): return lax.all_gather(values, 'row', axis=0, tiled=True)  148 us
    psum x1, waiting for transfers between devices, body(): lax.psum(token_product(ctx_full, gproj_full).astype(jnp.bfloat16), 'dp')  30 us
    dot_general x3, matrix products, token_product(): lax.dot_general(left, right, (((0,), (0,)), ((), ())), preferred_element_...  23 us
    dot_general x3, matrix products, col_total(): lax.dot_general(left, weight, (((1,), (contract,)), ((), ())), preferred_...  22.8 us
    dot_general x3, matrix products, row_total(): lax.dot_general(left, weight, (((1,), (contract,)), ((), ())), preferred_...  22.1 us
  transfers between devices with their start and end apart: 13, of which 13 were waited for; matrix products, arithmetic and copies ran while one was open for 6% of the time, Pallas kernels for 0%

commit v1 on v0

v1 whole, which is shorter than its diff:
```python
import jax
import jax.numpy as jnp
from jax import lax
from jax.sharding import PartitionSpec as P

SEQ = 128
MASKED = 20
HEAD = 32
GROUP = 8

coef = 0.7978845608
cubic = 0.044715


def gelu(value):
    inner = jnp.tanh(coef * (value + cubic * value * value * value))
    return 0.5 * value * (1.0 + inner)


def gelu_slope(value):
    inner = jnp.tanh(coef * (value + cubic * value * value * value))
    return 0.5 * (1.0 + inner) + 0.5 * value * (1.0 - inner * inner) * coef * (
        1.0 + 3.0 * cubic * value * value
    )


def gather(values, axis):
    rows, width = values.shape
    copies = jnp.broadcast_to(values[None], (GROUP, rows, width))
    return lax.all_to_all(copies, axis, 0, 0).reshape(GROUP * rows, width)


def scatter_sum(partial, axis):
    rows, width = partial.shape
    blocks = partial.reshape(GROUP, rows // GROUP, width)
    return jnp.sum(lax.all_to_all(blocks, axis, 0, 0).astype(jnp.float32), axis=0)


def product(left, weight, contract):
    return lax.dot_general(
        left, weight, (((1,), (contract,)), ((), ())), preferred_element_type=jnp.float32
    ).astype(jnp.bfloat16)


def select(matrix, values, contract):
    return lax.dot_general(
        matrix, values, (((contract,), (0,)), ((), ())), preferred_element_type=jnp.float32
    ).astype(jnp.bfloat16)


def selectors(positions):
    places = jnp.arange(SEQ, dtype=jnp.int32)
    index = positions.reshape(MASKED, 1)
    order = jnp.arange(MASKED, dtype=jnp.int32)[:, None]
    hit = index == places[None, :]
    masked = jnp.any(hit, axis=0)
    own = jnp.sum(jnp.where(hit, order, 0), axis=0)
    before = jnp.sum((index < places[None, :]).astype(jnp.int32), axis=0)
    slot = jnp.where(masked, own, MASKED + places - before)
    full = places[:, None] == slot[None, :]
    head = full[:HEAD] & masked[None, :]
    return full.astype(jnp.bfloat16), head.astype(jnp.bfloat16)


def forward(values, out_weight, up_weight, down_weight):
    ctx_full = gather(values, "col")
    projected = scatter_sum(product(ctx_full, out_weight, 0), "row").astype(jnp.bfloat16)
    proj_full = gather(projected, "row")
    pre_act = scatter_sum(product(proj_full, up_weight, 0), "col").astype(jnp.bfloat16)
    act = gelu(pre_act.astype(jnp.float32)).astype(jnp.bfloat16)
    act_full = gather(act, "col")
    block_out = scatter_sum(product(act_full, down_weight, 0), "row").astype(jnp.bfloat16)
    return ctx_full, proj_full, pre_act, act_full, block_out


def both_replicas(values, first):
    other = lax.ppermute(values, "dp", [(0, 1), (1, 0)])
    return jnp.concatenate(
        [jnp.where(first, values, other), jnp.where(first, other, values)], axis=0
    )


def token_product(left, right):
    return lax.dot_general(
        left, right, (((0,), (0,)), ((), ())), preferred_element_type=jnp.float32
    ).astype(jnp.bfloat16)


def body(context, out_weight, up_weight, down_weight, cotangent, masked_pos):
    crossed = [(r * GROUP + c, c * GROUP + r) for r in range(GROUP) for c in range(GROUP)]
    col_pos = lax.ppermute(masked_pos, ("row", "col"), crossed)
    row_full, row_head = selectors(masked_pos)
    col_full, col_head = selectors(col_pos)
    first = lax.axis_index("dp") == 0

    arranged = select(col_full, context, 1)
    ctx_full, proj_full, pre_act, act_full, head_out = forward(
        arranged[:HEAD], out_weight, up_weight, down_weight
    )
    grad_out = select(row_head, cotangent, 1)
    grad_full = gather(grad_out, "row")
    grad_act = scatter_sum(product(grad_full, down_weight, 1), "col")
    grad_hidden = (grad_act * gelu_slope(pre_act.astype(jnp.float32))).astype(jnp.bfloat16)
    hidden_full = gather(grad_hidden, "col")
    grad_proj = scatter_sum(product(hidden_full, up_weight, 1), "row").astype(jnp.bfloat16)
    gproj_full = gather(grad_proj, "row")
    grad_ctx = scatter_sum(product(gproj_full, out_weight, 1), "col").astype(jnp.bfloat16)
    context_grad = select(col_head, grad_ctx, 0)

    tail_out = forward(arranged[HEAD:], out_weight, up_weight, down_weight)[4]
    block_out = select(row_full, jnp.concatenate([head_out, tail_out], axis=0), 0)

    out_grad = token_product(both_replicas(ctx_full, first), both_replicas(gproj_full, first))
    up_grad = token_product(both_replicas(proj_full, first), both_replicas(hidden_full, first))
    down_grad = token_product(both_replicas(act_full, first), both_replicas(grad_full, first))
    return (block_out, context_grad, out_grad, up_grad, down_grad)


def solution(mesh):
    placed = (
        P(("dp", "col"), "row"),
        P("row", "col"),
        P("col", "row"),
        P("row", "col"),
        P(("dp", "row"), "col"),
        P(("dp", "row"), None),
    )
    return jax.shard_map(
        body,
        mesh=mesh,
        in_specs=placed,
        out_specs=(
            P(("dp", "row"), "col"),
            P(("dp", "col"), "row"),
            P("row", "col"),
            P("col", "row"),
            P("row", "col"),
        ),
        check_vma=False,
    )
```

time: 925 us -> 362 us (0.39)
  waiting for transfers between devices: 827 us -> 156 us
  starting transfers between devices: 0.93 us -> 83.4 us
  other arithmetic: 3.67 us -> 33.3 us
  blocking collectives: 0 us -> 15.6 us
  matrix products: 67.9 us -> 52.9 us
  between operations: 14 us -> 1.01 us
    reduce_scatter x6 -> x0, waiting for transfers between devices: 436 us -> none  [the longest x3 224 us: row_total(): lax.psum_scatter(lax.dot_general(left, weight, (((1,), (contract,)), ((),...]
    all_gather x6 -> x0, waiting for transfers between devices: 359 us -> none  [the longest x3 211 us: col_gather(): return lax.all_gather(values, 'col', axis=0, tiled=True)]
    all_to_all x0 -> x17, waiting for transfers between devices: none -> 155 us  [the longest x8 78.6 us: gather(): return lax.all_to_all(copies, axis, 0, 0).reshape(GROUP * rows, width)]
    all_to_all x0 -> x17, starting transfers between devices: none -> 80.3 us  [the longest x8 43.8 us: gather(): return lax.all_to_all(copies, axis, 0, 0).reshape(GROUP * rows, width)]
    psum x1 -> x0, waiting for transfers between devices: 30 us -> none  [body(): lax.psum(token_product(ctx_full, gproj_full).astype(jnp.bfloat16), 'dp')]
    reduce_sum x0 -> x11, other arithmetic: none -> 16.1 us  [the longest x9 15.2 us: scatter_sum(): jnp.sum(lax.all_to_all(blocks, axis, 0, 0).astype(jnp.float32), axis=0)]
    all_to_all x0 -> x1, blocking collectives: none -> 15.6 us  [gather(): return lax.all_to_all(copies, axis, 0, 0).reshape(GROUP * rows, width)]
    broadcast_in_dim x0 -> x9, local copies, waits for them, and re-layouts: none -> 13.4 us  [gather(): copies = jnp.broadcast_to(values[None], (GROUP, rows, width))]
  transfers between devices with their start and end apart: 13 -> 24, of which waited for: 13 -> 18; matrix products, arithmetic and copies ran while one was open for 6% -> 23% of each run, Pallas kernels for 0% -> 0%
where the time goes in v1:
time: 362 us; the launch traced here: 360 us
  waiting for transfers between devices  156 us (43%)
  starting transfers between devices  83.4 us (23%)
  matrix products  52.9 us (15%)
  other arithmetic  33.3 us (9%)
  local copies, waits for them, and re-layouts  17.8 us (5%)
  blocking collectives  15.6 us (4%)
    all_to_all x8, waiting for transfers between devices, gather(): return lax.all_to_all(copies, axis, 0, 0).reshape(GROUP * rows, width)  78.6 us
    all_to_all x9, waiting for transfers between devices, scatter_sum(): lax.all_to_all(blocks, axis, 0, 0).astype(jnp.float32)  76.8 us
    all_to_all x8, starting transfers between devices, gather(): return lax.all_to_all(copies, axis, 0, 0).reshape(GROUP * rows, width)  43.8 us
    dot_general x9, matrix products, product(): lax.dot_general(left, weight, (((1,), (contract,)), ((), ())), preferred_...  39.1 us
    all_to_all x9, starting transfers between devices, scatter_sum(): lax.all_to_all(blocks, axis, 0, 0).astype(jnp.float32)  36.4 us
    all_to_all x1, blocking collectives, gather(): return lax.all_to_all(copies, axis, 0, 0).reshape(GROUP * rows, width)  15.6 us
    reduce_sum x9, other arithmetic, scatter_sum(): jnp.sum(lax.all_to_all(blocks, axis, 0, 0).astype(jnp.float32), axis=0)  15.2 us
    broadcast_in_dim x9, local copies, waits for them, and re-layouts, gather(): copies = jnp.broadcast_to(values[None], (GROUP, rows, width))  13.4 us
  transfers between devices with their start and end apart: 24, of which 18 were waited for; matrix products, arithmetic and copies ran while one was open for 23% of the time, Pallas kernels for 0%

profile of v1, /device:TPU:0, one launch (start us, length us, event | category | flops | bytes accessed | tf_op | source)
XLA Modules:
  0.0 359.9 jit_solution(14409714037684932638)
XLA Ops:
  7.5 13.7 %all-to-all-start = ((bf16[8,32,1024]{2,1,0:T(8,128)(2,1)}), bf16[8,32,1024]{2,1,0:T(8,128)(2,1)S(1)}, u32[]{:S(2)}, u32[]{:S(2)}) async-start(bf16[8,32,1024]{2,1,0:T(8,128)(2,1)} %broadcast_in_dim.39), calls=%async_computation | async-start | bytes 1048576 | tf_op jit(solution)/shard_map/all_to_all | solution.py:30
  21.9 8.2 %all-to-all-done = bf16[8,32,1024]{2,1,0:T(8,128)(2,1)S(1)} async-done(((bf16[8,32,1024]{2,1,0:T(8,128)(2,1)}), bf16[8,32,1024]{2,1,0:T(8,128)(2,1)S(1)}, u32[]{:S(2)}, u32[]{:S(2)}) %all-to-all-start) | async-done | bytes 524320 | tf_op jit(solution)/shard_map/all_to_all | solution.py:30
  31.0 4.6 %all-to-all-start.12 = ((bf16[8,32,1024]{2,1,0:T(8,128)(2,1)}), bf16[8,32,1024]{2,1,0:T(8,128)(2,1)S(1)}, u32[]{:S(2)}, u32[]{:S(2)}) async-start(bf16[8,32,1024]{2,1,0:T(8,128)(2,1)} %broadcast_in_dim.45), calls=%async_computation.12 | async-start | bytes 1048576 | tf_op jit(solution)/shard_map/all_to_all | solution.py:30
  37.1 8.7 %all-to-all-done.12 = bf16[8,32,1024]{2,1,0:T(8,128)(2,1)S(1)} async-done(((bf16[8,32,1024]{2,1,0:T(8,128)(2,1)}), bf16[8,32,1024]{2,1,0:T(8,128)(2,1)S(1)}, u32[]{:S(2)}, u32[]{:S(2)}) %all-to-all-start.12) | async-done | bytes 524320 | tf_op jit(solution)/shard_map/all_to_all | solution.py:30
  54.0 6.1 %all-to-all-done.1 = bf16[8,32,1024]{2,1,0:T(8,128)(2,1)} async-done(((bf16[8,32,1024]{2,1,0:T(8,128)(2,1)}), bf16[8,32,1024]{2,1,0:T(8,128)(2,1)}, u32[]{:S(2)}, u32[]{:S(2)}) %all-to-all-start.1) | async-done | bytes 524320 | tf_op jit(solution)/shard_map/all_to_all | solution.py:36
  65.4 9.0 %all-to-all-done.13 = bf16[8,32,1792]{2,1,0:T(8,128)(2,1)S(1)} async-done(((bf16[8,32,1792]{2,1,0:T(8,128)(2,1)}), bf16[8,32,1792]{2,1,0:T(8,128)(2,1)S(1)}, u32[]{:S(2)}, u32[]{:S(2)}) %all-to-all-start.13) | async-done | bytes 917536 | tf_op jit(solution)/shard_map/all_to_all | solution.py:36
  82.0 8.6 %all-to-all-done.2 = bf16[8,32,1024]{2,1,0:T(8,128)(2,1)} async-done(((bf16[8,32,1024]{2,1,0:T(8,128)(2,1)}), bf16[8,32,1024]{2,1,0:T(8,128)(2,1)}, u32[]{:S(2)}, u32[]{:S(2)}) %all-to-all-start.2) | async-done | bytes 524320 | tf_op jit(solution)/shard_map/all_to_all | solution.py:30
  101.4 11.6 %all-to-all-done.6 = bf16[8,96,1024]{2,1,0:T(8,128)(2,1)} async-done(((bf16[8,96,1024]{2,1,0:T(8,128)(2,1)}), bf16[8,96,1024]{2,1,0:T(8,128)(2,1)}, u32[]{:S(2)}, u32[]{:S(2)}) %all-to-all-start.6) | async-done | bytes 1572896 | tf_op jit(solution)/shard_map/all_to_all | solution.py:30
  116.5 4.3 %convolution_convert_fusion.7 = bf16[768,1024]{1,0:T(8,128)(2,1)} fusion(bf16[768,1024]{1,0:T(8,128)(2,1)} %bitcast.8, bf16[1024,1024]{1,0:T(8,128)(2,1)S(1)} %copy-done), kind=kOutput, calls=%fused_computation.14 | convolution fusion | flops 1611399168 | bytes 5242880 | tf_op jit(solution)/shard_map/dot_general | solution.py:40
  120.8 8.5 %all-to-all-done.3 = bf16[8,32,1792]{2,1,0:T(8,128)(2,1)S(1)} async-done(((bf16[8,32,1792]{2,1,0:T(8,128)(2,1)}), bf16[8,32,1792]{2,1,0:T(8,128)(2,1)S(1)}, u32[]{:S(2)}, u32[]{:S(2)}) %all-to-all-start.3) | async-done | bytes 917536 | tf_op jit(solution)/shard_map/all_to_all | solution.py:36
  138.3 16.1 %all-to-all-done.7 = bf16[8,96,1024]{2,1,0:T(8,128)(2,1)} async-done(((bf16[8,96,1024]{2,1,0:T(8,128)(2,1)}), bf16[8,96,1024]{2,1,0:T(8,128)(2,1)}, u32[]{:S(2)}, u32[]{:S(2)}) %all-to-all-start.7) | async-done | bytes 1572896 | tf_op jit(solution)/shard_map/all_to_all | solution.py:36
  154.5 15.6 %all_to_all.90 = bf16[8,32,1792]{2,1,0:T(8,128)(2,1)S(1)} all-to-all(bf16[8,32,1792]{2,1,0:T(8,128)(2,1)S(1)} %broadcast_in_dim.41), channel_id=1, replica_groups=mesh['dp'=2,'row'=8,'col'=8] {'col'}, dimensions={0} | all-to-all | bytes 1835008 | tf_op jit(solution)/shard_map/all_to_all | solution.py:30
  177.7 13.4 %all-to-all-done.14 = bf16[8,32,1792]{2,1,0:T(8,128)(2,1)} async-done(((bf16[8,32,1792]{2,1,0:T(8,128)(2,1)}), bf16[8,32,1792]{2,1,0:T(8,128)(2,1)}, u32[]{:S(2)}, u32[]{:S(2)}) %all-to-all-start.14) | async-done | bytes 917536 | tf_op jit(solution)/shard_map/all_to_all | solution.py:30
  201.9 12.8 %all-to-all-done.8 = bf16[8,96,1024]{2,1,0:T(8,128)(2,1)} async-done(((bf16[8,96,1024]{2,1,0:T(8,128)(2,1)}), bf16[8,96,1024]{2,1,0:T(8,128)(2,1)}, u32[]{:S(2)}, u32[]{:S(2)}) %all-to-all-start.8) | async-done | bytes 1572896 | tf_op jit(solution)/shard_map/all_to_all | solution.py:30
  218.9 7.1 %convolution_convert_fusion.2 = bf16[768,1792]{1,0:T(8,128)(2,1)} fusion(bf16[768,1024]{1,0:T(8,128)(2,1)} %bitcast.10, bf16[1024,1792]{1,0:T(8,128)(2,1)} %param.8), kind=kOutput, calls=%fused_computation.2 | convolution fusion | flops 2819948544 | bytes 7995392 | tf_op jit(solution)/shard_map/dot_general | solution.py:40
  225.9 6.0 %all-to-all-done.15 = bf16[8,32,1024]{2,1,0:T(8,128)(2,1)} async-done(((bf16[8,32,1024]{2,1,0:T(8,128)(2,1)}), bf16[8,32,1024]{2,1,0:T(8,128)(2,1)}, u32[]{:S(2)}, u32[]{:S(2)}) %all-to-all-start.15) | async-done | bytes 524320 | tf_op jit(solution)/shard_map/all_to_all | solution.py:36
  231.9 4.4 %all-to-all-start.9 = ((bf16[8,96,1792]{2,1,0:T(8,128)(2,1)}), bf16[8,96,1792]{2,1,0:T(8,128)(2,1)}, u32[]{:S(2)}, u32[]{:S(2)}) async-start(bf16[8,96,1792]{2,1,0:T(8,128)(2,1)} %bitcast.55), calls=%async_computation.9 | async-start | bytes 5505024 | tf_op jit(solution)/shard_map/all_to_all | solution.py:36
  240.3 18.4 %all-to-all-done.9 = bf16[8,96,1792]{2,1,0:T(8,128)(2,1)} async-done(((bf16[8,96,1792]{2,1,0:T(8,128)(2,1)}), bf16[8,96,1792]{2,1,0:T(8,128)(2,1)}, u32[]{:S(2)}, u32[]{:S(2)}) %all-to-all-start.9) | async-done | bytes 2752544 | tf_op jit(solution)/shard_map/all_to_all | solution.py:36
  267.8 5.5 %all-to-all-done.5 = bf16[8,32,1024]{2,1,0:T(8,128)(2,1)} async-done(((bf16[8,32,1024]{2,1,0:T(8,128)(2,1)}), bf16[8,32,1024]{2,1,0:T(8,128)(2,1)}, u32[]{:S(2)}, u32[]{:S(2)}) %all-to-all-start.5) | async-done | bytes 524320 | tf_op jit(solution)/shard_map/all_to_all | solution.py:36
  281.1 11.1 %all-to-all-done.16 = bf16[8,32,1024]{2,1,0:T(8,128)(2,1)} async-done(((bf16[8,32,1024]{2,1,0:T(8,128)(2,1)}), bf16[8,32,1024]{2,1,0:T(8,128)(2,1)}, u32[]{:S(2)}, u32[]{:S(2)}) %all-to-all-start.16) | async-done | bytes 524320 | tf_op jit(solution)/shard_map/all_to_all | solution.py:30
  294.9 4.4 %all-to-all-start.10 = ((bf16[8,96,1792]{2,1,0:T(8,128)(2,1)}), bf16[8,96,1792]{2,1,0:T(8,128)(2,1)}, u32[]{:S(2)}, u32[]{:S(2)}) async-start(bf16[8,96,1792]{2,1,0:T(8,128)(2,1)} %broadcast_in_dim.44), calls=%async_computation.10 | async-start | bytes 5505024 | tf_op jit(solution)/shard_map/all_to_all | solution.py:30
  323.5 7.0 %convolution_convert_fusion.6 = bf16[768,1024]{1,0:T(8,128)(2,1)} fusion(bf16[768,1792]{1,0:T(8,128)(2,1)} %bitcast.12, bf16[1792,1024]{1,0:T(8,128)(2,1)} %param.9), kind=kOutput, calls=%fused_computation.13 | convolution fusion | flops 2819358720 | bytes 7995392 | tf_op jit(solution)/shard_map/dot_general | solution.py:40
  332.4 4.5 %all-to-all-start.11 = ((bf16[8,96,1024]{2,1,0:T(8,128)(2,1)}), bf16[8,96,1024]{2,1,0:T(8,128)(2,1)}, u32[]{:S(2)}, u32[]{:S(2)}) async-start(bf16[8,96,1024]{2,1,0:T(8,128)(2,1)} %bitcast.60), calls=%async_computation.11 | async-start | bytes 3145728 | tf_op jit(solution)/shard_map/all_to_all | solution.py:36
  351.9 5.3 %all-to-all-done.11 = bf16[8,96,1024]{2,1,0:T(8,128)(2,1)} async-done(((bf16[8,96,1024]{2,1,0:T(8,128)(2,1)}), bf16[8,96,1024]{2,1,0:T(8,128)(2,1)}, u32[]{:S(2)}, u32[]{:S(2)}) %all-to-all-start.11) | async-done | bytes 1572896 | tf_op jit(solution)/shard_map/all_to_all | solution.py:36
  (117 shorter events, 143.9 us)
Async XLA Ops:
  0.7 2.9 collective-permute-start
  7.5 22.7 %all-to-all-start = ((bf16[8,32,1024]{2,1,0:T(8,128)(2,1)}), bf16[8,32,1024]{2,1,0:T(8,128)(2,1)S(1)}, u32[]{:S(2)}, u32[]{:S(2)}) async-start(bf16[8,32,1024]{2,1,0:T(8,128)(2,1)} %broadcast_in_dim.39), calls=%async_computation | async-start | bytes 1048576 | tf_op jit(solution)/shard_map/all_to_all | solution.py:30
  31.0 14.8 %all-to-all-start.12 = ((bf16[8,32,1024]{2,1,0:T(8,128)(2,1)}), bf16[8,32,1024]{2,1,0:T(8,128)(2,1)S(1)}, u32[]{:S(2)}, u32[]{:S(2)}) async-start(bf16[8,32,1024]{2,1,0:T(8,128)(2,1)} %broadcast_in_dim.45), calls=%async_computation.12 | async-start | bytes 1048576 | tf_op jit(solution)/shard_map/all_to_all | solution.py:30
  45.8 14.4 %all-to-all-start.1 = ((bf16[8,32,1024]{2,1,0:T(8,128)(2,1)}), bf16[8,32,1024]{2,1,0:T(8,128)(2,1)}, u32[]{:S(2)}, u32[]{:S(2)}) async-start(bf16[8,32,1024]{2,1,0:T(8,128)(2,1)} %bitcast.67), calls=%async_computation.1 | async-start | bytes 1048576 | tf_op jit(solution)/shard_map/all_to_all | solution.py:36
  60.1 14.3 %all-to-all-start.13 = ((bf16[8,32,1792]{2,1,0:T(8,128)(2,1)}), bf16[8,32,1792]{2,1,0:T(8,128)(2,1)S(1)}, u32[]{:S(2)}, u32[]{:S(2)}) async-start(bf16[8,32,1792]{2,1,0:T(8,128)(2,1)} %bitcast.62), calls=%async_computation.13 | async-start | bytes 1835008 | tf_op jit(solution)/shard_map/all_to_all | solution.py:36
  76.2 14.4 %all-to-all-start.2 = ((bf16[8,32,1024]{2,1,0:T(8,128)(2,1)}), bf16[8,32,1024]{2,1,0:T(8,128)(2,1)}, u32[]{:S(2)}, u32[]{:S(2)}) async-start(bf16[8,32,1024]{2,1,0:T(8,128)(2,1)} %broadcast_in_dim.40), calls=%async_computation.2 | async-start | bytes 1048576 | tf_op jit(solution)/shard_map/all_to_all | solution.py:30
  92.8 20.1 %all-to-all-start.6 = ((bf16[8,96,1024]{2,1,0:T(8,128)(2,1)}), bf16[8,96,1024]{2,1,0:T(8,128)(2,1)}, u32[]{:S(2)}, u32[]{:S(2)}) async-start(bf16[8,96,1024]{2,1,0:T(8,128)(2,1)} %broadcast_in_dim.42), calls=%async_computation.6 | async-start | bytes 3145728 | tf_op jit(solution)/shard_map/all_to_all | solution.py:30
  112.9 16.4 %all-to-all-start.3 = ((bf16[8,32,1792]{2,1,0:T(8,128)(2,1)}), bf16[8,32,1792]{2,1,0:T(8,128)(2,1)S(1)}, u32[]{:S(2)}, u32[]{:S(2)}) async-start(bf16[8,32,1792]{2,1,0:T(8,128)(2,1)} %bitcast.63), calls=%async_computation.3 | async-start | bytes 1835008 | tf_op jit(solution)/shard_map/all_to_all | solution.py:36
  129.3 25.0 %all-to-all-start.7 = ((bf16[8,96,1024]{2,1,0:T(8,128)(2,1)}), bf16[8,96,1024]{2,1,0:T(8,128)(2,1)}, u32[]{:S(2)}, u32[]{:S(2)}) async-start(bf16[8,96,1024]{2,1,0:T(8,128)(2,1)} %bitcast.61), calls=%async_computation.7 | async-start | bytes 3145728 | tf_op jit(solution)/shard_map/all_to_all | solution.py:36
  171.0 20.0 %all-to-all-start.14 = ((bf16[8,32,1792]{2,1,0:T(8,128)(2,1)}), bf16[8,32,1792]{2,1,0:T(8,128)(2,1)}, u32[]{:S(2)}, u32[]{:S(2)}) async-start(bf16[8,32,1792]{2,1,0:T(8,128)(2,1)} %broadcast_in_dim.46), calls=%async_computation.14 | async-start | bytes 1835008 | tf_op jit(solution)/shard_map/all_to_all | solution.py:30
  193.3 21.4 %all-to-all-start.8 = ((bf16[8,96,1024]{2,1,0:T(8,128)(2,1)}), bf16[8,96,1024]{2,1,0:T(8,128)(2,1)}, u32[]{:S(2)}, u32[]{:S(2)}) async-start(bf16[8,96,1024]{2,1,0:T(8,128)(2,1)} %broadcast_in_dim.43), calls=%async_computation.8 | async-start | bytes 3145728 | tf_op jit(solution)/shard_map/all_to_all | solution.py:30
  214.7 17.2 %all-to-all-start.15 = ((bf16[8,32,1024]{2,1,0:T(8,128)(2,1)}), bf16[8,32,1024]{2,1,0:T(8,128)(2,1)}, u32[]{:S(2)}, u32[]{:S(2)}) async-start(bf16[8,32,1024]{2,1,0:T(8,128)(2,1)} %bitcast.65), calls=%async_computation.15 | async-start | bytes 1048576 | tf_op jit(solution)/shard_map/all_to_all | solution.py:36
  231.9 26.8 %all-to-all-start.9 = ((bf16[8,96,1792]{2,1,0:T(8,128)(2,1)}), bf16[8,96,1792]{2,1,0:T(8,128)(2,1)}, u32[]{:S(2)}, u32[]{:S(2)}) async-start(bf16[8,96,1792]{2,1,0:T(8,128)(2,1)} %bitcast.55), calls=%async_computation.9 | async-start | bytes 5505024 | tf_op jit(solution)/shard_map/all_to_all | solution.py:36
  258.7 14.5 %all-to-all-start.5 = ((bf16[8,32,1024]{2,1,0:T(8,128)(2,1)}), bf16[8,32,1024]{2,1,0:T(8,128)(2,1)}, u32[]{:S(2)}, u32[]{:S(2)}) async-start(bf16[8,32,1024]{2,1,0:T(8,128)(2,1)} %bitcast.64), calls=%async_computation.5 | async-start | bytes 1048576 | tf_op jit(solution)/shard_map/all_to_all | solution.py:36
  275.0 17.2 %all-to-all-start.16 = ((bf16[8,32,1024]{2,1,0:T(8,128)(2,1)}), bf16[8,32,1024]{2,1,0:T(8,128)(2,1)}, u32[]{:S(2)}, u32[]{:S(2)}) async-start(bf16[8,32,1024]{2,1,0:T(8,128)(2,1)} %broadcast_in_dim.47), calls=%async_computation.16 | async-start | bytes 1048576 | tf_op jit(solution)/shard_map/all_to_all | solution.py:30
  294.9 25.1 %all-to-all-start.10 = ((bf16[8,96,1792]{2,1,0:T(8,128)(2,1)}), bf16[8,96,1792]{2,1,0:T(8,128)(2,1)}, u32[]{:S(2)}, u32[]{:S(2)}) async-start(bf16[8,96,1792]{2,1,0:T(8,128)(2,1)} %broadcast_in_dim.44), calls=%async_computation.10 | async-start | bytes 5505024 | tf_op jit(solution)/shard_map/all_to_all | solution.py:30
  299.3 2.3 collective-permute-start.6
  299.4 4.5 %collective-permute-start.1 = (bf16[256,1024]{1,0:T(8,128)(2,1)S(1)}, bf16[256,1024]{1,0:T(8,128)(2,1)}, u32[]{:S(2)}, u32[]{:S(2)}) collective-permute-start(bf16[256,1024]{1,0:T(8,128)(2,1)S(1)} %bitcast.57), channel_id=1, source_target_pairs={{0,64},{64,0},{1,65},{65,1},{2,66},{66,2},{3,67},{67,3},{4,68},{68... | collective-permute-start | bytes 1572872 | tf_op jit(solution)/shard_map/ppermute | solution.py:77
  299.9 10.5 %collective-permute-start.4 = (bf16[256,1792]{1,0:T(8,128)(2,1)}, bf16[256,1792]{1,0:T(8,128)(2,1)}, u32[]{:S(2)}, u32[]{:S(2)}) collective-permute-start(bf16[256,1792]{1,0:T(8,128)(2,1)} %bitcast.16), channel_id=1, source_target_pairs={{0,64},{64,0},{1,65},{65,1},{2,66},{66,2},{3,67},{67,3},{4,68},{68... | collective-permute-start | bytes 2752520 | tf_op jit(solution)/shard_map/ppermute | solution.py:77
  300.6 5.4 %collective-permute-start.3 = (bf16[256,1024]{1,0:T(8,128)(2,1)}, bf16[256,1024]{1,0:T(8,128)(2,1)S(1)}, u32[]{:S(2)}, u32[]{:S(2)}) collective-permute-start(bf16[256,1024]{1,0:T(8,128)(2,1)} %bitcast.4), channel_id=1, source_target_pairs={{0,64},{64,0},{1,65},{65,1},{2,66},{66,2},{3,67},{67,3},{4,68},{68... | collective-permute-start | bytes 1572872 | tf_op jit(solution)/shard_map/ppermute | solution.py:77
  308.1 28.8 %collective-permute-start.5 = (bf16[256,1792]{1,0:T(8,128)(2,1)S(1)}, bf16[256,1792]{1,0:T(8,128)(2,1)}, u32[]{:S(2)}, u32[]{:S(2)}) collective-permute-start(bf16[256,1792]{1,0:T(8,128)(2,1)S(1)} %bitcast.54), channel_id=1, source_target_pairs={{0,64},{64,0},{1,65},{65,1},{2,66},{66,2},{3,67},{67,3},{4,68},{68... | collective-permute-start | bytes 2752520 | tf_op jit(solution)/shard_map/ppermute | solution.py:77
  310.0 37.9 %collective-permute-start.2 = (bf16[256,1024]{1,0:T(8,128)(2,1)}, bf16[256,1024]{1,0:T(8,128)(2,1)}, u32[]{:S(2)}, u32[]{:S(2)}) collective-permute-start(bf16[256,1024]{1,0:T(8,128)(2,1)} %bitcast.18), channel_id=1, source_target_pairs={{0,64},{64,0},{1,65},{65,1},{2,66},{66,2},{3,67},{67,3},{4,68},{68... | collective-permute-start | bytes 1572872 | tf_op jit(solution)/shard_map/ppermute | solution.py:77
  320.0 12.4 %all-to-all-start.17 = ((bf16[8,32,1024]{2,1,0:T(8,128)(2,1)}), bf16[8,32,1024]{2,1,0:T(8,128)(2,1)S(1)}, u32[]{:S(2)}, u32[]{:S(2)}) async-start(bf16[8,32,1024]{2,1,0:T(8,128)(2,1)} %bitcast.66), calls=%async_computation.17 | async-start | bytes 1048576 | tf_op jit(solution)/shard_map/all_to_all | solution.py:36
  332.4 24.8 %all-to-all-start.11 = ((bf16[8,96,1024]{2,1,0:T(8,128)(2,1)}), bf16[8,96,1024]{2,1,0:T(8,128)(2,1)}, u32[]{:S(2)}, u32[]{:S(2)}) async-start(bf16[8,96,1024]{2,1,0:T(8,128)(2,1)} %bitcast.60), calls=%async_computation.11 | async-start | bytes 3145728 | tf_op jit(solution)/shard_map/all_to_all | solution.py:36
  (20 other events, 143.5 us)

commit v2 on v1

v2 whole, which is shorter than its diff:
```python
import jax
import jax.numpy as jnp
from jax import lax
from jax.sharding import PartitionSpec as P

SEQ = 128
MASKED = 20
HEAD = 24
GROUP = 8
RING = 4
RINGS = [[0, 2, 4, 6], [1, 3, 5, 7]]
PAIRS = [(i, i ^ 1) for i in range(GROUP)]
CORES = [(0, 1), (1, 0)]

coef = 0.7978845608
cubic = 0.044715


def gelu(value):
    inner = jnp.tanh(coef * (value + cubic * value * value * value))
    return 0.5 * value * (1.0 + inner)


def gelu_slope(value):
    inner = jnp.tanh(coef * (value + cubic * value * value * value))
    return 0.5 * (1.0 + inner) + 0.5 * value * (1.0 - inner * inner) * coef * (
        1.0 + 3.0 * cubic * value * value
    )


def exchange(blocks, axis):
    groups = RINGS if blocks.shape[0] == RING else None
    return lax.all_to_all(blocks, axis, 0, 0, axis_index_groups=groups)


def gather(values, axis, count=GROUP):
    return exchange(jnp.broadcast_to(values[None], (count,) + values.shape), axis)


def scatter_sum(blocks, axis):
    return jnp.sum(exchange(blocks, axis).astype(jnp.float32), axis=0)


def dot(left, right, contract):
    return lax.dot_general(
        left, right, (((1,), (contract,)), ((), ())), preferred_element_type=jnp.float32
    )


def product(left, weight, contract):
    return dot(left, weight, contract).astype(jnp.bfloat16)


def flat(blocks):
    return blocks.reshape(-1, blocks.shape[-1])


def select(matrix, values, contract):
    return lax.dot_general(
        matrix, values, (((contract,), (0,)), ((), ())), preferred_element_type=jnp.float32
    ).astype(jnp.bfloat16)


def select_each(matrix, values):
    return lax.dot_general(
        matrix, values, (((2,), (1,)), ((0,), (0,))), preferred_element_type=jnp.float32
    ).astype(jnp.bfloat16)


def heads(positions):
    places = jnp.arange(SEQ, dtype=jnp.int32)
    short = jnp.pad(
        positions,
        [(0, 0)] * (positions.ndim - 1) + [(0, HEAD - MASKED)],
        constant_values=-1,
    )
    return (short[..., None] == places).astype(jnp.bfloat16)


def neighbour_weight(weight, core, after):
    half = weight.shape[0] // 2
    mine = lax.dynamic_slice_in_dim(weight, core * half, half, 0)
    if after is not None:
        mine = lax.optimization_barrier((mine, after))[0]
    got = lax.ppermute(mine, "col", PAIRS)
    other = lax.ppermute(got, "dp", CORES)
    first = core == 0
    whole = jnp.concatenate(
        [jnp.where(first, got, other), jnp.where(first, other, got)], axis=0
    )
    return whole, got


def interleave(own, other, side):
    even = jnp.stack([own, other], axis=1)
    odd = jnp.stack([other, own], axis=1)
    return jnp.where(side == 0, even, odd).reshape(-1, own.shape[-1])


def both_replicas(values, core):
    other = lax.ppermute(values, "dp", CORES)
    first = core == 0
    return jnp.concatenate(
        [jnp.where(first, values, other), jnp.where(first, other, values)], axis=0
    )


def token_product(left, right, core):
    return lax.dot_general(
        both_replicas(left, core),
        both_replicas(right, core),
        (((0,), (0,)), ((), ())),
        preferred_element_type=jnp.float32,
    ).astype(jnp.bfloat16)


def body(context, out_weight, up_weight, down_weight, cotangent, masked_pos):
    side = lax.axis_index("col") & 1
    core = lax.axis_index("dp")
    live = jnp.arange(HEAD) < MASKED
    crossed = [(r * GROUP + c, c * GROUP + r) for r in range(GROUP) for c in range(GROUP)]
    col_pos = lax.ppermute(masked_pos, ("row", "col"), crossed)

    ctx = gather(context, "col", RING)
    out_near, got = neighbour_weight(out_weight, core, None)
    up_near, got = neighbour_weight(up_weight, core, got)
    down_near, got = neighbour_weight(down_weight, core, got)

    noted = jnp.pad(
        masked_pos.astype(jnp.bfloat16),
        [(MASKED, HEAD - MASKED - 1), (0, cotangent.shape[1] - MASKED)],
    )
    grad_full = gather(select(heads(masked_pos[0]), cotangent, 1) + noted, "row")
    positions = grad_full[:, MASKED, :MASKED].astype(jnp.int32)
    grad_full = flat(jnp.where(live[None, :, None], grad_full, jnp.zeros_like(grad_full)))
    grad_act = lax.psum_scatter(
        product(grad_full, down_weight, 1), "col", scatter_dimension=0, tiled=True
    ).astype(jnp.float32)

    eighth = (GROUP, RING * SEQ // GROUP, context.shape[1])
    proj_own = scatter_sum(product(flat(ctx), out_weight, 0).reshape(eighth), "row")
    proj_near = scatter_sum(product(flat(ctx), out_near, 0).reshape(eighth), "row")
    own_full = flat(gather(proj_own.astype(jnp.bfloat16), "row"))
    near_full = flat(gather(proj_near.astype(jnp.bfloat16), "row"))
    up_part = (dot(own_full, up_weight, 0) + dot(near_full, up_near, 0)).astype(jnp.bfloat16)
    pre_act = scatter_sum(up_part.reshape(RING, SEQ, -1), "col").astype(jnp.bfloat16)
    act = gelu(pre_act.astype(jnp.float32)).astype(jnp.bfloat16)
    col_heads = heads(col_pos[0])
    slope = gelu_slope(select(col_heads, pre_act, 1).astype(jnp.float32))
    grad_hidden = (grad_act * slope).astype(jnp.bfloat16)

    hidden_full = flat(gather(grad_hidden, "col"))
    act_full = gather(act, "col", RING)
    hidden_full, act_full = lax.optimization_barrier((hidden_full, act_full))

    grad_proj = scatter_sum(product(hidden_full, up_weight, 1).reshape(GROUP, HEAD, -1), "row")
    gproj_full = flat(gather(grad_proj.astype(jnp.bfloat16), "row"))
    grad_ctx = scatter_sum(product(gproj_full, out_weight, 1).reshape(GROUP, HEAD, -1), "col")
    context_grad = select(col_heads, grad_ctx.astype(jnp.bfloat16), 0)

    down_part = jnp.stack(
        [
            product(flat(act_full), down_weight, 0).reshape(RING, SEQ, -1),
            product(flat(act_full), down_near, 0).reshape(RING, SEQ, -1),
        ],
        axis=1,
    )
    piece = scatter_sum(down_part.reshape(GROUP, SEQ, -1), "row").astype(jnp.bfloat16)
    moved = [
        (
            (2 * y + h) * GROUP + 2 * z + x,
            (2 * y + x) * GROUP + 2 * z + (h ^ x),
        )
        for y in range(RING)
        for h in range(2)
        for z in range(RING)
        for x in range(2)
    ]
    block_out = lax.ppermute(piece, ("row", "col"), moved)

    by_side = positions.reshape(RING, 2, MASKED)
    ring_heads = heads(jnp.where(side == 0, by_side[:, 0], by_side[:, 1]))
    ctx_own = select_each(ring_heads, ctx)
    ctx_head = interleave(ctx_own, lax.ppermute(ctx_own, "col", PAIRS), side)
    proj_head = interleave(
        select_each(ring_heads, own_full.reshape(RING, SEQ, -1)),
        lax.ppermute(
            select_each(ring_heads, near_full.reshape(RING, SEQ, -1)), "col", PAIRS
        ),
        side,
    )
    act_own = select_each(ring_heads, act_full)
    act_head = interleave(act_own, lax.ppermute(act_own, "col", PAIRS), side)
    out_grad = token_product(ctx_head, gproj_full, core)
    up_grad = token_product(proj_head, hidden_full, core)
    down_grad = token_product(act_head, grad_full, core)
    return (block_out, context_grad, out_grad, up_grad, down_grad)


def solution(mesh):
    placed = (
        P(("dp", "col"), "row"),
        P("row", "col"),
        P("col", "row"),
        P("row", "col"),
        P(("dp", "row"), "col"),
        P(("dp", "row"), None),
    )
    return jax.shard_map(
        body,
        mesh=mesh,
        in_specs=placed,
        out_specs=(
            P(("dp", "row"), "col"),
            P(("dp", "col"), "row"),
            P("row", "col"),
            P("col", "row"),
            P("row", "col"),
        ),
        check_vma=False,
    )
```

time: 362 us -> 372 us (1.028)
  waiting for transfers between devices: 156 us -> 174 us
  blocking collectives: 15.6 us -> 0 us
  starting transfers between devices: 83.4 us -> 68.9 us
  between operations: 1.01 us -> 14.5 us
  matrix products: 52.9 us -> 57.2 us
    ppermute x6 -> x16, waiting for transfers between devices: 0.54 us -> 33.9 us  [the longest x3 31 us: neighbour_weight(): got = lax.ppermute(mine, 'col', PAIRS)]
    all_to_all x17 -> x13, starting transfers between devices: 80.3 us -> 60.9 us  [exchange(): return lax.all_to_all(blocks, axis, 0, 0, axis_index_groups=groups)]
    all_to_all x1 -> x0, blocking collectives: 15.6 us -> none  [gather(): return lax.all_to_all(copies, axis, 0, 0).reshape(GROUP * rows, width)]
    all_to_all x17 -> x13, waiting for transfers between devices: 155 us -> 140 us  [exchange(): return lax.all_to_all(blocks, axis, 0, 0, axis_index_groups=groups)]
    select_n x2 -> x8, other arithmetic: 0.01 us -> 13.4 us  [the longest x3 9.94 us: neighbour_weight(): jnp.where(first, got, other)]
    reduce_sum x11 -> x6, other arithmetic: 16.1 us -> 9.24 us  [scatter_sum(): return jnp.sum(exchange(blocks, axis).astype(jnp.float32), axis=0)]
    dynamic_slice x0 -> x3, local copies, waits for them, and re-layouts: none -> 6.75 us  [neighbour_weight(): mine = lax.dynamic_slice_in_dim(weight, core * half, half, 0)]
    ppermute x6 -> x16, starting transfers between devices: 1.68 us -> 7.26 us  [the longest x3 3.54 us: neighbour_weight(): got = lax.ppermute(mine, 'col', PAIRS)]
  transfers between devices with their start and end apart: 24 -> 31, of which waited for: 18 -> 15; matrix products, arithmetic and copies ran while one was open for 23% -> 29% of each run, Pallas kernels for 0% -> 0%
where the time goes in v2:
time: 372 us; the launch traced here: 366 us
  waiting for transfers between devices  174 us (47%)
  starting transfers between devices  68.9 us (19%)
  matrix products  57.2 us (15%)
  other arithmetic  33.8 us (9%)
  local copies, waits for them, and re-layouts  18 us (5%)
  between operations  14.5 us (4%)
    all_to_all x13, waiting for transfers between devices, exchange(): return lax.all_to_all(blocks, axis, 0, 0, axis_index_groups=groups)  140 us
    all_to_all x13, starting transfers between devices, exchange(): return lax.all_to_all(blocks, axis, 0, 0, axis_index_groups=groups)  60.9 us
    dot_general x9, matrix products, dot(): lax.dot_general(left, right, (((1,), (contract,)), ((), ())), preferred_e...  38.2 us
    ppermute x3, waiting for transfers between devices, neighbour_weight(): got = lax.ppermute(mine, 'col', PAIRS)  31 us
    dot_general x3, matrix products, token_product(): lax.dot_general(both_replicas(left, core), both_replicas(right, core), ((...  10.5 us
    select_n x3, other arithmetic, neighbour_weight(): jnp.where(first, got, other)  9.94 us
    reduce_sum x6, other arithmetic, scatter_sum(): return jnp.sum(exchange(blocks, axis).astype(jnp.float32), axis=0)  9.24 us
    broadcast_in_dim x7, local copies, waits for them, and re-layouts, gather(): jnp.broadcast_to(values[None], (count,) + values.shape)  8.04 us
  transfers between devices with their start and end apart: 31, of which 15 were waited for; matrix products, arithmetic and copies ran while one was open for 29% of the time, Pallas kernels for 0%

profile of v2, /device:TPU:0, one launch (start us, length us, event | category | flops | bytes accessed | tf_op | source)
XLA Modules:
  0.0 366.2 jit_solution(11554033450379679693)
XLA Ops:
  12.5 5.3 %all-to-all-start.1 = ((bf16[4,128,1024]{2,1,0:T(8,128)(2,1)}), bf16[4,128,1024]{2,1,0:T(8,128)(2,1)S(1)}, u32[]{:S(2)}, u32[]{:S(2)}) async-start(bf16[4,128,1024]{2,1,0:T(8,128)(2,1)} %broadcast_in_dim.27), calls=%async_computation.2 | async-start | bytes 2097152 | tf_op jit(solution)/shard_map/all_to_all | solution.py:33
  17.8 17.0 %collective-permute-done.1 = bf16[512,1024]{1,0:T(8,128)(2,1)} collective-permute-done((bf16[512,1024]{1,0:T(8,128)(2,1)}, bf16[512,1024]{1,0:T(8,128)(2,1)}, u32[]{:S(2)}, u32[]{:S(2)}) %collective-permute-start.1) | collective-permute-done | bytes 1048608 | tf_op jit(solution)/shard_map/ppermute | solution.py:85
  40.4 6.6 %all-to-all-start = ((bf16[8,24,1024]{2,1,0:T(8,128)(2,1)}), bf16[8,24,1024]{2,1,0:T(8,128)(2,1)S(1)}, u32[]{:S(2)}, u32[]{:S(2)}) async-start(bf16[8,24,1024]{2,1,0:T(8,128)(2,1)} %broadcast_in_dim.25), calls=%async_computation | async-start | bytes 786432 | tf_op jit(solution)/shard_map/all_to_all | solution.py:33
  49.3 40.1 %all-to-all-done = bf16[8,24,1024]{2,1,0:T(8,128)(2,1)S(1)} async-done(((bf16[8,24,1024]{2,1,0:T(8,128)(2,1)}), bf16[8,24,1024]{2,1,0:T(8,128)(2,1)S(1)}, u32[]{:S(2)}, u32[]{:S(2)}) %all-to-all-start) | async-done | bytes 393248 | tf_op jit(solution)/shard_map/all_to_all | solution.py:33
  97.7 13.5 %all-to-all-done.2 = bf16[8,64,1024]{2,1,0:T(8,128)(2,1)} async-done(((bf16[8,64,1024]{2,1,0:T(8,128)(2,1)}), bf16[8,64,1024]{2,1,0:T(8,128)(2,1)}, u32[]{:S(2)}, u32[]{:S(2)}) %all-to-all-start.2) | async-done | bytes 1048608 | tf_op jit(solution)/shard_map/all_to_all | solution.py:33
  116.9 14.9 %all-to-all-done.4 = bf16[8,64,1024]{2,1,0:T(8,128)(2,1)} async-done(((bf16[8,64,1024]{2,1,0:T(8,128)(2,1)}), bf16[8,64,1024]{2,1,0:T(8,128)(2,1)}, u32[]{:S(2)}, u32[]{:S(2)}) %all-to-all-start.4) | async-done | bytes 1048608 | tf_op jit(solution)/shard_map/all_to_all | solution.py:33
  144.8 7.6 %all-to-all-done.3 = bf16[8,64,1024]{2,1,0:T(8,128)(2,1)} async-done(((bf16[8,64,1024]{2,1,0:T(8,128)(2,1)}), bf16[8,64,1024]{2,1,0:T(8,128)(2,1)}, u32[]{:S(2)}, u32[]{:S(2)}) %all-to-all-start.3) | async-done | bytes 1048608 | tf_op jit(solution)/shard_map/all_to_all | solution.py:33
  158.7 6.3 %fusion.66 = f32[512,1792]{1,0:T(8,128)} fusion(bf16[512,1024]{1,0:T(8,128)(2,1)} %bitcast.5, bf16[1024,1792]{1,0:T(8,128)(2,1)} %param.8), kind=kOutput, calls=%fused_computation.115 | convolution fusion | flops 1879048192 | bytes 8388608 | tf_op jit(solution)/shard_map/dot_general | solution.py:45
  169.1 12.4 %all-to-all-done.5 = bf16[8,64,1024]{2,1,0:T(8,128)(2,1)} async-done(((bf16[8,64,1024]{2,1,0:T(8,128)(2,1)}), bf16[8,64,1024]{2,1,0:T(8,128)(2,1)}, u32[]{:S(2)}, u32[]{:S(2)}) %all-to-all-start.5) | async-done | bytes 1048608 | tf_op jit(solution)/shard_map/all_to_all | solution.py:33
  181.5 6.8 %add_convert_fusion = bf16[512,1792]{1,0:T(8,128)(2,1)} fusion(f32[512,1792]{1,0:T(8,128)} %fusion.66, bf16[512,1024]{1,0:T(8,128)(2,1)} %bitcast.8, bf16[512,1792]{1,0:T(8,128)(2,1)} %get-tuple-element.16, bf16[512,1792]{1,0:T(8,128)(2,1)} %get-tuple-element.15), kind=kOutput, calls=%fused_computation.10 | convolution fusion | flops 1888223232 | bytes 10223616 | tf_op jit(solution)/shard_map/dot_general | solution.py:45
  188.3 7.3 %all-to-all-start.6 = ((bf16[4,128,1792]{2,1,0:T(8,128)(2,1)}), bf16[4,128,1792]{2,1,0:T(8,128)(2,1)}, u32[]{:S(2)}, u32[]{:S(2)}) async-start(bf16[4,128,1792]{2,1,0:T(8,128)(2,1)} %bitcast.77), calls=%async_computation.7 | async-start | bytes 3670016 | tf_op jit(solution)/shard_map/all_to_all | solution.py:33
  200.2 15.6 %all-to-all-done.6 = bf16[4,128,1792]{2,1,0:T(8,128)(2,1)} async-done(((bf16[4,128,1792]{2,1,0:T(8,128)(2,1)}), bf16[4,128,1792]{2,1,0:T(8,128)(2,1)}, u32[]{:S(2)}, u32[]{:S(2)}) %all-to-all-start.6) | async-done | bytes 1835040 | tf_op jit(solution)/shard_map/all_to_all | solution.py:33
  220.6 4.4 %all-to-all-start.7 = ((bf16[8,24,1792]{2,1,0:T(8,128)(2,1)}), bf16[8,24,1792]{2,1,0:T(8,128)(2,1)}, u32[]{:S(2)}, u32[]{:S(2)}) async-start(bf16[8,24,1792]{2,1,0:T(8,128)(2,1)} %broadcast_in_dim.30), calls=%async_computation.8 | async-start | bytes 1376256 | tf_op jit(solution)/shard_map/all_to_all | solution.py:33
  227.8 14.0 %collective-permute-done.5 = bf16[896,1024]{1,0:T(8,128)(2,1)} collective-permute-done((bf16[896,1024]{1,0:T(8,128)(2,1)}, bf16[896,1024]{1,0:T(8,128)(2,1)}, u32[]{:S(2)}, u32[]{:S(2)}) %collective-permute-start.5) | collective-permute-done | bytes 1835040 | tf_op jit(solution)/shard_map/ppermute | solution.py:85
  243.0 5.5 %all-to-all-done.7 = bf16[8,24,1792]{2,1,0:T(8,128)(2,1)} async-done(((bf16[8,24,1792]{2,1,0:T(8,128)(2,1)}), bf16[8,24,1792]{2,1,0:T(8,128)(2,1)}, u32[]{:S(2)}, u32[]{:S(2)}) %all-to-all-start.7) | async-done | bytes 688160 | tf_op jit(solution)/shard_map/all_to_all | solution.py:33
  249.9 4.4 %all-to-all-start.8 = ((bf16[4,128,1792]{2,1,0:T(8,128)(2,1)}), bf16[4,128,1792]{2,1,0:T(8,128)(2,1)}, u32[]{:S(2)}, u32[]{:S(2)}) async-start(bf16[4,128,1792]{2,1,0:T(8,128)(2,1)} %broadcast_in_dim.31), calls=%async_computation.9 | async-start | bytes 3670016 | tf_op jit(solution)/shard_map/all_to_all | solution.py:33
  265.7 8.0 %all-to-all-done.8 = bf16[4,128,1792]{2,1,0:T(8,128)(2,1)} async-done(((bf16[4,128,1792]{2,1,0:T(8,128)(2,1)}), bf16[4,128,1792]{2,1,0:T(8,128)(2,1)}, u32[]{:S(2)}, u32[]{:S(2)}) %all-to-all-start.8) | async-done | bytes 1835040 | tf_op jit(solution)/shard_map/all_to_all | solution.py:33
  273.6 4.3 %convolution_convert_fusion.9 = bf16[192,1024]{1,0:T(8,128)(2,1)} fusion(bf16[192,1792]{1,0:T(8,128)(2,1)} %bitcast.10, bf16[1024,1792]{1,0:T(8,128)(2,1)} %param.8), kind=kOutput, calls=%fused_computation.41 | convolution fusion | flops 704839680 | bytes 4751360 | tf_op jit(solution)/shard_map/dot_general | solution.py:45
  291.7 4.6 %all-to-all-start.11 = ((bf16[8,24,1024]{2,1,0:T(8,128)(2,1)}), bf16[8,24,1024]{2,1,0:T(8,128)(2,1)S(1)}, u32[]{:S(2)}, u32[]{:S(2)}) async-start(bf16[8,24,1024]{2,1,0:T(8,128)(2,1)} %broadcast_in_dim.32), calls=%async_computation.12 | async-start | bytes 786432 | tf_op jit(solution)/shard_map/all_to_all | solution.py:33
  296.4 5.6 %convolution_convert_fusion.7 = bf16[512,1024]{1,0:T(8,128)(2,1)} fusion(bf16[512,1792]{1,0:T(8,128)(2,1)} %bitcast.11, bf16[1792,1024]{1,0:T(8,128)(2,1)} %param.9), kind=kOutput, calls=%fused_computation.33 | convolution fusion | flops 1879572480 | bytes 6553600 | tf_op jit(solution)/shard_map/dot_general | solution.py:45
  302.0 4.9 %all-to-all-done.11 = bf16[8,24,1024]{2,1,0:T(8,128)(2,1)S(1)} async-done(((bf16[8,24,1024]{2,1,0:T(8,128)(2,1)}), bf16[8,24,1024]{2,1,0:T(8,128)(2,1)S(1)}, u32[]{:S(2)}, u32[]{:S(2)}) %all-to-all-start.11) | async-done | bytes 393248 | tf_op jit(solution)/shard_map/all_to_all | solution.py:33
  312.0 4.7 %fusion.18 = bf16[512,1024]{1,0:T(8,128)(2,1)S(1)} fusion(bf16[512,1792]{1,0:T(8,128)(2,1)} %bitcast.11, bf16[896,1024]{1,0:T(8,128)(2,1)} %get-tuple-element.14, bf16[896,1024]{1,0:T(8,128)(2,1)} %get-tuple-element.13), kind=kOutput, calls=%fused_computation.31 | convolution fusion | flops 1886912512 | bytes 6553600 | tf_op jit(solution)/shard_map/dot_general | solution.py:45
  320.9 4.4 %all-to-all-start.9 = ((bf16[8,128,1024]{2,1,0:T(8,128)(2,1)}), bf16[8,128,1024]{2,1,0:T(8,128)(2,1)}, u32[]{:S(2)}, u32[]{:S(2)}) async-start(bf16[8,128,1024]{2,1,0:T(8,128)(2,1)} %bitcast.69), calls=%async_computation.10 | async-start | bytes 4194304 | tf_op jit(solution)/shard_map/all_to_all | solution.py:33
  339.9 12.5 %all-to-all-done.9 = bf16[8,128,1024]{2,1,0:T(8,128)(2,1)} async-done(((bf16[8,128,1024]{2,1,0:T(8,128)(2,1)}), bf16[8,128,1024]{2,1,0:T(8,128)(2,1)}, u32[]{:S(2)}, u32[]{:S(2)}) %all-to-all-start.9) | async-done | bytes 2097184 | tf_op jit(solution)/shard_map/all_to_all | solution.py:33
  (126 shorter events, 120.9 us)
Async XLA Ops:
  9.8 25.0 %collective-permute-start.1 = (bf16[512,1024]{1,0:T(8,128)(2,1)}, bf16[512,1024]{1,0:T(8,128)(2,1)}, u32[]{:S(2)}, u32[]{:S(2)}) collective-permute-start(bf16[512,1024]{1,0:T(8,128)(2,1)} %constant_dynamic-slice_fusion.2), channel_id=1, source_target_pairs={{0,1},{1,0},{2,3},{3,2},{4,5},{5,4},{6,7},{7,6},{8,9},{9,8},{10,11... | collective-permute-start | bytes 3145736 | tf_op jit(solution)/shard_map/ppermute | solution.py:85
  12.5 27.2 %all-to-all-start.1 = ((bf16[4,128,1024]{2,1,0:T(8,128)(2,1)}), bf16[4,128,1024]{2,1,0:T(8,128)(2,1)S(1)}, u32[]{:S(2)}, u32[]{:S(2)}) async-start(bf16[4,128,1024]{2,1,0:T(8,128)(2,1)} %broadcast_in_dim.27), calls=%async_computation.2 | async-start | bytes 2097152 | tf_op jit(solution)/shard_map/all_to_all | solution.py:33
  34.8 58.9 %collective-permute-start.2 = (bf16[512,1024]{1,0:T(8,128)(2,1)}, bf16[512,1024]{1,0:T(8,128)(2,1)}, u32[]{:S(2)}, u32[]{:S(2)}) collective-permute-start(bf16[512,1024]{1,0:T(8,128)(2,1)} %collective-permute-done.1), channel_id=1, source_target_pairs={{0,64},{64,0},{1,65},{65,1},{2,66},{66,2},{3,67},{67,3},{4,68},{68... | collective-permute-start | bytes 3145736 | tf_op jit(solution)/shard_map/ppermute | solution.py:86
  37.7 77.7 %collective-permute-start.3 = (bf16[512,1792]{1,0:T(8,128)(2,1)}, bf16[512,1792]{1,0:T(8,128)(2,1)}, u32[]{:S(2)}, u32[]{:S(2)}) collective-permute-start(bf16[512,1792]{1,0:T(8,128)(2,1)} %constant_dynamic-slice_fusion.1), channel_id=1, source_target_pairs={{0,1},{1,0},{2,3},{3,2},{4,5},{5,4},{6,7},{7,6},{8,9},{9,8},{10,11... | collective-permute-start | bytes 5505032 | tf_op jit(solution)/shard_map/ppermute | solution.py:85
  40.4 49.0 %all-to-all-start = ((bf16[8,24,1024]{2,1,0:T(8,128)(2,1)}), bf16[8,24,1024]{2,1,0:T(8,128)(2,1)S(1)}, u32[]{:S(2)}, u32[]{:S(2)}) async-start(bf16[8,24,1024]{2,1,0:T(8,128)(2,1)} %broadcast_in_dim.25), calls=%async_computation | async-start | bytes 786432 | tf_op jit(solution)/shard_map/all_to_all | solution.py:33
  89.4 21.7 %all-to-all-start.2 = ((bf16[8,64,1024]{2,1,0:T(8,128)(2,1)}), bf16[8,64,1024]{2,1,0:T(8,128)(2,1)}, u32[]{:S(2)}, u32[]{:S(2)}) async-start(bf16[8,64,1024]{2,1,0:T(8,128)(2,1)} %bitcast.81), calls=%async_computation.3 | async-start | bytes 2097152 | tf_op jit(solution)/shard_map/all_to_all | solution.py:33
  111.1 20.7 %all-to-all-start.4 = ((bf16[8,64,1024]{2,1,0:T(8,128)(2,1)}), bf16[8,64,1024]{2,1,0:T(8,128)(2,1)}, u32[]{:S(2)}, u32[]{:S(2)}) async-start(bf16[8,64,1024]{2,1,0:T(8,128)(2,1)} %bitcast.82), calls=%async_computation.5 | async-start | bytes 2097152 | tf_op jit(solution)/shard_map/all_to_all | solution.py:33
  115.4 49.6 %collective-permute-start.4 = (bf16[512,1792]{1,0:T(8,128)(2,1)}, bf16[512,1792]{1,0:T(8,128)(2,1)}, u32[]{:S(2)}, u32[]{:S(2)}) collective-permute-start(bf16[512,1792]{1,0:T(8,128)(2,1)} %collective-permute-done.3), channel_id=1, source_target_pairs={{0,64},{64,0},{1,65},{65,1},{2,66},{66,2},{3,67},{67,3},{4,68},{68... | collective-permute-start | bytes 5505032 | tf_op jit(solution)/shard_map/ppermute | solution.py:86
  133.0 19.5 %all-to-all-start.3 = ((bf16[8,64,1024]{2,1,0:T(8,128)(2,1)}), bf16[8,64,1024]{2,1,0:T(8,128)(2,1)}, u32[]{:S(2)}, u32[]{:S(2)}) async-start(bf16[8,64,1024]{2,1,0:T(8,128)(2,1)} %broadcast_in_dim.28), calls=%async_computation.4 | async-start | bytes 2097152 | tf_op jit(solution)/shard_map/all_to_all | solution.py:33
  137.2 81.2 %reduce-scatter.2.cloned.1.call-start = ((), (), s32[]{:S(2)}) async-start(), calls=%async_computation.14 | async-start | bytes 774144 | tf_op jit(solution)/shard_map/reduce_scatter | solution.py:136
  154.4 27.1 %all-to-all-start.5 = ((bf16[8,64,1024]{2,1,0:T(8,128)(2,1)}), bf16[8,64,1024]{2,1,0:T(8,128)(2,1)}, u32[]{:S(2)}, u32[]{:S(2)}) async-start(bf16[8,64,1024]{2,1,0:T(8,128)(2,1)} %broadcast_in_dim.29), calls=%async_computation.6 | async-start | bytes 2097152 | tf_op jit(solution)/shard_map/all_to_all | solution.py:33
  188.3 27.4 %all-to-all-start.6 = ((bf16[4,128,1792]{2,1,0:T(8,128)(2,1)}), bf16[4,128,1792]{2,1,0:T(8,128)(2,1)}, u32[]{:S(2)}, u32[]{:S(2)}) async-start(bf16[4,128,1792]{2,1,0:T(8,128)(2,1)} %bitcast.77), calls=%async_computation.7 | async-start | bytes 3670016 | tf_op jit(solution)/shard_map/all_to_all | solution.py:33
  198.4 43.3 %collective-permute-start.5 = (bf16[896,1024]{1,0:T(8,128)(2,1)}, bf16[896,1024]{1,0:T(8,128)(2,1)}, u32[]{:S(2)}, u32[]{:S(2)}) collective-permute-start(bf16[896,1024]{1,0:T(8,128)(2,1)} %constant_dynamic-slice_fusion), channel_id=1, source_target_pairs={{0,1},{1,0},{2,3},{3,2},{4,5},{5,4},{6,7},{7,6},{8,9},{9,8},{10,11... | collective-permute-start | bytes 5505032 | tf_op jit(solution)/shard_map/ppermute | solution.py:85
  199.3 62.4 %collective-permute-start.16 = (bf16[192,1024]{1,0:T(8,128)(2,1)S(1)}, bf16[192,1024]{1,0:T(8,128)(2,1)}, u32[]{:S(2)}, u32[]{:S(2)}) collective-permute-start(bf16[192,1024]{1,0:T(8,128)(2,1)S(1)} %bitcast.73), channel_id=1, source_target_pairs={{0,64},{64,0},{1,65},{65,1},{2,66},{66,2},{3,67},{67,3},{4,68},{68... | collective-permute-start | bytes 1179656 | tf_op jit(solution)/shard_map/ppermute | solution.py:101
  220.6 27.9 %all-to-all-start.7 = ((bf16[8,24,1792]{2,1,0:T(8,128)(2,1)}), bf16[8,24,1792]{2,1,0:T(8,128)(2,1)}, u32[]{:S(2)}, u32[]{:S(2)}) async-start(bf16[8,24,1792]{2,1,0:T(8,128)(2,1)} %broadcast_in_dim.30), calls=%async_computation.8 | async-start | bytes 1376256 | tf_op jit(solution)/shard_map/all_to_all | solution.py:33
  226.0 29.9 %collective-permute-start.8 = (bf16[4,24,1024]{2,1,0:T(8,128)(2,1)}, bf16[4,24,1024]{2,1,0:T(8,128)(2,1)S(1)}, u32[]{:S(2)}, u32[]{:S(2)}) collective-permute-start(bf16[4,24,1024]{2,1,0:T(8,128)(2,1)} %convolution_convert_fusion.13), channel_id=1, source_target_pairs={{0,1},{1,0},{2,3},{3,2},{4,5},{5,4},{6,7},{7,6},{8,9},{9,8},{10,11... | collective-permute-start | bytes 589832 | tf_op jit(solution)/shard_map/ppermute | solution.py:184
  241.7 39.7 %collective-permute-start.6 = (bf16[896,1024]{1,0:T(8,128)(2,1)}, bf16[896,1024]{1,0:T(8,128)(2,1)}, u32[]{:S(2)}, u32[]{:S(2)}) collective-permute-start(bf16[896,1024]{1,0:T(8,128)(2,1)} %collective-permute-done.5), channel_id=1, source_target_pairs={{0,64},{64,0},{1,65},{65,1},{2,66},{66,2},{3,67},{67,3},{4,68},{68... | collective-permute-start | bytes 5505032 | tf_op jit(solution)/shard_map/ppermute | solution.py:86
  249.9 23.7 %all-to-all-start.8 = ((bf16[4,128,1792]{2,1,0:T(8,128)(2,1)}), bf16[4,128,1792]{2,1,0:T(8,128)(2,1)}, u32[]{:S(2)}, u32[]{:S(2)}) async-start(bf16[4,128,1792]{2,1,0:T(8,128)(2,1)} %broadcast_in_dim.31), calls=%async_computation.9 | async-start | bytes 3670016 | tf_op jit(solution)/shard_map/all_to_all | solution.py:33
  278.0 12.9 %all-to-all-start.10 = ((bf16[8,24,1024]{2,1,0:T(8,128)(2,1)}), bf16[8,24,1024]{2,1,0:T(8,128)(2,1)S(1)}, u32[]{:S(2)}, u32[]{:S(2)}) async-start(bf16[8,24,1024]{2,1,0:T(8,128)(2,1)} %bitcast.17), calls=%async_computation.11 | async-start | bytes 786432 | tf_op jit(solution)/shard_map/all_to_all | solution.py:33
  285.6 41.6 %collective-permute-start.13 = (bf16[192,1792]{1,0:T(8,128)(2,1)}, bf16[192,1792]{1,0:T(8,128)(2,1)}, u32[]{:S(2)}, u32[]{:S(2)}) collective-permute-start(bf16[192,1792]{1,0:T(8,128)(2,1)} %bitcast.10), channel_id=1, source_target_pairs={{0,64},{64,0},{1,65},{65,1},{2,66},{66,2},{3,67},{67,3},{4,68},{68... | collective-permute-start | bytes 2064392 | tf_op jit(solution)/shard_map/ppermute | solution.py:101
  287.5 37.8 %collective-permute-start.14 = (bf16[4,24,1792]{2,1,0:T(8,128)(2,1)S(1)}, bf16[4,24,1792]{2,1,0:T(8,128)(2,1)}, u32[]{:S(2)}, u32[]{:S(2)}) collective-permute-start(bf16[4,24,1792]{2,1,0:T(8,128)(2,1)S(1)} %convolution_convert_fusion.3), channel_id=1, source_target_pairs={{0,1},{1,0},{2,3},{3,2},{4,5},{5,4},{6,7},{7,6},{8,9},{9,8},{10,11... | collective-permute-start | bytes 1032200 | tf_op jit(solution)/shard_map/ppermute | solution.py:193
  291.7 15.2 %all-to-all-start.11 = ((bf16[8,24,1024]{2,1,0:T(8,128)(2,1)}), bf16[8,24,1024]{2,1,0:T(8,128)(2,1)S(1)}, u32[]{:S(2)}, u32[]{:S(2)}) async-start(bf16[8,24,1024]{2,1,0:T(8,128)(2,1)} %broadcast_in_dim.32), calls=%async_computation.12 | async-start | bytes 786432 | tf_op jit(solution)/shard_map/all_to_all | solution.py:33
  320.9 31.4 %all-to-all-start.9 = ((bf16[8,128,1024]{2,1,0:T(8,128)(2,1)}), bf16[8,128,1024]{2,1,0:T(8,128)(2,1)}, u32[]{:S(2)}, u32[]{:S(2)}) async-start(bf16[8,128,1024]{2,1,0:T(8,128)(2,1)} %bitcast.69), calls=%async_computation.10 | async-start | bytes 4194304 | tf_op jit(solution)/shard_map/all_to_all | solution.py:33
  326.6 28.3 %collective-permute-start.10 = (bf16[192,1024]{1,0:T(8,128)(2,1)S(1)}, bf16[192,1024]{1,0:T(8,128)(2,1)}, u32[]{:S(2)}, u32[]{:S(2)}) collective-permute-start(bf16[192,1024]{1,0:T(8,128)(2,1)S(1)} %bitcast.75), channel_id=1, source_target_pairs={{0,64},{64,0},{1,65},{65,1},{2,66},{66,2},{3,67},{67,3},{4,68},{68... | collective-permute-start | bytes 1179656 | tf_op jit(solution)/shard_map/ppermute | solution.py:101
  (20 other events, 127.3 us)
Sparse Core Ops, SparseCore 0:
  142.8 44.5 reduce-scatter.1

commit v3 on v1

v3 whole, which is shorter than its diff:
```python
import jax
import jax.numpy as jnp
from jax import lax
from jax.sharding import PartitionSpec as P

SEQ = 128
MASKED = 20
HEAD = 24
GROUP = 8
CORES = [(0, 1), (1, 0)]

coef = 0.7978845608
cubic = 0.044715


def gelu(value):
    inner = jnp.tanh(coef * (value + cubic * value * value * value))
    return 0.5 * value * (1.0 + inner)


def gelu_slope(value):
    inner = jnp.tanh(coef * (value + cubic * value * value * value))
    return 0.5 * (1.0 + inner) + 0.5 * value * (1.0 - inner * inner) * coef * (
        1.0 + 3.0 * cubic * value * value
    )


def gather(values, axis):
    copies = jnp.broadcast_to(values[None], (GROUP,) + values.shape)
    return lax.all_to_all(copies, axis, 0, 0)


def scatter_sum(blocks, axis):
    return jnp.sum(lax.all_to_all(blocks, axis, 0, 0).astype(jnp.float32), axis=0)


def product(blocks, weight, contract):
    out = lax.dot_general(
        flat(blocks), weight, (((1,), (contract,)), ((), ())), preferred_element_type=jnp.float32
    )
    return out.astype(jnp.bfloat16).reshape(GROUP, -1, out.shape[1])


def replace_tail(blocks, tail):
    return lax.dynamic_update_slice(blocks, tail, (0, blocks.shape[1] - tail.shape[1], 0))


def flat(blocks):
    return blocks.reshape(-1, blocks.shape[-1])


def select(matrix, values, contract):
    return lax.dot_general(
        matrix, values, (((contract,), (0,)), ((), ())), preferred_element_type=jnp.float32
    ).astype(jnp.bfloat16)


def select_each(matrix, values):
    return lax.dot_general(
        matrix, values, (((2,), (1,)), ((0,), (0,))), preferred_element_type=jnp.float32
    ).astype(jnp.bfloat16)


def heads(positions, width):
    places = jnp.arange(width, dtype=jnp.int32)
    short = jnp.pad(
        positions,
        [(0, 0)] * (positions.ndim - 1) + [(0, HEAD - MASKED)],
        constant_values=-1,
    )
    return (short[..., None] == places).astype(jnp.bfloat16)


def both_replicas(values, core):
    other = lax.ppermute(values, "dp", CORES)
    first = core == 0
    return jnp.concatenate(
        [jnp.where(first, values, other), jnp.where(first, other, values)], axis=0
    )


def token_product(left, right, core):
    return lax.dot_general(
        both_replicas(flat(left), core),
        both_replicas(flat(right), core),
        (((0,), (0,)), ((), ())),
        preferred_element_type=jnp.float32,
    ).astype(jnp.bfloat16)


def body(context, out_weight, up_weight, down_weight, cotangent, masked_pos):
    core = lax.axis_index("dp")
    live = jnp.arange(HEAD) < MASKED
    crossed = [(r * GROUP + c, c * GROUP + r) for r in range(GROUP) for c in range(GROUP)]
    col_pos = lax.ppermute(masked_pos, ("row", "col"), crossed)

    ctx = gather(context, "col")
    noted = jnp.pad(
        masked_pos.astype(jnp.bfloat16),
        [(MASKED, HEAD - MASKED - 1), (0, cotangent.shape[1] - MASKED)],
    )
    grad_rows = select(heads(masked_pos[0], SEQ), cotangent, 1) + noted

    projected = scatter_sum(product(ctx, out_weight, 0), "row").astype(jnp.bfloat16)
    row_full = gather(jnp.concatenate([projected, grad_rows], axis=0), "row")
    grad_full = row_full[:, SEQ:]
    positions = grad_full[:, MASKED, :MASKED].astype(jnp.int32)
    up_part = replace_tail(product(row_full, up_weight, 0), product(grad_full, down_weight, 1))
    hidden_sum = scatter_sum(up_part, "col")
    pre_act = hidden_sum[:SEQ].astype(jnp.bfloat16)
    grad_act = hidden_sum[SEQ:]
    act = gelu(pre_act.astype(jnp.float32)).astype(jnp.bfloat16)
    col_heads = heads(col_pos[0], SEQ)
    slope = gelu_slope(select(col_heads, pre_act, 1).astype(jnp.float32))
    grad_hidden = jnp.where(live[:, None], grad_act * slope, 0.0).astype(jnp.bfloat16)

    col_full = gather(jnp.concatenate([act, grad_hidden], axis=0), "col")
    hidden_full = col_full[:, SEQ:]
    down_part = replace_tail(
        product(col_full, down_weight, 0), product(hidden_full, up_weight, 1)
    )
    out_sum = scatter_sum(down_part, "row").astype(jnp.bfloat16)
    block_out = out_sum[:SEQ]
    gproj_full = gather(out_sum[SEQ:], "row")
    grad_ctx = scatter_sum(product(gproj_full, out_weight, 1), "col").astype(jnp.bfloat16)
    context_grad = select(col_heads, grad_ctx, 0)

    out_grad = token_product(
        select_each(heads(positions, SEQ), ctx), gproj_full, core
    )
    up_grad = token_product(
        select_each(heads(positions, SEQ + HEAD), row_full), hidden_full, core
    )
    grad_full = jnp.where(live[None, :, None], grad_full, jnp.zeros_like(grad_full))
    down_grad = token_product(
        select_each(heads(positions, SEQ + HEAD), col_full), grad_full, core
    )
    return (block_out, context_grad, out_grad, up_grad, down_grad)


def solution(mesh):
    placed = (
        P(("dp", "col"), "row"),
        P("row", "col"),
        P("col", "row"),
        P("row", "col"),
        P(("dp", "row"), "col"),
        P(("dp", "row"), None),
    )
    return jax.shard_map(
        body,
        mesh=mesh,
        in_specs=placed,
        out_specs=(
            P(("dp", "row"), "col"),
            P(("dp", "col"), "row"),
            P("row", "col"),
            P("col", "row"),
            P("row", "col"),
        ),
        check_vma=False,
    )
```

time: 362 us -> 333 us (0.920)
  starting transfers between devices: 83.4 us -> 36.4 us
  waiting for transfers between devices: 156 us -> 180 us
  blocking collectives: 15.6 us -> 33.4 us
  other arithmetic: 33.3 us -> 19 us
  local copies, waits for them, and re-layouts: 17.8 us -> 10.7 us
    all_to_all x8 -> x3, starting transfers between devices: 43.8 us -> 12.4 us  [gather(): return lax.all_to_all(copies, axis, 0, 0)]
    all_to_all x1, blocking collectives: 15.6 us -> 33.4 us  [gather(): return lax.all_to_all(copies, axis, 0, 0)]
    all_to_all x9 -> x4, waiting for transfers between devices: 76.8 us -> 91.4 us  [scatter_sum(): lax.all_to_all(blocks, axis, 0, 0).astype(jnp.float32)]
    all_to_all x9 -> x4, starting transfers between devices: 36.4 us -> 22 us  [scatter_sum(): lax.all_to_all(blocks, axis, 0, 0).astype(jnp.float32)]
    all_to_all x8 -> x3, waiting for transfers between devices: 78.6 us -> 87.3 us  [gather(): return lax.all_to_all(copies, axis, 0, 0)]
    reduce_sum x9 -> x4, other arithmetic: 15.2 us -> 7.16 us  [scatter_sum(): jnp.sum(lax.all_to_all(blocks, axis, 0, 0).astype(jnp.float32), axis=0)]
    broadcast_in_dim x9 -> x4, local copies, waits for them, and re-layouts: 13.4 us -> 6.3 us  [gather(): copies = jnp.broadcast_to(values[None], (GROUP,) + values.shape)]
  transfers between devices with their start and end apart: 24 -> 14, of which waited for: 18 -> 7; matrix products, arithmetic and copies ran while one was open for 23% -> 9% of each run, Pallas kernels for 0% -> 0%
where the time goes in v3:
time: 333 us; the launch traced here: 330 us
  waiting for transfers between devices  180 us (54%)
  matrix products  50.4 us (15%)
  starting transfers between devices  36.4 us (11%)
  blocking collectives  33.4 us (10%)
  other arithmetic  19 us (6%)
  local copies, waits for them, and re-layouts  10.7 us (3%)
    all_to_all x4, waiting for transfers between devices, scatter_sum(): lax.all_to_all(blocks, axis, 0, 0).astype(jnp.float32)  91.4 us
    all_to_all x3, waiting for transfers between devices, gather(): return lax.all_to_all(copies, axis, 0, 0)  87.3 us
    all_to_all x1, blocking collectives, gather(): return lax.all_to_all(copies, axis, 0, 0)  33.4 us
    dot_general x6, matrix products, product(): lax.dot_general(flat(blocks), weight, (((1,), (contract,)), ((), ())), pr...  29.2 us
    all_to_all x4, starting transfers between devices, scatter_sum(): lax.all_to_all(blocks, axis, 0, 0).astype(jnp.float32)  22 us
    dot_general x3, matrix products, token_product(): lax.dot_general(both_replicas(flat(left), core), both_replicas(flat(right...  13.1 us
    all_to_all x3, starting transfers between devices, gather(): return lax.all_to_all(copies, axis, 0, 0)  12.4 us
    select_n x6, other arithmetic, both_replicas(): jnp.where(first, values, other)  9.62 us
  transfers between devices with their start and end apart: 14, of which 7 were waited for; matrix products, arithmetic and copies ran while one was open for 9% of the time, Pallas kernels for 0%

profile of v3, /device:TPU:0, one launch (start us, length us, event | category | flops | bytes accessed | tf_op | source)
XLA Modules:
  0.0 330.5 jit_solution(14197607835615567178)
XLA Ops:
  2.0 33.4 %all_to_all.40 = bf16[8,128,1024]{2,1,0:T(8,128)(2,1)S(1)} all-to-all(bf16[8,128,1024]{2,1,0:T(8,128)(2,1)S(1)} %broadcast_in_dim.27), channel_id=1, replica_groups=mesh['dp'=2,'row'=8,'col'=8] {'col'}, dimensions={0} | all-to-all | bytes 4194304 | tf_op jit(solution)/shard_map/all_to_all | solution.py:30
  35.4 3.7 %convolution_convert_fusion.8 = bf16[1024,1024]{1,0:T(8,128)(2,1)} fusion(bf16[1024,1024]{1,0:T(8,128)(2,1)S(1)} %bitcast.50, bf16[1024,1024]{1,0:T(8,128)(2,1)S(1)} %copy-done), kind=kOutput, calls=%fused_computation.10 | convolution fusion | flops 2148532224 | bytes 6291456 | tf_op jit(solution)/shard_map/dot_general | solution.py:38
  39.0 6.8 %all-to-all-start.1 = ((bf16[8,128,1024]{2,1,0:T(8,128)(2,1)}), bf16[8,128,1024]{2,1,0:T(8,128)(2,1)}, u32[]{:S(2)}, u32[]{:S(2)}) async-start(bf16[8,128,1024]{2,1,0:T(8,128)(2,1)} %bitcast.57), calls=%async_computation.1 | async-start | bytes 4194304 | tf_op jit(solution)/shard_map/all_to_all | solution.py:34
  46.1 27.2 %all-to-all-done.1 = bf16[8,128,1024]{2,1,0:T(8,128)(2,1)} async-done(((bf16[8,128,1024]{2,1,0:T(8,128)(2,1)}), bf16[8,128,1024]{2,1,0:T(8,128)(2,1)}, u32[]{:S(2)}, u32[]{:S(2)}) %all-to-all-start.1) | async-done | bytes 2097184 | tf_op jit(solution)/shard_map/all_to_all | solution.py:34
  77.0 4.4 %all-to-all-start.2 = ((bf16[8,152,1024]{2,1,0:T(8,128)(2,1)}), bf16[8,152,1024]{2,1,0:T(8,128)(2,1)}, u32[]{:S(2)}, u32[]{:S(2)}) async-start(bf16[8,152,1024]{2,1,0:T(8,128)(2,1)} %broadcast_in_dim.28), calls=%async_computation.2 | async-start | bytes 4980736 | tf_op jit(solution)/shard_map/all_to_all | solution.py:30
  81.4 31.2 %all-to-all-done.2 = bf16[8,152,1024]{2,1,0:T(8,128)(2,1)} async-done(((bf16[8,152,1024]{2,1,0:T(8,128)(2,1)}), bf16[8,152,1024]{2,1,0:T(8,128)(2,1)}, u32[]{:S(2)}, u32[]{:S(2)}) %all-to-all-start.2) | async-done | bytes 2490400 | tf_op jit(solution)/shard_map/all_to_all | solution.py:30
  114.5 3.6 %convolution_convert_fusion.5 = bf16[192,1792]{1,0:T(8,128)(2,1)S(1)} fusion(bf16[192,1024]{1,0:T(8,128)(2,1)S(1)} %bitcast.59, bf16[1792,1024]{1,0:T(8,128)(2,1)} %param.9), kind=kOutput, calls=%fused_computation.6 | convolution fusion | flops 704987136 | bytes 4751360 | tf_op jit(solution)/shard_map/dot_general | solution.py:38
  118.1 8.7 %convolution_convert_fusion = bf16[1216,1792]{1,0:T(8,128)(2,1)} fusion(bf16[1216,1024]{1,0:T(8,128)(2,1)} %bitcast.3, bf16[1024,1792]{1,0:T(8,128)(2,1)S(1)} %copy-done.14), kind=kOutput, calls=%fused_computation.1 | convolution fusion | flops 4464918528 | bytes 10518528 | tf_op jit(solution)/shard_map/dot_general | solution.py:38
  127.7 4.6 %all-to-all-start.3 = ((bf16[8,152,1792]{2,1,0:T(8,128)(2,1)}), bf16[8,152,1792]{2,1,0:T(8,128)(2,1)}, u32[]{:S(2)}, u32[]{:S(2)}) async-start(bf16[8,152,1792]{2,1,0:T(8,128)(2,1)} %constant_dynamic-update-slice_fusion.1), calls=%async_computation.3 | async-start | bytes 8716288 | tf_op jit(solution)/shard_map/all_to_all | solution.py:34
  133.0 48.1 %all-to-all-done.3 = bf16[8,152,1792]{2,1,0:T(8,128)(2,1)} async-done(((bf16[8,152,1792]{2,1,0:T(8,128)(2,1)}), bf16[8,152,1792]{2,1,0:T(8,128)(2,1)}, u32[]{:S(2)}, u32[]{:S(2)}) %all-to-all-start.3) | async-done | bytes 4358176 | tf_op jit(solution)/shard_map/all_to_all | solution.py:34
  187.0 4.6 %all-to-all-start.4 = ((bf16[8,152,1792]{2,1,0:T(8,128)(2,1)}), bf16[8,152,1792]{2,1,0:T(8,128)(2,1)}, u32[]{:S(2)}, u32[]{:S(2)}) async-start(bf16[8,152,1792]{2,1,0:T(8,128)(2,1)} %broadcast_in_dim.31), calls=%async_computation.4 | async-start | bytes 8716288 | tf_op jit(solution)/shard_map/all_to_all | solution.py:30
  192.4 48.8 %all-to-all-done.4 = bf16[8,152,1792]{2,1,0:T(8,128)(2,1)} async-done(((bf16[8,152,1792]{2,1,0:T(8,128)(2,1)}), bf16[8,152,1792]{2,1,0:T(8,128)(2,1)}, u32[]{:S(2)}, u32[]{:S(2)}) %all-to-all-start.4) | async-done | bytes 4358176 | tf_op jit(solution)/shard_map/all_to_all | solution.py:30
  242.3 3.5 %convolution_convert_fusion.12 = bf16[192,1024]{1,0:T(8,128)(2,1)S(1)} fusion(bf16[192,1792]{1,0:T(8,128)(2,1)S(1)} %bitcast.54, bf16[1024,1792]{1,0:T(8,128)(2,1)} %param.8), kind=kOutput, calls=%fused_computation.25 | convolution fusion | flops 704839680 | bytes 4751360 | tf_op jit(solution)/shard_map/dot_general | solution.py:38
  245.9 8.2 %convolution_convert_fusion.3 = bf16[1216,1024]{1,0:T(8,128)(2,1)} fusion(bf16[1216,1792]{1,0:T(8,128)(2,1)} %bitcast.8, bf16[1792,1024]{1,0:T(8,128)(2,1)S(1)} %copy-done.3), kind=kOutput, calls=%fused_computation.4 | convolution fusion | flops 4463984640 | bytes 10518528 | tf_op jit(solution)/shard_map/dot_general | solution.py:38
  254.8 6.8 %all-to-all-start.5 = ((bf16[8,152,1024]{2,1,0:T(8,128)(2,1)}), bf16[8,152,1024]{2,1,0:T(8,128)(2,1)}, u32[]{:S(2)}, u32[]{:S(2)}) async-start(bf16[8,152,1024]{2,1,0:T(8,128)(2,1)} %constant_dynamic-update-slice_fusion), calls=%async_computation.5 | async-start | bytes 4980736 | tf_op jit(solution)/shard_map/all_to_all | solution.py:34
  261.7 3.1 convolution_convert_fusion.9
  271.1 3.0 convolution_convert_fusion.4
  276.8 16.1 %all-to-all-done.5 = bf16[8,152,1024]{2,1,0:T(8,128)(2,1)} async-done(((bf16[8,152,1024]{2,1,0:T(8,128)(2,1)}), bf16[8,152,1024]{2,1,0:T(8,128)(2,1)}, u32[]{:S(2)}, u32[]{:S(2)}) %all-to-all-start.5) | async-done | bytes 2490400 | tf_op jit(solution)/shard_map/all_to_all | solution.py:34
  295.9 3.5 %all-to-all-start.6 = ((bf16[8,24,1024]{2,1,0:T(8,128)(2,1)}), bf16[8,24,1024]{2,1,0:T(8,128)(2,1)S(1)}, u32[]{:S(2)}, u32[]{:S(2)}) async-start(bf16[8,24,1024]{2,1,0:T(8,128)(2,1)} %broadcast_in_dim.32), calls=%async_computation.6 | async-start | bytes 786432 | tf_op jit(solution)/shard_map/all_to_all | solution.py:30
  301.7 7.3 %all-to-all-done.6 = bf16[8,24,1024]{2,1,0:T(8,128)(2,1)S(1)} async-done(((bf16[8,24,1024]{2,1,0:T(8,128)(2,1)}), bf16[8,24,1024]{2,1,0:T(8,128)(2,1)S(1)}, u32[]{:S(2)}, u32[]{:S(2)}) %all-to-all-start.6) | async-done | bytes 393248 | tf_op jit(solution)/shard_map/all_to_all | solution.py:30
  310.6 3.8 %all-to-all-start.7 = ((bf16[8,24,1024]{2,1,0:T(8,128)(2,1)}), bf16[8,24,1024]{2,1,0:T(8,128)(2,1)S(1)}, u32[]{:S(2)}, u32[]{:S(2)}) async-start(bf16[8,24,1024]{2,1,0:T(8,128)(2,1)} %bitcast.13), calls=%async_computation.7 | async-start | bytes 786432 | tf_op jit(solution)/shard_map/all_to_all | solution.py:34
  314.5 5.5 %convolution_convert_fusion.1 = bf16[1792,1024]{1,0:T(8,128)(2,1)} fusion(bf16[192,1792]{1,0:T(8,128)(2,1)} %get-tuple-element.8, bf16[192,1792]{1,0:T(8,128)(2,1)} %get-tuple-element.7, bf16[192,1024]{1,0:T(8,128)(2,1)} %get-tuple-element.12, bf16[192,1024]{1,0:T(8,128)(2,1)S(1)} %copy-done.12), kind=kOutput, calls=%fused_computation.2 | convolution fusion | flops 1415446528 | bytes 5832704 | tf_op jit(solution)/shard_map/dot_general | solution.py:83
  320.0 4.0 %convolution_convert_fusion.2 = bf16[1024,1792]{1,0:T(8,128)(2,1)} fusion(bf16[192,1792]{1,0:T(8,128)(2,1)S(1)} %copy-done.8, bf16[192,1792]{1,0:T(8,128)(2,1)S(1)} %copy-done.7, bf16[192,1024]{1,0:T(8,128)(2,1)S(1)} %copy-done.11, bf16[192,1024]{1,0:T(8,128)(2,1)S(1)} %copy-done.10), kind=kOutput, calls=%fused_computation.3 | convolution fusion | flops 1415446528 | bytes 5832704 | tf_op jit(solution)/shard_map/dot_general | solution.py:83
  326.9 3.6 %convolution_convert_fusion.7 = bf16[1024,1024]{1,0:T(8,128)(2,1)} fusion(bf16[192,1024]{1,0:T(8,128)(2,1)} %get-tuple-element.18, bf16[192,1024]{1,0:T(8,128)(2,1)S(1)} %copy-done.9, bf16[192,1024]{1,0:T(8,128)(2,1)S(1)} %get-tuple-element.16, bf16[192,1024]{1,0:T(8,128)(2,1)S(1)} %get-tuple-element.15), kind=kOutput, calls=%fused_computation.9 | convolution fusion | flops 809500672 | bytes 3670016 | tf_op jit(solution)/shard_map/dot_general | solution.py:83
  (82 shorter events, 36.1 us)
Async XLA Ops:
  0.6 34.7 %copy-start = (bf16[1024,1024]{1,0:T(8,128)(2,1)S(1)}, bf16[1024,1024]{1,0:T(8,128)(2,1)}, u32[]{:S(2)}) copy-start(bf16[1024,1024]{1,0:T(8,128)(2,1)} %param.7) | copy-start | bytes 6291460
  35.4 3.7 %copy-start.1 = (bf16[8,128,1024]{2,1,0:T(8,128)(2,1)}, bf16[8,128,1024]{2,1,0:T(8,128)(2,1)S(1)}, u32[]{:S(2)}) copy-start(bf16[8,128,1024]{2,1,0:T(8,128)(2,1)S(1)} %all_to_all.40) | copy-start | bytes 6291460
  39.0 6.8 %copy-start.15 = (s32[1,20]{1,0:T(1,128)S(1)}, s32[1,20]{1,0:T(1,128)}, u32[]{:S(2)}) copy-start(s32[1,20]{1,0:T(1,128)} %param.11) | copy-start | bytes 244
  39.0 6.8 %copy-start.13 = (bf16[128,1024]{1,0:T(8,128)(2,1)S(1)}, bf16[128,1024]{1,0:T(8,128)(2,1)}, u32[]{:S(2)}) copy-start(bf16[128,1024]{1,0:T(8,128)(2,1)} %param.10) | copy-start | bytes 786436
  39.0 34.2 %all-to-all-start.1 = ((bf16[8,128,1024]{2,1,0:T(8,128)(2,1)}), bf16[8,128,1024]{2,1,0:T(8,128)(2,1)}, u32[]{:S(2)}, u32[]{:S(2)}) async-start(bf16[8,128,1024]{2,1,0:T(8,128)(2,1)} %bitcast.57), calls=%async_computation.1 | async-start | bytes 4194304 | tf_op jit(solution)/shard_map/all_to_all | solution.py:34
  77.0 35.7 %all-to-all-start.2 = ((bf16[8,152,1024]{2,1,0:T(8,128)(2,1)}), bf16[8,152,1024]{2,1,0:T(8,128)(2,1)}, u32[]{:S(2)}, u32[]{:S(2)}) async-start(bf16[8,152,1024]{2,1,0:T(8,128)(2,1)} %broadcast_in_dim.28), calls=%async_computation.2 | async-start | bytes 4980736 | tf_op jit(solution)/shard_map/all_to_all | solution.py:30
  127.7 53.4 %all-to-all-start.3 = ((bf16[8,152,1792]{2,1,0:T(8,128)(2,1)}), bf16[8,152,1792]{2,1,0:T(8,128)(2,1)}, u32[]{:S(2)}, u32[]{:S(2)}) async-start(bf16[8,152,1792]{2,1,0:T(8,128)(2,1)} %constant_dynamic-update-slice_fusion.1), calls=%async_computation.3 | async-start | bytes 8716288 | tf_op jit(solution)/shard_map/all_to_all | solution.py:34
  132.3 0.7 collective-permute-start
  187.0 54.2 %all-to-all-start.4 = ((bf16[8,152,1792]{2,1,0:T(8,128)(2,1)}), bf16[8,152,1792]{2,1,0:T(8,128)(2,1)}, u32[]{:S(2)}, u32[]{:S(2)}) async-start(bf16[8,152,1792]{2,1,0:T(8,128)(2,1)} %broadcast_in_dim.31), calls=%async_computation.4 | async-start | bytes 8716288 | tf_op jit(solution)/shard_map/all_to_all | solution.py:30
  254.8 38.1 %all-to-all-start.5 = ((bf16[8,152,1024]{2,1,0:T(8,128)(2,1)}), bf16[8,152,1024]{2,1,0:T(8,128)(2,1)}, u32[]{:S(2)}, u32[]{:S(2)}) async-start(bf16[8,152,1024]{2,1,0:T(8,128)(2,1)} %constant_dynamic-update-slice_fusion), calls=%async_computation.5 | async-start | bytes 4980736 | tf_op jit(solution)/shard_map/all_to_all | solution.py:34
  264.8 2.1 collective-permute-start.3
  265.3 3.9 %collective-permute-start.1 = (bf16[192,1024]{1,0:T(8,128)(2,1)S(1)}, bf16[192,1024]{1,0:T(8,128)(2,1)}, u32[]{:S(2)}, u32[]{:S(2)}) collective-permute-start(bf16[192,1024]{1,0:T(8,128)(2,1)S(1)} %bitcast.58), channel_id=1, source_target_pairs={{0,64},{64,0},{1,65},{65,1},{2,66},{66,2},{3,67},{67,3},{4,68},{68... | collective-permute-start | bytes 1179656 | tf_op jit(solution)/shard_map/ppermute | solution.py:75
  265.8 8.7 %collective-permute-start.6 = (bf16[192,1024]{1,0:T(8,128)(2,1)}, bf16[192,1024]{1,0:T(8,128)(2,1)S(1)}, u32[]{:S(2)}, u32[]{:S(2)}) collective-permute-start(bf16[192,1024]{1,0:T(8,128)(2,1)} %bitcast.60), channel_id=1, source_target_pairs={{0,64},{64,0},{1,65},{65,1},{2,66},{66,2},{3,67},{67,3},{4,68},{68... | collective-permute-start | bytes 1179656 | tf_op jit(solution)/shard_map/ppermute | solution.py:75
  269.0 6.5 %collective-permute-start.4 = (bf16[192,1792]{1,0:T(8,128)(2,1)S(1)}, bf16[192,1792]{1,0:T(8,128)(2,1)S(1)}, u32[]{:S(2)}, u32[]{:S(2)}) collective-permute-start(bf16[192,1792]{1,0:T(8,128)(2,1)S(1)} %bitcast.55), channel_id=1, source_target_pairs={{0,64},{64,0},{1,65},{65,1},{2,66},{66,2},{3,67},{67,3},{4,68},{68... | collective-permute-start | bytes 2064392 | tf_op jit(solution)/shard_map/ppermute | solution.py:75
  274.1 25.3 %collective-permute-start.5 = (bf16[192,1792]{1,0:T(8,128)(2,1)S(1)}, bf16[192,1792]{1,0:T(8,128)(2,1)}, u32[]{:S(2)}, u32[]{:S(2)}) collective-permute-start(bf16[192,1792]{1,0:T(8,128)(2,1)S(1)} %bitcast.56), channel_id=1, source_target_pairs={{0,64},{64,0},{1,65},{65,1},{2,66},{66,2},{3,67},{67,3},{4,68},{68... | collective-permute-start | bytes 2064392 | tf_op jit(solution)/shard_map/ppermute | solution.py:75
  295.9 13.1 %all-to-all-start.6 = ((bf16[8,24,1024]{2,1,0:T(8,128)(2,1)}), bf16[8,24,1024]{2,1,0:T(8,128)(2,1)S(1)}, u32[]{:S(2)}, u32[]{:S(2)}) async-start(bf16[8,24,1024]{2,1,0:T(8,128)(2,1)} %broadcast_in_dim.32), calls=%async_computation.6 | async-start | bytes 786432 | tf_op jit(solution)/shard_map/all_to_all | solution.py:30
  301.7 12.7 %copy-start.12 = (bf16[192,1024]{1,0:T(8,128)(2,1)S(1)}, bf16[192,1024]{1,0:T(8,128)(2,1)}, u32[]{:S(2)}) copy-start(bf16[192,1024]{1,0:T(8,128)(2,1)} %get-tuple-element.11) | copy-start | bytes 1179652
  310.6 14.1 %all-to-all-start.7 = ((bf16[8,24,1024]{2,1,0:T(8,128)(2,1)}), bf16[8,24,1024]{2,1,0:T(8,128)(2,1)S(1)}, u32[]{:S(2)}, u32[]{:S(2)}) async-start(bf16[8,24,1024]{2,1,0:T(8,128)(2,1)} %bitcast.13), calls=%async_computation.7 | async-start | bytes 786432 | tf_op jit(solution)/shard_map/all_to_all | solution.py:34
  314.4 5.5 %copy-start.7 = (bf16[192,1792]{1,0:T(8,128)(2,1)S(1)}, bf16[192,1792]{1,0:T(8,128)(2,1)}, u32[]{:S(2)}) copy-start(bf16[192,1792]{1,0:T(8,128)(2,1)} %get-tuple-element.9) | copy-start | bytes 2064388
  314.4 5.5 %copy-start.8 = (bf16[192,1792]{1,0:T(8,128)(2,1)S(1)}, bf16[192,1792]{1,0:T(8,128)(2,1)}, u32[]{:S(2)}) copy-start(bf16[192,1792]{1,0:T(8,128)(2,1)} %get-tuple-element.10) | copy-start | bytes 2064388
  314.4 5.5 %copy-start.10 = (bf16[192,1024]{1,0:T(8,128)(2,1)S(1)}, bf16[192,1024]{1,0:T(8,128)(2,1)}, u32[]{:S(2)}) copy-start(bf16[192,1024]{1,0:T(8,128)(2,1)} %get-tuple-element.13) | copy-start | bytes 1179652
  314.5 5.5 %copy-start.11 = (bf16[192,1024]{1,0:T(8,128)(2,1)S(1)}, bf16[192,1024]{1,0:T(8,128)(2,1)}, u32[]{:S(2)}) copy-start(bf16[192,1024]{1,0:T(8,128)(2,1)} %get-tuple-element.14) | copy-start | bytes 1179652
  320.0 5.8 %collective-permute-start.2 = (bf16[192,1024]{1,0:T(8,128)(2,1)S(1)}, bf16[192,1024]{1,0:T(8,128)(2,1)}, u32[]{:S(2)}, u32[]{:S(2)}) collective-permute-start(bf16[192,1024]{1,0:T(8,128)(2,1)S(1)} %bitcast.52), channel_id=1, source_target_pairs={{0,64},{64,0},{1,65},{65,1},{2,66},{66,2},{3,67},{67,3},{4,68},{68... | collective-permute-start | bytes 1179656 | tf_op jit(solution)/shard_map/ppermute | solution.py:75
  320.0 4.0 %copy-start.6 = (bf16[152,1024]{1,0:T(8,128)(2,1)S(1)}, bf16[152,1024]{1,0:T(8,128)(2,1)}, u32[]{:S(2)}) copy-start(bf16[152,1024]{1,0:T(8,128)(2,1)} %copy-done.5) | copy-start | bytes 933892
  (6 other events, 17.5 us)

commit v4 on v3

--- a/solution.py
+++ b/solution.py
@@ -94,7 +94,21 @@
     crossed = [(r * GROUP + c, c * GROUP + r) for r in range(GROUP) for c in range(GROUP)]
     col_pos = lax.ppermute(masked_pos, ("row", "col"), crossed)
 
-    ctx = gather(context, "col")
+    ahead = lax.cond(
+        core == 0,
+        lambda rows: gather(rows, "col"),
+        lambda rows: jnp.zeros((GROUP,) + rows.shape, rows.dtype),
+        context,
+    )
+    turn = lax.ppermute(ahead[0, :8, :128], "dp", [(0, 1)])
+    context = jnp.where(turn[:1, :1] == jnp.inf, jnp.zeros_like(context), context)
+    ctx = lax.cond(
+        core == 0,
+        lambda rows, done: done,
+        lambda rows, done: gather(rows, "col"),
+        context,
+        ahead,
+    )
     noted = jnp.pad(
         masked_pos.astype(jnp.bfloat16),
         [(MASKED, HEAD - MASKED - 1), (0, cotangent.shape[1] - MASKED)],
@@ -119,22 +133,22 @@
     down_part = replace_tail(
         product(col_full, down_weight, 0), product(hidden_full, up_weight, 1)
     )
+    wide = heads(positions, SEQ + HEAD)
+    ctx_head = select_each(heads(positions, SEQ), ctx)
+    proj_head = select_each(wide, row_full)
+    act_head = select_each(wide, col_full)
+    held = (ctx_head, proj_head, act_head, hidden_full, grad_full)
+    held, down_part = lax.optimization_barrier((held, down_part))
+    ctx_head, proj_head, act_head, hidden_full, grad_full = held
     out_sum = scatter_sum(down_part, "row").astype(jnp.bfloat16)
+    down_grad = token_product(act_head, grad_full, core)
+    up_grad = token_product(proj_head, hidden_full, core)
+    down_grad, up_grad, out_sum = lax.optimization_barrier((down_grad, up_grad, out_sum))
     block_out = out_sum[:SEQ]
     gproj_full = gather(out_sum[SEQ:], "row")
     grad_ctx = scatter_sum(product(gproj_full, out_weight, 1), "col").astype(jnp.bfloat16)
     context_grad = select(col_heads, grad_ctx, 0)
-
-    out_grad = token_product(
-        select_each(heads(positions, SEQ), ctx), gproj_full, core
-    )
-    up_grad = token_product(
-        select_each(heads(positions, SEQ + HEAD), row_full), hidden_full, core
-    )
-    grad_full = jnp.where(live[None, :, None], grad_full, jnp.zeros_like(grad_full))
-    down_grad = token_product(
-        select_each(heads(positions, SEQ + HEAD), col_full), grad_full, core
-    )
+    out_grad = token_product(ctx_head, gproj_full, core)
     return (block_out, context_grad, out_grad, up_grad, down_grad)
 
 

time: 333 us -> 308 us (0.925)
  waiting for transfers between devices: 180 us -> 122 us
  blocking collectives: 33.4 us -> 57.3 us
  starting transfers between devices: 36.4 us -> 55.3 us
  other arithmetic: 19 us -> 12.1 us
  matrix products: 50.4 us -> 47 us
    all_to_all x3 -> x2, waiting for transfers between devices: 87.3 us -> 43.5 us  [gather(): return lax.all_to_all(copies, axis, 0, 0)]
    ppermute x6, starting transfers between devices: 1.28 us -> 26 us  [both_replicas(): other = lax.ppermute(values, 'dp', CORES)]
    all_to_all x1 -> x2, blocking collectives: 33.4 us -> 57.3 us  [gather(): return lax.all_to_all(copies, axis, 0, 0)]
    all_to_all x4, waiting for transfers between devices: 91.4 us -> 76.6 us  [scatter_sum(): lax.all_to_all(blocks, axis, 0, 0).astype(jnp.float32)]
    select_n x6, other arithmetic: 9.62 us -> 4.53 us  [both_replicas(): jnp.where(first, values, other)]
    all_to_all x3 -> x2, starting transfers between devices: 12.4 us -> 8.22 us  [gather(): return lax.all_to_all(copies, axis, 0, 0)]
    dot_general x6, matrix products: 29.2 us -> 25.2 us  [product(): lax.dot_general(flat(blocks), weight, (((1,), (contract,)), ((), ())), pr...]
  transfers between devices with their start and end apart: 14 -> 14, of which waited for: 7 -> 8; matrix products, arithmetic and copies ran while one was open for 9% -> 7% of each run, Pallas kernels for 0% -> 0%
where the time goes in v4:
time: 308 us; the launch traced here: 307 us
  waiting for transfers between devices  122 us (40%)
  blocking collectives  57.3 us (19%)
  starting transfers between devices  55.3 us (18%)
  matrix products  47 us (15%)
  other arithmetic  12.1 us (4%)
  local copies, waits for them, and re-layouts  11.8 us (4%)
    all_to_all x4, waiting for transfers between devices, scatter_sum(): lax.all_to_all(blocks, axis, 0, 0).astype(jnp.float32)  76.6 us
    all_to_all x2, blocking collectives, gather(): return lax.all_to_all(copies, axis, 0, 0)  57.3 us
    all_to_all x2, waiting for transfers between devices, gather(): return lax.all_to_all(copies, axis, 0, 0)  43.5 us
    ppermute x6, starting transfers between devices, both_replicas(): other = lax.ppermute(values, 'dp', CORES)  26 us
    dot_general x6, matrix products, product(): lax.dot_general(flat(blocks), weight, (((1,), (contract,)), ((), ())), pr...  25.2 us
    all_to_all x4, starting transfers between devices, scatter_sum(): lax.all_to_all(blocks, axis, 0, 0).astype(jnp.float32)  19.2 us
    dot_general x3, matrix products, token_product(): lax.dot_general(both_replicas(flat(left), core), both_replicas(flat(right...  11.5 us
    dot_general x3, matrix products, select_each(): lax.dot_general(matrix, values, (((2,), (1,)), ((0,), (0,))), preferred_e...  8.79 us
  transfers between devices with their start and end apart: 14, of which 8 were waited for; matrix products, arithmetic and copies ran while one was open for 7% of the time, Pallas kernels for 0%

profile of v4, /device:TPU:0, one launch (start us, length us, event | category | flops | bytes accessed | tf_op | source)
XLA Modules:
  0.0 306.9 jit_solution(10869935272982521545)
XLA Ops:
  0.7 24.7 %conditional.2 = (bf16[8,128,1024]{2,1,0:T(8,128)(2,1)}) conditional(s32[]{:T(128)} %convert_element_type.84, () %tuple.34, bf16[128,1024]{1,0:T(8,128)(2,1)} %param.10), branch_computations={%region_0.0_spmd, %region_1.0_spmd} | conditional | bytes 6553608 | solution.py:97
  2.0 23.3 %all_to_all.43 = bf16[8,128,1024]{2,1,0:T(8,128)(2,1)} all-to-all(bf16[8,128,1024]{2,1,0:T(8,128)(2,1)S(1)} %broadcast_in_dim.31), channel_id=1, replica_groups=mesh['dp'=2,'row'=8,'col'=8] {'col'}, dimensions={0} | all-to-all | bytes 4194304 | tf_op jit(solution)/shard_map/cond/branch_1_fun/all_to_all | solution.py:30
  28.1 5.2 %convolution_convert_fusion.8 = bf16[1024,1024]{1,0:T(8,128)(2,1)} fusion(bf16[1024,1024]{1,0:T(8,128)(2,1)} %bitcast.55, bf16[1024,1024]{1,0:T(8,128)(2,1)S(1)} %copy-done), kind=kOutput, calls=%fused_computation.11 | convolution fusion | flops 2148532224 | bytes 6291456 | tf_op jit(solution)/shard_map/dot_general | solution.py:38
  33.3 6.8 %all-to-all-start.2 = ((bf16[8,128,1024]{2,1,0:T(8,128)(2,1)}), bf16[8,128,1024]{2,1,0:T(8,128)(2,1)}, u32[]{:S(2)}, u32[]{:S(2)}) async-start(bf16[8,128,1024]{2,1,0:T(8,128)(2,1)} %bitcast.65), calls=%async_computation.2 | async-start | bytes 4194304 | tf_op jit(solution)/shard_map/all_to_all | solution.py:34
  40.3 22.4 %all-to-all-done.2 = bf16[8,128,1024]{2,1,0:T(8,128)(2,1)} async-done(((bf16[8,128,1024]{2,1,0:T(8,128)(2,1)}), bf16[8,128,1024]{2,1,0:T(8,128)(2,1)}, u32[]{:S(2)}, u32[]{:S(2)}) %all-to-all-start.2) | async-done | bytes 2097184 | tf_op jit(solution)/shard_map/all_to_all | solution.py:34
  65.1 33.9 %all_to_all.45 = bf16[8,152,1024]{2,1,0:T(8,128)(2,1)S(1)} all-to-all(bf16[8,152,1024]{2,1,0:T(8,128)(2,1)S(1)} %broadcast_in_dim.45), channel_id=1, replica_groups=mesh['dp'=2,'row'=8,'col'=8] {'row'}, dimensions={0} | all-to-all | bytes 4980736 | tf_op jit(solution)/shard_map/all_to_all | solution.py:30
  102.0 6.3 %convolution_convert_fusion = bf16[1216,1792]{1,0:T(8,128)(2,1)} fusion(bf16[1216,1024]{1,0:T(8,128)(2,1)S(1)} %bitcast.54, bf16[1024,1792]{1,0:T(8,128)(2,1)S(1)} %copy-done.11), kind=kOutput, calls=%fused_computation.2 | convolution fusion | flops 4464918528 | bytes 10518528 | tf_op jit(solution)/shard_map/dot_general | solution.py:38
  109.2 4.6 %all-to-all-start.4 = ((bf16[8,152,1792]{2,1,0:T(8,128)(2,1)}), bf16[8,152,1792]{2,1,0:T(8,128)(2,1)}, u32[]{:S(2)}, u32[]{:S(2)}) async-start(bf16[8,152,1792]{2,1,0:T(8,128)(2,1)} %constant_dynamic-update-slice_fusion.1), calls=%async_computation.4 | async-start | bytes 8716288 | tf_op jit(solution)/shard_map/all_to_all | solution.py:34
  114.5 28.6 %all-to-all-done.4 = bf16[8,152,1792]{2,1,0:T(8,128)(2,1)} async-done(((bf16[8,152,1792]{2,1,0:T(8,128)(2,1)}), bf16[8,152,1792]{2,1,0:T(8,128)(2,1)}, u32[]{:S(2)}, u32[]{:S(2)}) %all-to-all-start.4) | async-done | bytes 4358176 | tf_op jit(solution)/shard_map/all_to_all | solution.py:34
  149.0 4.8 %all-to-all-start.5 = ((bf16[8,152,1792]{2,1,0:T(8,128)(2,1)}), bf16[8,152,1792]{2,1,0:T(8,128)(2,1)}, u32[]{:S(2)}, u32[]{:S(2)}) async-start(bf16[8,152,1792]{2,1,0:T(8,128)(2,1)} %broadcast_in_dim.48), calls=%async_computation.5 | async-start | bytes 8716288 | tf_op jit(solution)/shard_map/all_to_all | solution.py:30
  158.8 33.9 %all-to-all-done.5 = bf16[8,152,1792]{2,1,0:T(8,128)(2,1)} async-done(((bf16[8,152,1792]{2,1,0:T(8,128)(2,1)}), bf16[8,152,1792]{2,1,0:T(8,128)(2,1)}, u32[]{:S(2)}, u32[]{:S(2)}) %all-to-all-start.5) | async-done | bytes 4358176 | tf_op jit(solution)/shard_map/all_to_all | solution.py:30
  193.8 3.5 %convolution_convert_fusion.10 = bf16[192,1024]{1,0:T(8,128)(2,1)S(1)} fusion(bf16[192,1792]{1,0:T(8,128)(2,1)S(1)} %bitcast.61, bf16[1024,1792]{1,0:T(8,128)(2,1)} %param.12), kind=kOutput, calls=%fused_computation.24 | convolution fusion | flops 704839680 | bytes 4751360 | tf_op jit(solution)/shard_map/dot_general | solution.py:38
  197.4 7.2 %convolution_convert_fusion.3 = bf16[1216,1024]{1,0:T(8,128)(2,1)S(1)} fusion(bf16[1216,1792]{1,0:T(8,128)(2,1)} %bitcast.10, bf16[1792,1024]{1,0:T(8,128)(2,1)S(1)} %copy-done.4), kind=kOutput, calls=%fused_computation.5 | convolution fusion | flops 4463984640 | bytes 10518528 | tf_op jit(solution)/shard_map/dot_general | solution.py:38
  204.6 4.7 %convolution_convert_fusion.4 = bf16[8,24,1792]{2,1,0:T(8,128)(2,1)} fusion(bf16[8,152,1792]{2,1,0:T(8,128)(2,1)} %all-to-all-done.5, s32[8,24]{1,0:T(8,128)S(1)} %pad_convert_fusion), kind=kOutput, calls=%fused_computation.6 | convolution fusion | flops 104968704 | bytes 5047040 | tf_op jit(solution)/shard_map/dot_general | solution.py:59
  209.3 25.1 %collective-permute-start.4 = (bf16[192,1024]{1,0:T(8,128)(2,1)}, bf16[192,1024]{1,0:T(8,128)(2,1)}, u32[]{:S(2)}, u32[]{:S(2)}) collective-permute-start(bf16[192,1024]{1,0:T(8,128)(2,1)} %bitcast.16), channel_id=1, source_target_pairs={{0,64},{64,0},{1,65},{65,1},{2,66},{66,2},{3,67},{67,3},{4,68},{68... | collective-permute-start | bytes 1179656 | tf_op jit(solution)/shard_map/ppermute | solution.py:75
  234.4 4.4 %all-to-all-start.6 = ((bf16[8,152,1024]{2,1,0:T(8,128)(2,1)}), bf16[8,152,1024]{2,1,0:T(8,128)(2,1)}, u32[]{:S(2)}, u32[]{:S(2)}) async-start(bf16[8,152,1024]{2,1,0:T(8,128)(2,1)} %copy-done.6), calls=%async_computation.6 | async-start | bytes 4980736 | tf_op jit(solution)/shard_map/all_to_all | solution.py:34
  242.4 4.0 %convolution_convert_fusion.1 = bf16[1024,1792]{1,0:T(8,128)(2,1)} fusion(bf16[192,1792]{1,0:T(8,128)(2,1)S(1)} %get-tuple-element.52, bf16[192,1792]{1,0:T(8,128)(2,1)S(1)} %get-tuple-element.51, bf16[192,1024]{1,0:T(8,128)(2,1)S(1)} %get-tuple-element.60, bf16[192,1024]{1,0:T(8,128)(2,1)S(1)} %get-tuple-element.59), kind=kOutput, calls=%fused_computation.3 | convolution fusion | flops 1415446528 | bytes 5832704 | tf_op jit(solution)/shard_map/dot_general | solution.py:83
  246.5 3.9 %convolution_convert_fusion.2 = bf16[1792,1024]{1,0:T(8,128)(2,1)} fusion(bf16[192,1792]{1,0:T(8,128)(2,1)S(1)} %get-tuple-element.54, bf16[192,1792]{1,0:T(8,128)(2,1)S(1)} %get-tuple-element.53, bf16[192,1024]{1,0:T(8,128)(2,1)S(1)} %get-tuple-element.62, bf16[192,1024]{1,0:T(8,128)(2,1)S(1)} %get-tuple-element.61), kind=kOutput, calls=%fused_computation.4 | convolution fusion | flops 1415446528 | bytes 5832704 | tf_op jit(solution)/shard_map/dot_general | solution.py:83
  250.4 21.5 %all-to-all-done.6 = bf16[8,152,1024]{2,1,0:T(8,128)(2,1)} async-done(((bf16[8,152,1024]{2,1,0:T(8,128)(2,1)}), bf16[8,152,1024]{2,1,0:T(8,128)(2,1)}, u32[]{:S(2)}, u32[]{:S(2)}) %all-to-all-start.6) | async-done | bytes 2490400 | tf_op jit(solution)/shard_map/all_to_all | solution.py:34
  275.0 3.5 %all-to-all-start.7 = ((bf16[8,24,1024]{2,1,0:T(8,128)(2,1)}), bf16[8,24,1024]{2,1,0:T(8,128)(2,1)S(1)}, u32[]{:S(2)}, u32[]{:S(2)}) async-start(bf16[8,24,1024]{2,1,0:T(8,128)(2,1)} %broadcast_in_dim.49), calls=%async_computation.7 | async-start | bytes 786432 | tf_op jit(solution)/shard_map/all_to_all | solution.py:30
  278.5 9.6 %all-to-all-done.7 = bf16[8,24,1024]{2,1,0:T(8,128)(2,1)S(1)} async-done(((bf16[8,24,1024]{2,1,0:T(8,128)(2,1)}), bf16[8,24,1024]{2,1,0:T(8,128)(2,1)S(1)}, u32[]{:S(2)}, u32[]{:S(2)}) %all-to-all-start.7) | async-done | bytes 393248 | tf_op jit(solution)/shard_map/all_to_all | solution.py:30
  289.7 3.5 %all-to-all-start.8 = ((bf16[8,24,1024]{2,1,0:T(8,128)(2,1)}), bf16[8,24,1024]{2,1,0:T(8,128)(2,1)S(1)}, u32[]{:S(2)}, u32[]{:S(2)}) async-start(bf16[8,24,1024]{2,1,0:T(8,128)(2,1)} %bitcast.67), calls=%async_computation.8 | async-start | bytes 786432 | tf_op jit(solution)/shard_map/all_to_all | solution.py:34
  296.9 4.1 %all-to-all-done.8 = bf16[8,24,1024]{2,1,0:T(8,128)(2,1)S(1)} async-done(((bf16[8,24,1024]{2,1,0:T(8,128)(2,1)}), bf16[8,24,1024]{2,1,0:T(8,128)(2,1)S(1)}, u32[]{:S(2)}, u32[]{:S(2)}) %all-to-all-start.8) | async-done | bytes 393248 | tf_op jit(solution)/shard_map/all_to_all | solution.py:34
  303.3 3.6 %convolution_convert_fusion.7 = bf16[1024,1024]{1,0:T(8,128)(2,1)} fusion(bf16[192,1024]{1,0:T(8,128)(2,1)} %get-tuple-element.58, bf16[192,1024]{1,0:T(8,128)(2,1)S(1)} %copy-done.9, bf16[192,1024]{1,0:T(8,128)(2,1)S(1)} %get-tuple-element.56, bf16[192,1024]{1,0:T(8,128)(2,1)S(1)} %get-tuple-element.55), kind=kOutput, calls=%fused_computation.10 | convolution fusion | flops 809500672 | bytes 3670016 | tf_op jit(solution)/shard_map/dot_general | solution.py:83
  (80 shorter events, 37.5 us)
Async XLA Ops:
  0.6 27.5 %copy-start = (bf16[1024,1024]{1,0:T(8,128)(2,1)S(1)}, bf16[1024,1024]{1,0:T(8,128)(2,1)}, u32[]{:S(2)}) copy-start(bf16[1024,1024]{1,0:T(8,128)(2,1)} %param.11) | copy-start | bytes 6291460
  26.0 2.1 collective-permute-start
  33.3 6.8 %copy-start.12 = (s32[1,20]{1,0:T(1,128)S(1)}, s32[1,20]{1,0:T(1,128)}, u32[]{:S(2)}) copy-start(s32[1,20]{1,0:T(1,128)} %param.15) | copy-start | bytes 244
  33.3 6.8 %copy-start.10 = (bf16[128,1024]{1,0:T(8,128)(2,1)S(1)}, bf16[128,1024]{1,0:T(8,128)(2,1)}, u32[]{:S(2)}) copy-start(bf16[128,1024]{1,0:T(8,128)(2,1)} %param.14) | copy-start | bytes 786436
  33.3 29.4 %all-to-all-start.2 = ((bf16[8,128,1024]{2,1,0:T(8,128)(2,1)}), bf16[8,128,1024]{2,1,0:T(8,128)(2,1)}, u32[]{:S(2)}, u32[]{:S(2)}) async-start(bf16[8,128,1024]{2,1,0:T(8,128)(2,1)} %bitcast.65), calls=%async_computation.2 | async-start | bytes 4194304 | tf_op jit(solution)/shard_map/all_to_all | solution.py:34
  65.1 34.0 %copy-start.3 = (bf16[1792,1024]{1,0:T(8,128)(2,1)S(1)}, bf16[1792,1024]{1,0:T(8,128)(2,1)}, u32[]{:S(2)}) copy-start(bf16[1792,1024]{1,0:T(8,128)(2,1)} %param.13) | copy-start | bytes 11010052
  109.2 33.9 %all-to-all-start.4 = ((bf16[8,152,1792]{2,1,0:T(8,128)(2,1)}), bf16[8,152,1792]{2,1,0:T(8,128)(2,1)}, u32[]{:S(2)}, u32[]{:S(2)}) async-start(bf16[8,152,1792]{2,1,0:T(8,128)(2,1)} %constant_dynamic-update-slice_fusion.1), calls=%async_computation.4 | async-start | bytes 8716288 | tf_op jit(solution)/shard_map/all_to_all | solution.py:34
  113.8 0.7 collective-permute-start.1
  149.0 43.6 %all-to-all-start.5 = ((bf16[8,152,1792]{2,1,0:T(8,128)(2,1)}), bf16[8,152,1792]{2,1,0:T(8,128)(2,1)}, u32[]{:S(2)}, u32[]{:S(2)}) async-start(bf16[8,152,1792]{2,1,0:T(8,128)(2,1)} %broadcast_in_dim.48), calls=%async_computation.5 | async-start | bytes 8716288 | tf_op jit(solution)/shard_map/all_to_all | solution.py:30
  153.8 3.7 %copy-start.2 = (bf16[8,152,1024]{2,1,0:T(8,128)(2,1)S(1)}, bf16[8,152,1024]{2,1,0:T(8,128)(2,1)}, u32[]{:S(2)}) copy-start(bf16[8,152,1024]{2,1,0:T(8,128)(2,1)} %copy-done.1) | copy-start | bytes 7471108
  193.8 3.5 %copy-start.4 = (bf16[1792,1024]{1,0:T(8,128)(2,1)S(1)}, bf16[1792,1024]{1,0:T(8,128)(2,1)}, u32[]{:S(2)}) copy-start(bf16[1792,1024]{1,0:T(8,128)(2,1)} %param.13) | copy-start | bytes 11010052
  204.6 4.8 %copy-start.6 = (bf16[8,152,1024]{2,1,0:T(8,128)(2,1)}, bf16[8,152,1024]{2,1,0:T(8,128)(2,1)S(1)}, u32[]{:S(2)}) copy-start(bf16[8,152,1024]{2,1,0:T(8,128)(2,1)S(1)} %constant_dynamic-update-slice_fusion) | copy-start | bytes 7471108
  209.3 30.2 %collective-permute-start.4 = (bf16[192,1024]{1,0:T(8,128)(2,1)}, bf16[192,1024]{1,0:T(8,128)(2,1)}, u32[]{:S(2)}, u32[]{:S(2)}) collective-permute-start(bf16[192,1024]{1,0:T(8,128)(2,1)} %bitcast.16), channel_id=1, source_target_pairs={{0,64},{64,0},{1,65},{65,1},{2,66},{66,2},{3,67},{67,3},{4,68},{68... | collective-permute-start | bytes 1179656 | tf_op jit(solution)/shard_map/ppermute | solution.py:75
  234.4 37.5 %all-to-all-start.6 = ((bf16[8,152,1024]{2,1,0:T(8,128)(2,1)}), bf16[8,152,1024]{2,1,0:T(8,128)(2,1)}, u32[]{:S(2)}, u32[]{:S(2)}) async-start(bf16[8,152,1024]{2,1,0:T(8,128)(2,1)} %copy-done.6), calls=%async_computation.6 | async-start | bytes 4980736 | tf_op jit(solution)/shard_map/all_to_all | solution.py:34
  238.8 3.4 %collective-permute-start.5 = (bf16[192,1792]{1,0:T(8,128)(2,1)S(1)}, bf16[192,1792]{1,0:T(8,128)(2,1)S(1)}, u32[]{:S(2)}, u32[]{:S(2)}) collective-permute-start(bf16[192,1792]{1,0:T(8,128)(2,1)S(1)} %bitcast.62), channel_id=1, source_target_pairs={{0,64},{64,0},{1,65},{65,1},{2,66},{66,2},{3,67},{67,3},{4,68},{68... | collective-permute-start | bytes 2064392 | tf_op jit(solution)/shard_map/ppermute | solution.py:75
  238.9 3.3 %collective-permute-start.3 = (bf16[192,1024]{1,0:T(8,128)(2,1)S(1)}, bf16[192,1024]{1,0:T(8,128)(2,1)S(1)}, u32[]{:S(2)}, u32[]{:S(2)}) collective-permute-start(bf16[192,1024]{1,0:T(8,128)(2,1)S(1)} %bitcast.57), channel_id=1, source_target_pairs={{0,64},{64,0},{1,65},{65,1},{2,66},{66,2},{3,67},{67,3},{4,68},{68... | collective-permute-start | bytes 1179656 | tf_op jit(solution)/shard_map/ppermute | solution.py:75
  239.4 7.0 %collective-permute-start.2 = (bf16[192,1792]{1,0:T(8,128)(2,1)}, bf16[192,1792]{1,0:T(8,128)(2,1)S(1)}, u32[]{:S(2)}, u32[]{:S(2)}) collective-permute-start(bf16[192,1792]{1,0:T(8,128)(2,1)} %bitcast.63), channel_id=1, source_target_pairs={{0,64},{64,0},{1,65},{65,1},{2,66},{66,2},{3,67},{67,3},{4,68},{68... | collective-permute-start | bytes 2064392 | tf_op jit(solution)/shard_map/ppermute | solution.py:75
  242.4 4.0 %copy-start.5 = (bf16[8,24,1792]{2,1,0:T(8,128)(2,1)S(1)}, bf16[8,24,1792]{2,1,0:T(8,128)(2,1)}, u32[]{:S(2)}) copy-start(bf16[8,24,1792]{2,1,0:T(8,128)(2,1)} %convolution_convert_fusion.4) | copy-start | bytes 2064388
  250.4 28.0 %copy-start.7 = (bf16[8,24,1024]{2,1,0:T(8,128)(2,1)S(1)}, bf16[8,24,1024]{2,1,0:T(8,128)(2,1)}, u32[]{:S(2)}) copy-start(bf16[8,24,1024]{2,1,0:T(8,128)(2,1)} %convolution_convert_fusion.12) | copy-start | bytes 1179652
  275.0 13.1 %all-to-all-start.7 = ((bf16[8,24,1024]{2,1,0:T(8,128)(2,1)}), bf16[8,24,1024]{2,1,0:T(8,128)(2,1)S(1)}, u32[]{:S(2)}, u32[]{:S(2)}) async-start(bf16[8,24,1024]{2,1,0:T(8,128)(2,1)} %broadcast_in_dim.49), calls=%async_computation.7 | async-start | bytes 786432 | tf_op jit(solution)/shard_map/all_to_all | solution.py:30
  278.5 14.8 %collective-permute-start.6 = (bf16[192,1024]{1,0:T(8,128)(2,1)S(1)}, bf16[192,1024]{1,0:T(8,128)(2,1)}, u32[]{:S(2)}, u32[]{:S(2)}) collective-permute-start(bf16[192,1024]{1,0:T(8,128)(2,1)S(1)} %bitcast.66), channel_id=1, source_target_pairs={{0,64},{64,0},{1,65},{65,1},{2,66},{66,2},{3,67},{67,3},{4,68},{68... | collective-permute-start | bytes 1179656 | tf_op jit(solution)/shard_map/ppermute | solution.py:75
  289.7 11.4 %all-to-all-start.8 = ((bf16[8,24,1024]{2,1,0:T(8,128)(2,1)}), bf16[8,24,1024]{2,1,0:T(8,128)(2,1)S(1)}, u32[]{:S(2)}, u32[]{:S(2)}) async-start(bf16[8,24,1024]{2,1,0:T(8,128)(2,1)} %bitcast.67), calls=%async_computation.8 | async-start | bytes 786432 | tf_op jit(solution)/shard_map/all_to_all | solution.py:34
  293.2 9.0 %collective-permute-start.7 = (bf16[192,1024]{1,0:T(8,128)(2,1)S(1)}, bf16[192,1024]{1,0:T(8,128)(2,1)}, u32[]{:S(2)}, u32[]{:S(2)}) collective-permute-start(bf16[192,1024]{1,0:T(8,128)(2,1)S(1)} %bitcast.59), channel_id=1, source_target_pairs={{0,64},{64,0},{1,65},{65,1},{2,66},{66,2},{3,67},{67,3},{4,68},{68... | collective-permute-start | bytes 1179656 | tf_op jit(solution)/shard_map/ppermute | solution.py:75
  295.2 8.0 %copy-start.9 = (bf16[192,1024]{1,0:T(8,128)(2,1)S(1)}, bf16[192,1024]{1,0:T(8,128)(2,1)}, u32[]{:S(2)}) copy-start(bf16[192,1024]{1,0:T(8,128)(2,1)} %get-tuple-element.57) | copy-start | bytes 1179652
  (3 other events, 5.2 us)

commit v5 on v4

--- a/solution.py
+++ b/solution.py
@@ -94,19 +94,20 @@
     crossed = [(r * GROUP + c, c * GROUP + r) for r in range(GROUP) for c in range(GROUP)]
     col_pos = lax.ppermute(masked_pos, ("row", "col"), crossed)
 
+    copies = jnp.broadcast_to(context[None], (GROUP,) + context.shape)
     ahead = lax.cond(
         core == 0,
-        lambda rows: gather(rows, "col"),
-        lambda rows: jnp.zeros((GROUP,) + rows.shape, rows.dtype),
-        context,
+        lambda rows: lax.all_to_all(rows, "col", 0, 0),
+        lambda rows: jnp.zeros_like(rows),
+        copies,
     )
     turn = lax.ppermute(ahead[0, :8, :128], "dp", [(0, 1)])
-    context = jnp.where(turn[:1, :1] == jnp.inf, jnp.zeros_like(context), context)
+    copies, turn = lax.optimization_barrier((copies, turn))
     ctx = lax.cond(
         core == 0,
         lambda rows, done: done,
-        lambda rows, done: gather(rows, "col"),
-        context,
+        lambda rows, done: lax.all_to_all(rows, "col", 0, 0),
+        copies,
         ahead,
     )
     noted = jnp.pad(
@@ -114,6 +115,7 @@
         [(MASKED, HEAD - MASKED - 1), (0, cotangent.shape[1] - MASKED)],
     )
     grad_rows = select(heads(masked_pos[0], SEQ), cotangent, 1) + noted
+    grad_rows = jnp.where(turn[:1, :1] == jnp.inf, jnp.zeros_like(grad_rows), grad_rows)
 
     projected = scatter_sum(product(ctx, out_weight, 0), "row").astype(jnp.bfloat16)
     row_full = gather(jnp.concatenate([projected, grad_rows], axis=0), "row")
@@ -136,18 +138,17 @@
     wide = heads(positions, SEQ + HEAD)
     ctx_head = select_each(heads(positions, SEQ), ctx)
     proj_head = select_each(wide, row_full)
+    held = (ctx_head, proj_head, wide, hidden_full, grad_full)
+    held, down_part = lax.optimization_barrier((held, down_part))
+    ctx_head, proj_head, wide, hidden_full, grad_full = held
     act_head = select_each(wide, col_full)
-    held = (ctx_head, proj_head, act_head, hidden_full, grad_full)
-    held, down_part = lax.optimization_barrier((held, down_part))
-    ctx_head, proj_head, act_head, hidden_full, grad_full = held
     out_sum = scatter_sum(down_part, "row").astype(jnp.bfloat16)
+    block_out = out_sum[:SEQ]
     down_grad = token_product(act_head, grad_full, core)
-    up_grad = token_product(proj_head, hidden_full, core)
-    down_grad, up_grad, out_sum = lax.optimization_barrier((down_grad, up_grad, out_sum))
-    block_out = out_sum[:SEQ]
-    gproj_full = gather(out_sum[SEQ:], "row")
+    gproj_full, down_grad = lax.optimization_barrier((gather(out_sum[SEQ:], "row"), down_grad))
     grad_ctx = scatter_sum(product(gproj_full, out_weight, 1), "col").astype(jnp.bfloat16)
     context_grad = select(col_heads, grad_ctx, 0)
+    up_grad = token_product(proj_head, hidden_full, core)
     out_grad = token_product(ctx_head, gproj_full, core)
     return (block_out, context_grad, out_grad, up_grad, down_grad)
 

time: 308 us -> 291 us (0.945)
  waiting for transfers between devices: 122 us -> 87.5 us
  starting transfers between devices: 55.3 us -> 65.4 us
  other arithmetic: 12.1 us -> 16.3 us
    all_to_all x4, waiting for transfers between devices: 76.6 us -> 48.6 us  [scatter_sum(): lax.all_to_all(blocks, axis, 0, 0).astype(jnp.float32)]
    all_to_all x2 -> x1, blocking collectives: 57.3 us -> 32.9 us  [gather(): return lax.all_to_all(copies, axis, 0, 0)]
    all_to_all x0 -> x1, blocking collectives: none -> 23.5 us  [body(): lax.all_to_all(rows, 'col', 0, 0)]
    ppermute x6, starting transfers between devices: 26 us -> 32.5 us  [both_replicas(): other = lax.ppermute(values, 'dp', CORES)]
    all_to_all x2, waiting for transfers between devices: 43.5 us -> 38.1 us  [gather(): return lax.all_to_all(copies, axis, 0, 0)]
    select_n x6, other arithmetic: 4.53 us -> 8.66 us  [both_replicas(): jnp.where(first, values, other)]
    all_to_all x2, starting transfers between devices: 8.22 us -> 11.3 us  [gather(): return lax.all_to_all(copies, axis, 0, 0)]
  transfers between devices with their start and end apart: 14 -> 14, of which waited for: 8 -> 5; matrix products, arithmetic and copies ran while one was open for 7% -> 11% of each run, Pallas kernels for 0% -> 0%
where the time goes in v5:
time: 291 us; the launch traced here: 288 us
  waiting for transfers between devices  87.5 us (30%)
  starting transfers between devices  65.4 us (22%)
  blocking collectives  56.5 us (19%)
  matrix products  46.6 us (16%)
  other arithmetic  16.3 us (6%)
  local copies, waits for them, and re-layouts  14.2 us (5%)
    all_to_all x4, waiting for transfers between devices, scatter_sum(): lax.all_to_all(blocks, axis, 0, 0).astype(jnp.float32)  48.6 us
    all_to_all x2, waiting for transfers between devices, gather(): return lax.all_to_all(copies, axis, 0, 0)  38.1 us
    all_to_all x1, blocking collectives, gather(): return lax.all_to_all(copies, axis, 0, 0)  32.9 us
    ppermute x6, starting transfers between devices, both_replicas(): other = lax.ppermute(values, 'dp', CORES)  32.5 us
    dot_general x6, matrix products, product(): lax.dot_general(flat(blocks), weight, (((1,), (contract,)), ((), ())), pr...  26.4 us
    all_to_all x1, blocking collectives, body(): lax.all_to_all(rows, 'col', 0, 0)  23.5 us
    all_to_all x4, starting transfers between devices, scatter_sum(): lax.all_to_all(blocks, axis, 0, 0).astype(jnp.float32)  19.6 us
    dot_general x3, matrix products, token_product(): lax.dot_general(both_replicas(flat(left), core), both_replicas(flat(right...  11.6 us
  transfers between devices with their start and end apart: 14, of which 5 were waited for; matrix products, arithmetic and copies ran while one was open for 11% of the time, Pallas kernels for 0%

profile of v5, /device:TPU:0, one launch (start us, length us, event | category | flops | bytes accessed | tf_op | source)
XLA Modules:
  0.0 288.0 jit_solution(10917327471521717420)
XLA Ops:
  3.3 23.5 %conditional.2 = (bf16[8,128,1024]{2,1,0:T(8,128)(2,1)}) conditional(s32[]{:T(128)} %convert_element_type.86, () %tuple.33, bf16[8,128,1024]{2,1,0:T(8,128)(2,1)} %broadcast_in_dim.35), branch_computations={%region_0.0_spmd, %region_1.0_spmd} | conditional | bytes 4194312 | solution.py:98
  3.3 23.5 %all_to_all.43 = bf16[8,128,1024]{2,1,0:T(8,128)(2,1)} all-to-all(bf16[8,128,1024]{2,1,0:T(8,128)(2,1)} %param.1), channel_id=1, replica_groups=mesh['dp'=2,'row'=8,'col'=8] {'col'}, dimensions={0} | all-to-all | bytes 4194304 | tf_op jit(solution)/shard_map/cond/branch_1_fun/all_to_all | solution.py:100
  29.6 5.2 %convolution_convert_fusion.8 = bf16[1024,1024]{1,0:T(8,128)(2,1)} fusion(bf16[1024,1024]{1,0:T(8,128)(2,1)} %bitcast.56, bf16[1024,1024]{1,0:T(8,128)(2,1)S(1)} %copy-done), kind=kOutput, calls=%fused_computation.10 | convolution fusion | flops 2148532224 | bytes 6291456 | tf_op jit(solution)/shard_map/dot_general | solution.py:38
  34.8 6.8 %all-to-all-start.2 = ((bf16[8,128,1024]{2,1,0:T(8,128)(2,1)}), bf16[8,128,1024]{2,1,0:T(8,128)(2,1)}, u32[]{:S(2)}, u32[]{:S(2)}) async-start(bf16[8,128,1024]{2,1,0:T(8,128)(2,1)} %bitcast.63), calls=%async_computation.2 | async-start | bytes 4194304 | tf_op jit(solution)/shard_map/all_to_all | solution.py:34
  43.0 20.0 %all-to-all-done.2 = bf16[8,128,1024]{2,1,0:T(8,128)(2,1)} async-done(((bf16[8,128,1024]{2,1,0:T(8,128)(2,1)}), bf16[8,128,1024]{2,1,0:T(8,128)(2,1)}, u32[]{:S(2)}, u32[]{:S(2)}) %all-to-all-start.2) | async-done | bytes 2097184 | tf_op jit(solution)/shard_map/all_to_all | solution.py:34
  65.3 32.9 %all_to_all.45 = bf16[8,152,1024]{2,1,0:T(8,128)(2,1)S(1)} all-to-all(bf16[8,152,1024]{2,1,0:T(8,128)(2,1)S(1)} %broadcast_in_dim.39), channel_id=1, replica_groups=mesh['dp'=2,'row'=8,'col'=8] {'row'}, dimensions={0} | all-to-all | bytes 4980736 | tf_op jit(solution)/shard_map/all_to_all | solution.py:30
  101.2 6.3 %convolution_convert_fusion = bf16[1216,1792]{1,0:T(8,128)(2,1)} fusion(bf16[1216,1024]{1,0:T(8,128)(2,1)S(1)} %bitcast.55, bf16[1024,1792]{1,0:T(8,128)(2,1)S(1)} %copy-done.10), kind=kOutput, calls=%fused_computation.1 | convolution fusion | flops 4464918528 | bytes 10518528 | tf_op jit(solution)/shard_map/dot_general | solution.py:38
  108.4 4.6 %all-to-all-start.4 = ((bf16[8,152,1792]{2,1,0:T(8,128)(2,1)}), bf16[8,152,1792]{2,1,0:T(8,128)(2,1)}, u32[]{:S(2)}, u32[]{:S(2)}) async-start(bf16[8,152,1792]{2,1,0:T(8,128)(2,1)} %constant_dynamic-update-slice_fusion.1), calls=%async_computation.4 | async-start | bytes 8716288 | tf_op jit(solution)/shard_map/all_to_all | solution.py:34
  113.7 28.6 %all-to-all-done.4 = bf16[8,152,1792]{2,1,0:T(8,128)(2,1)} async-done(((bf16[8,152,1792]{2,1,0:T(8,128)(2,1)}), bf16[8,152,1792]{2,1,0:T(8,128)(2,1)}, u32[]{:S(2)}, u32[]{:S(2)}) %all-to-all-start.4) | async-done | bytes 4358176 | tf_op jit(solution)/shard_map/all_to_all | solution.py:34
  142.3 3.0 %convert_reduce_fusion = f32[152,1792]{1,0:T(8,128)S(1)} fusion(bf16[8,152,1792]{2,1,0:T(8,128)(2,1)} %all-to-all-done.4), kind=kLoop, calls=%fused_computation | loop fusion | flops 4085760 | bytes 5447680 | tf_op jit(solution)/shard_map/reduce_sum | solution.py:34
  148.3 4.6 %all-to-all-start.5 = ((bf16[8,152,1792]{2,1,0:T(8,128)(2,1)}), bf16[8,152,1792]{2,1,0:T(8,128)(2,1)}, u32[]{:S(2)}, u32[]{:S(2)}) async-start(bf16[8,152,1792]{2,1,0:T(8,128)(2,1)} %broadcast_in_dim.68), calls=%async_computation.5 | async-start | bytes 8716288 | tf_op jit(solution)/shard_map/all_to_all | solution.py:30
  158.0 33.8 %all-to-all-done.5 = bf16[8,152,1792]{2,1,0:T(8,128)(2,1)} async-done(((bf16[8,152,1792]{2,1,0:T(8,128)(2,1)}), bf16[8,152,1792]{2,1,0:T(8,128)(2,1)}, u32[]{:S(2)}, u32[]{:S(2)}) %all-to-all-start.5) | async-done | bytes 4358176 | tf_op jit(solution)/shard_map/all_to_all | solution.py:30
  193.8 3.7 %convolution_convert_fusion.10 = bf16[192,1024]{1,0:T(8,128)(2,1)S(1)} fusion(bf16[192,1792]{1,0:T(8,128)(2,1)} %bitcast.12, bf16[1024,1792]{1,0:T(8,128)(2,1)} %param.12), kind=kOutput, calls=%fused_computation.23 | convolution fusion | flops 704839680 | bytes 4751360 | tf_op jit(solution)/shard_map/dot_general | solution.py:38
  197.6 8.2 %convolution_convert_fusion.3 = bf16[1216,1024]{1,0:T(8,128)(2,1)} fusion(bf16[1216,1792]{1,0:T(8,128)(2,1)} %bitcast.10, bf16[1792,1024]{1,0:T(8,128)(2,1)S(1)} %copy-done.4), kind=kOutput, calls=%fused_computation.4 | convolution fusion | flops 4463984640 | bytes 10518528 | tf_op jit(solution)/shard_map/dot_general | solution.py:38
  206.5 4.6 %all-to-all-start.6 = ((bf16[8,152,1024]{2,1,0:T(8,128)(2,1)}), bf16[8,152,1024]{2,1,0:T(8,128)(2,1)}, u32[]{:S(2)}, u32[]{:S(2)}) async-start(bf16[8,152,1024]{2,1,0:T(8,128)(2,1)} %constant_dynamic-update-slice_fusion), calls=%async_computation.6 | async-start | bytes 4980736 | tf_op jit(solution)/shard_map/all_to_all | solution.py:34
  211.1 25.4 %collective-permute-start.6 = (bf16[192,1024]{1,0:T(8,128)(2,1)}, bf16[192,1024]{1,0:T(8,128)(2,1)S(1)}, u32[]{:S(2)}, u32[]{:S(2)}) collective-permute-start(bf16[192,1024]{1,0:T(8,128)(2,1)} %bitcast.19), channel_id=1, source_target_pairs={{0,64},{64,0},{1,65},{65,1},{2,66},{66,2},{3,67},{67,3},{4,68},{68... | collective-permute-start | bytes 1179656 | tf_op jit(solution)/shard_map/ppermute | solution.py:75
  237.0 3.0 %convolution_convert_fusion.4 = bf16[8,24,1792]{2,1,0:T(8,128)(2,1)S(1)} fusion(bf16[8,24,152]{2,1,0:T(8,128)(2,1)S(1)} %fusion.26, bf16[8,152,1792]{2,1,0:T(8,128)(2,1)} %all-to-all-done.5), kind=kOutput, calls=%fused_computation.5 | convolution fusion | flops 104939520 | bytes 5104640 | tf_op jit(solution)/shard_map/dot_general | solution.py:59
  248.4 6.7 %all-to-all-start.7 = ((bf16[8,24,1024]{2,1,0:T(8,128)(2,1)}), bf16[8,24,1024]{2,1,0:T(8,128)(2,1)S(1)}, u32[]{:S(2)}, u32[]{:S(2)}) async-start(bf16[8,24,1024]{2,1,0:T(8,128)(2,1)} %broadcast_in_dim.69), calls=%async_computation.7 | async-start | bytes 786432 | tf_op jit(solution)/shard_map/all_to_all | solution.py:30
  256.5 3.9 %convolution_convert_fusion.2 = bf16[1792,1024]{1,0:T(8,128)(2,1)} fusion(bf16[192,1792]{1,0:T(8,128)(2,1)S(1)} %get-tuple-element.43, bf16[192,1792]{1,0:T(8,128)(2,1)S(1)} %get-tuple-element.42, bf16[192,1024]{1,0:T(8,128)(2,1)S(1)} %copy-done.8, bf16[192,1024]{1,0:T(8,128)(2,1)S(1)} %copy-done.7), kind=kOutput, calls=%fused_computation.3 | convolution fusion | flops 1415446528 | bytes 5832704 | tf_op jit(solution)/shard_map/dot_general | solution.py:83
  260.4 4.2 %all-to-all-done.7 = bf16[8,24,1024]{2,1,0:T(8,128)(2,1)S(1)} async-done(((bf16[8,24,1024]{2,1,0:T(8,128)(2,1)}), bf16[8,24,1024]{2,1,0:T(8,128)(2,1)S(1)}, u32[]{:S(2)}, u32[]{:S(2)}) %all-to-all-start.7) | async-done | bytes 393248 | tf_op jit(solution)/shard_map/all_to_all | solution.py:30
  266.3 3.7 %all-to-all-start.8 = ((bf16[8,24,1024]{2,1,0:T(8,128)(2,1)}), bf16[8,24,1024]{2,1,0:T(8,128)(2,1)S(1)}, u32[]{:S(2)}, u32[]{:S(2)}) async-start(bf16[8,24,1024]{2,1,0:T(8,128)(2,1)} %bitcast.17), calls=%async_computation.8 | async-start | bytes 786432 | tf_op jit(solution)/shard_map/all_to_all | solution.py:34
  271.5 6.0 %collective-permute-start.5 = (bf16[192,1024]{1,0:T(8,128)(2,1)S(1)}, bf16[192,1024]{1,0:T(8,128)(2,1)}, u32[]{:S(2)}, u32[]{:S(2)}) collective-permute-start(bf16[192,1024]{1,0:T(8,128)(2,1)S(1)} %bitcast.60), channel_id=1, source_target_pairs={{0,64},{64,0},{1,65},{65,1},{2,66},{66,2},{3,67},{67,3},{4,68},{68... | collective-permute-start | bytes 1179656 | tf_op jit(solution)/shard_map/ppermute | solution.py:75
  277.4 3.9 %convolution_convert_fusion.1 = bf16[1024,1792]{1,0:T(8,128)(2,1)} fusion(bf16[192,1792]{1,0:T(8,128)(2,1)S(1)} %get-tuple-element.41, bf16[192,1792]{1,0:T(8,128)(2,1)S(1)} %get-tuple-element.40, bf16[192,1024]{1,0:T(8,128)(2,1)S(1)} %copy-done.6, bf16[192,1024]{1,0:T(8,128)(2,1)S(1)} %copy-done.5), kind=kOutput, calls=%fused_computation.2 | convolution fusion | flops 1415446528 | bytes 5832704 | tf_op jit(solution)/shard_map/dot_general | solution.py:83
  284.3 3.7 %convolution_convert_fusion.7 = bf16[1024,1024]{1,0:T(8,128)(2,1)} fusion(bf16[192,1024]{1,0:T(8,128)(2,1)} %get-tuple-element.49, bf16[192,1024]{1,0:T(8,128)(2,1)} %get-tuple-element.48, bf16[192,1024]{1,0:T(8,128)(2,1)S(1)} %get-tuple-element.47, bf16[192,1024]{1,0:T(8,128)(2,1)S(1)} %get-tuple-element.46), kind=kOutput, calls=%fused_computation.9 | convolution fusion | flops 809500672 | bytes 3670016 | tf_op jit(solution)/shard_map/dot_general | solution.py:83
  (80 shorter events, 40.0 us)
Async XLA Ops:
  0.6 29.0 %copy-start = (bf16[1024,1024]{1,0:T(8,128)(2,1)S(1)}, bf16[1024,1024]{1,0:T(8,128)(2,1)}, u32[]{:S(2)}) copy-start(bf16[1024,1024]{1,0:T(8,128)(2,1)} %param.11) | copy-start | bytes 6291460
  27.5 2.1 collective-permute-start
  34.8 6.8 %copy-start.11 = (s32[1,20]{1,0:T(1,128)S(1)}, s32[1,20]{1,0:T(1,128)}, u32[]{:S(2)}) copy-start(s32[1,20]{1,0:T(1,128)} %param.15) | copy-start | bytes 244
  34.8 8.0 %copy-start.9 = (bf16[128,1024]{1,0:T(8,128)(2,1)S(1)}, bf16[128,1024]{1,0:T(8,128)(2,1)}, u32[]{:S(2)}) copy-start(bf16[128,1024]{1,0:T(8,128)(2,1)} %param.14) | copy-start | bytes 786436
  34.8 28.2 %all-to-all-start.2 = ((bf16[8,128,1024]{2,1,0:T(8,128)(2,1)}), bf16[8,128,1024]{2,1,0:T(8,128)(2,1)}, u32[]{:S(2)}, u32[]{:S(2)}) async-start(bf16[8,128,1024]{2,1,0:T(8,128)(2,1)} %bitcast.63), calls=%async_computation.2 | async-start | bytes 4194304 | tf_op jit(solution)/shard_map/all_to_all | solution.py:34
  65.3 33.0 %copy-start.3 = (bf16[1792,1024]{1,0:T(8,128)(2,1)S(1)}, bf16[1792,1024]{1,0:T(8,128)(2,1)}, u32[]{:S(2)}) copy-start(bf16[1792,1024]{1,0:T(8,128)(2,1)} %param.13) | copy-start | bytes 11010052
  98.3 1.4 copy-start.1
  98.3 2.9 %copy-start.10 = (bf16[1024,1792]{1,0:T(8,128)(2,1)S(1)}, bf16[1024,1792]{1,0:T(8,128)(2,1)}, u32[]{:S(2)}) copy-start(bf16[1024,1792]{1,0:T(8,128)(2,1)} %param.12) | copy-start | bytes 11010052
  108.4 33.9 %all-to-all-start.4 = ((bf16[8,152,1792]{2,1,0:T(8,128)(2,1)}), bf16[8,152,1792]{2,1,0:T(8,128)(2,1)}, u32[]{:S(2)}, u32[]{:S(2)}) async-start(bf16[8,152,1792]{2,1,0:T(8,128)(2,1)} %constant_dynamic-update-slice_fusion.1), calls=%async_computation.4 | async-start | bytes 8716288 | tf_op jit(solution)/shard_map/all_to_all | solution.py:34
  113.0 0.7 collective-permute-start.1
  148.3 43.5 %all-to-all-start.5 = ((bf16[8,152,1792]{2,1,0:T(8,128)(2,1)}), bf16[8,152,1792]{2,1,0:T(8,128)(2,1)}, u32[]{:S(2)}, u32[]{:S(2)}) async-start(bf16[8,152,1792]{2,1,0:T(8,128)(2,1)} %broadcast_in_dim.68), calls=%async_computation.5 | async-start | bytes 8716288 | tf_op jit(solution)/shard_map/all_to_all | solution.py:30
  152.9 3.8 %copy-start.2 = (bf16[8,152,1024]{2,1,0:T(8,128)(2,1)S(1)}, bf16[8,152,1024]{2,1,0:T(8,128)(2,1)}, u32[]{:S(2)}) copy-start(bf16[8,152,1024]{2,1,0:T(8,128)(2,1)} %copy-done.1) | copy-start | bytes 7471108
  193.8 3.7 %copy-start.4 = (bf16[1792,1024]{1,0:T(8,128)(2,1)S(1)}, bf16[1792,1024]{1,0:T(8,128)(2,1)}, u32[]{:S(2)}) copy-start(bf16[1792,1024]{1,0:T(8,128)(2,1)} %param.13) | copy-start | bytes 11010052
  206.5 38.9 %all-to-all-start.6 = ((bf16[8,152,1024]{2,1,0:T(8,128)(2,1)}), bf16[8,152,1024]{2,1,0:T(8,128)(2,1)}, u32[]{:S(2)}, u32[]{:S(2)}) async-start(bf16[8,152,1024]{2,1,0:T(8,128)(2,1)} %constant_dynamic-update-slice_fusion), calls=%async_computation.6 | async-start | bytes 4980736 | tf_op jit(solution)/shard_map/all_to_all | solution.py:34
  211.1 29.5 %collective-permute-start.6 = (bf16[192,1024]{1,0:T(8,128)(2,1)}, bf16[192,1024]{1,0:T(8,128)(2,1)S(1)}, u32[]{:S(2)}, u32[]{:S(2)}) collective-permute-start(bf16[192,1024]{1,0:T(8,128)(2,1)} %bitcast.19), channel_id=1, source_target_pairs={{0,64},{64,0},{1,65},{65,1},{2,66},{66,2},{3,67},{67,3},{4,68},{68... | collective-permute-start | bytes 1179656 | tf_op jit(solution)/shard_map/ppermute | solution.py:75
  236.5 6.0 %collective-permute-start.4 = (bf16[192,1024]{1,0:T(8,128)(2,1)}, bf16[192,1024]{1,0:T(8,128)(2,1)S(1)}, u32[]{:S(2)}, u32[]{:S(2)}) collective-permute-start(bf16[192,1024]{1,0:T(8,128)(2,1)} %bitcast.18), channel_id=1, source_target_pairs={{0,64},{64,0},{1,65},{65,1},{2,66},{66,2},{3,67},{67,3},{4,68},{68... | collective-permute-start | bytes 1179656 | tf_op jit(solution)/shard_map/ppermute | solution.py:75
  236.6 7.9 %collective-permute-start.3 = (bf16[192,1024]{1,0:T(8,128)(2,1)S(1)}, bf16[192,1024]{1,0:T(8,128)(2,1)S(1)}, u32[]{:S(2)}, u32[]{:S(2)}) collective-permute-start(bf16[192,1024]{1,0:T(8,128)(2,1)S(1)} %bitcast.58), channel_id=1, source_target_pairs={{0,64},{64,0},{1,65},{65,1},{2,66},{66,2},{3,67},{67,3},{4,68},{68... | collective-permute-start | bytes 1179656 | tf_op jit(solution)/shard_map/ppermute | solution.py:75
  240.0 15.2 %collective-permute-start.2 = (bf16[192,1792]{1,0:T(8,128)(2,1)S(1)}, bf16[192,1792]{1,0:T(8,128)(2,1)}, u32[]{:S(2)}, u32[]{:S(2)}) collective-permute-start(bf16[192,1792]{1,0:T(8,128)(2,1)S(1)} %bitcast.61), channel_id=1, source_target_pairs={{0,64},{64,0},{1,65},{65,1},{2,66},{66,2},{3,67},{67,3},{4,68},{68... | collective-permute-start | bytes 2064392 | tf_op jit(solution)/shard_map/ppermute | solution.py:75
  240.1 29.8 %collective-permute-start.7 = (bf16[192,1792]{1,0:T(8,128)(2,1)}, bf16[192,1792]{1,0:T(8,128)(2,1)}, u32[]{:S(2)}, u32[]{:S(2)}) collective-permute-start(bf16[192,1792]{1,0:T(8,128)(2,1)} %bitcast.20), channel_id=1, source_target_pairs={{0,64},{64,0},{1,65},{65,1},{2,66},{66,2},{3,67},{67,3},{4,68},{68... | collective-permute-start | bytes 2064392 | tf_op jit(solution)/shard_map/ppermute | solution.py:75
  248.4 16.2 %all-to-all-start.7 = ((bf16[8,24,1024]{2,1,0:T(8,128)(2,1)}), bf16[8,24,1024]{2,1,0:T(8,128)(2,1)S(1)}, u32[]{:S(2)}, u32[]{:S(2)}) async-start(bf16[8,24,1024]{2,1,0:T(8,128)(2,1)} %broadcast_in_dim.69), calls=%async_computation.7 | async-start | bytes 786432 | tf_op jit(solution)/shard_map/all_to_all | solution.py:30
  266.3 15.8 %all-to-all-start.8 = ((bf16[8,24,1024]{2,1,0:T(8,128)(2,1)}), bf16[8,24,1024]{2,1,0:T(8,128)(2,1)S(1)}, u32[]{:S(2)}, u32[]{:S(2)}) async-start(bf16[8,24,1024]{2,1,0:T(8,128)(2,1)} %bitcast.17), calls=%async_computation.8 | async-start | bytes 786432 | tf_op jit(solution)/shard_map/all_to_all | solution.py:34
  270.0 7.5 %copy-start.5 = (bf16[192,1024]{1,0:T(8,128)(2,1)S(1)}, bf16[192,1024]{1,0:T(8,128)(2,1)}, u32[]{:S(2)}) copy-start(bf16[192,1024]{1,0:T(8,128)(2,1)} %get-tuple-element.44) | copy-start | bytes 1179652
  270.0 7.5 %copy-start.6 = (bf16[192,1024]{1,0:T(8,128)(2,1)S(1)}, bf16[192,1024]{1,0:T(8,128)(2,1)}, u32[]{:S(2)}) copy-start(bf16[192,1024]{1,0:T(8,128)(2,1)} %get-tuple-element.45) | copy-start | bytes 1179652
  271.5 11.7 %collective-permute-start.5 = (bf16[192,1024]{1,0:T(8,128)(2,1)S(1)}, bf16[192,1024]{1,0:T(8,128)(2,1)}, u32[]{:S(2)}, u32[]{:S(2)}) collective-permute-start(bf16[192,1024]{1,0:T(8,128)(2,1)S(1)} %bitcast.60), channel_id=1, source_target_pairs={{0,64},{64,0},{1,65},{65,1},{2,66},{66,2},{3,67},{67,3},{4,68},{68... | collective-permute-start | bytes 1179656 | tf_op jit(solution)/shard_map/ppermute | solution.py:75
  (2 other events, 2.6 us)

commit v6 on v5

--- a/solution.py
+++ b/solution.py
@@ -94,20 +94,18 @@
     crossed = [(r * GROUP + c, c * GROUP + r) for r in range(GROUP) for c in range(GROUP)]
     col_pos = lax.ppermute(masked_pos, ("row", "col"), crossed)
 
-    copies = jnp.broadcast_to(context[None], (GROUP,) + context.shape)
     ahead = lax.cond(
         core == 0,
-        lambda rows: lax.all_to_all(rows, "col", 0, 0),
-        lambda rows: jnp.zeros_like(rows),
-        copies,
+        lambda rows: gather(rows, "col"),
+        lambda rows: jnp.broadcast_to(rows[None], (GROUP,) + rows.shape),
+        context,
     )
     turn = lax.ppermute(ahead[0, :8, :128], "dp", [(0, 1)])
-    copies, turn = lax.optimization_barrier((copies, turn))
+    ahead, turn = lax.optimization_barrier((ahead, turn))
     ctx = lax.cond(
         core == 0,
-        lambda rows, done: done,
-        lambda rows, done: lax.all_to_all(rows, "col", 0, 0),
-        copies,
+        lambda done: done,
+        lambda copies: lax.all_to_all(copies, "col", 0, 0),
         ahead,
     )
     noted = jnp.pad(

time: 291 us -> 290 us (level)
    all_to_all x1 -> x2, blocking collectives: 32.9 us -> 56.6 us  [gather(): return lax.all_to_all(copies, axis, 0, 0)]
    all_to_all x1 -> x0, blocking collectives: 23.5 us -> none  [body(): lax.all_to_all(rows, 'col', 0, 0)]
where the time goes in v6:
time: 290 us; the launch traced here: 287 us
  waiting for transfers between devices  87.6 us (30%)
  starting transfers between devices  65.1 us (22%)
  blocking collectives  56.6 us (20%)
  matrix products  46.6 us (16%)
  other arithmetic  16.3 us (6%)
  local copies, waits for them, and re-layouts  12.9 us (4%)
    all_to_all x2, blocking collectives, gather(): return lax.all_to_all(copies, axis, 0, 0)  56.6 us
    all_to_all x4, waiting for transfers between devices, scatter_sum(): lax.all_to_all(blocks, axis, 0, 0).astype(jnp.float32)  49 us
    all_to_all x2, waiting for transfers between devices, gather(): return lax.all_to_all(copies, axis, 0, 0)  37.8 us
    ppermute x6, starting transfers between devices, both_replicas(): other = lax.ppermute(values, 'dp', CORES)  32.3 us
    dot_general x6, matrix products, product(): lax.dot_general(flat(blocks), weight, (((1,), (contract,)), ((), ())), pr...  26.4 us
    all_to_all x4, starting transfers between devices, scatter_sum(): lax.all_to_all(blocks, axis, 0, 0).astype(jnp.float32)  19.6 us
    dot_general x3, matrix products, token_product(): lax.dot_general(both_replicas(flat(left), core), both_replicas(flat(right...  11.6 us
    all_to_all x2, starting transfers between devices, gather(): return lax.all_to_all(copies, axis, 0, 0)  11.3 us
  transfers between devices with their start and end apart: 14, of which 5 were waited for; matrix products, arithmetic and copies ran while one was open for 11% of the time, Pallas kernels for 0%

profile of v6, /device:TPU:0, one launch (start us, length us, event | category | flops | bytes accessed | tf_op | source)
XLA Modules:
  0.0 286.8 jit_solution(981651083820532312)
XLA Ops:
  0.7 24.7 %conditional.2 = (bf16[8,128,1024]{2,1,0:T(8,128)(2,1)}) conditional(s32[]{:T(128)} %convert_element_type.86, bf16[128,1024]{1,0:T(8,128)(2,1)} %param.10, bf16[128,1024]{1,0:T(8,128)(2,1)} %param.10), branch_computations={%region_0.0_spmd, %region_1.0_spmd} | conditional | bytes 6553608 | solution.py:97
  2.0 23.3 %all_to_all.43 = bf16[8,128,1024]{2,1,0:T(8,128)(2,1)} all-to-all(bf16[8,128,1024]{2,1,0:T(8,128)(2,1)S(1)} %broadcast_in_dim.29), channel_id=1, replica_groups=mesh['dp'=2,'row'=8,'col'=8] {'col'}, dimensions={0} | all-to-all | bytes 4194304 | tf_op jit(solution)/shard_map/cond/branch_1_fun/all_to_all | solution.py:30
  28.1 5.2 %convolution_convert_fusion.8 = bf16[1024,1024]{1,0:T(8,128)(2,1)} fusion(bf16[1024,1024]{1,0:T(8,128)(2,1)} %bitcast.55, bf16[1024,1024]{1,0:T(8,128)(2,1)S(1)} %copy-done), kind=kOutput, calls=%fused_computation.10 | convolution fusion | flops 2148532224 | bytes 6291456 | tf_op jit(solution)/shard_map/dot_general | solution.py:38
  33.3 6.8 %all-to-all-start.2 = ((bf16[8,128,1024]{2,1,0:T(8,128)(2,1)}), bf16[8,128,1024]{2,1,0:T(8,128)(2,1)}, u32[]{:S(2)}, u32[]{:S(2)}) async-start(bf16[8,128,1024]{2,1,0:T(8,128)(2,1)} %bitcast.63), calls=%async_computation.2 | async-start | bytes 4194304 | tf_op jit(solution)/shard_map/all_to_all | solution.py:34
  41.5 20.4 %all-to-all-done.2 = bf16[8,128,1024]{2,1,0:T(8,128)(2,1)} async-done(((bf16[8,128,1024]{2,1,0:T(8,128)(2,1)}), bf16[8,128,1024]{2,1,0:T(8,128)(2,1)}, u32[]{:S(2)}, u32[]{:S(2)}) %all-to-all-start.2) | async-done | bytes 2097184 | tf_op jit(solution)/shard_map/all_to_all | solution.py:34
  64.3 33.3 %all_to_all.45 = bf16[8,152,1024]{2,1,0:T(8,128)(2,1)S(1)} all-to-all(bf16[8,152,1024]{2,1,0:T(8,128)(2,1)S(1)} %broadcast_in_dim.45), channel_id=1, replica_groups=mesh['dp'=2,'row'=8,'col'=8] {'row'}, dimensions={0} | all-to-all | bytes 4980736 | tf_op jit(solution)/shard_map/all_to_all | solution.py:30
  100.5 6.3 %convolution_convert_fusion = bf16[1216,1792]{1,0:T(8,128)(2,1)} fusion(bf16[1216,1024]{1,0:T(8,128)(2,1)S(1)} %bitcast.56, bf16[1024,1792]{1,0:T(8,128)(2,1)S(1)} %copy-done.10), kind=kOutput, calls=%fused_computation.1 | convolution fusion | flops 4464918528 | bytes 10518528 | tf_op jit(solution)/shard_map/dot_general | solution.py:38
  107.7 4.6 %all-to-all-start.4 = ((bf16[8,152,1792]{2,1,0:T(8,128)(2,1)}), bf16[8,152,1792]{2,1,0:T(8,128)(2,1)}, u32[]{:S(2)}, u32[]{:S(2)}) async-start(bf16[8,152,1792]{2,1,0:T(8,128)(2,1)} %constant_dynamic-update-slice_fusion.1), calls=%async_computation.4 | async-start | bytes 8716288 | tf_op jit(solution)/shard_map/all_to_all | solution.py:34
  113.0 28.6 %all-to-all-done.4 = bf16[8,152,1792]{2,1,0:T(8,128)(2,1)} async-done(((bf16[8,152,1792]{2,1,0:T(8,128)(2,1)}), bf16[8,152,1792]{2,1,0:T(8,128)(2,1)}, u32[]{:S(2)}, u32[]{:S(2)}) %all-to-all-start.4) | async-done | bytes 4358176 | tf_op jit(solution)/shard_map/all_to_all | solution.py:34
  141.6 3.0 %convert_reduce_fusion = f32[152,1792]{1,0:T(8,128)S(1)} fusion(bf16[8,152,1792]{2,1,0:T(8,128)(2,1)} %all-to-all-done.4), kind=kLoop, calls=%fused_computation | loop fusion | flops 4085760 | bytes 5447680 | tf_op jit(solution)/shard_map/reduce_sum | solution.py:34
  147.6 4.6 %all-to-all-start.5 = ((bf16[8,152,1792]{2,1,0:T(8,128)(2,1)}), bf16[8,152,1792]{2,1,0:T(8,128)(2,1)}, u32[]{:S(2)}, u32[]{:S(2)}) async-start(bf16[8,152,1792]{2,1,0:T(8,128)(2,1)} %broadcast_in_dim.48), calls=%async_computation.5 | async-start | bytes 8716288 | tf_op jit(solution)/shard_map/all_to_all | solution.py:30
  157.3 33.6 %all-to-all-done.5 = bf16[8,152,1792]{2,1,0:T(8,128)(2,1)} async-done(((bf16[8,152,1792]{2,1,0:T(8,128)(2,1)}), bf16[8,152,1792]{2,1,0:T(8,128)(2,1)}, u32[]{:S(2)}, u32[]{:S(2)}) %all-to-all-start.5) | async-done | bytes 4358176 | tf_op jit(solution)/shard_map/all_to_all | solution.py:30
  192.9 3.7 %convolution_convert_fusion.10 = bf16[192,1024]{1,0:T(8,128)(2,1)S(1)} fusion(bf16[192,1792]{1,0:T(8,128)(2,1)} %bitcast.12, bf16[1024,1792]{1,0:T(8,128)(2,1)} %param.12), kind=kOutput, calls=%fused_computation.23 | convolution fusion | flops 704839680 | bytes 4751360 | tf_op jit(solution)/shard_map/dot_general | solution.py:38
  196.6 8.2 %convolution_convert_fusion.3 = bf16[1216,1024]{1,0:T(8,128)(2,1)} fusion(bf16[1216,1792]{1,0:T(8,128)(2,1)} %bitcast.10, bf16[1792,1024]{1,0:T(8,128)(2,1)S(1)} %copy-done.4), kind=kOutput, calls=%fused_computation.4 | convolution fusion | flops 4463984640 | bytes 10518528 | tf_op jit(solution)/shard_map/dot_general | solution.py:38
  205.6 4.6 %all-to-all-start.6 = ((bf16[8,152,1024]{2,1,0:T(8,128)(2,1)}), bf16[8,152,1024]{2,1,0:T(8,128)(2,1)}, u32[]{:S(2)}, u32[]{:S(2)}) async-start(bf16[8,152,1024]{2,1,0:T(8,128)(2,1)} %constant_dynamic-update-slice_fusion), calls=%async_computation.6 | async-start | bytes 4980736 | tf_op jit(solution)/shard_map/all_to_all | solution.py:34
  210.2 25.2 %collective-permute-start.6 = (bf16[192,1024]{1,0:T(8,128)(2,1)}, bf16[192,1024]{1,0:T(8,128)(2,1)S(1)}, u32[]{:S(2)}, u32[]{:S(2)}) collective-permute-start(bf16[192,1024]{1,0:T(8,128)(2,1)} %bitcast.19), channel_id=1, source_target_pairs={{0,64},{64,0},{1,65},{65,1},{2,66},{66,2},{3,67},{67,3},{4,68},{68... | collective-permute-start | bytes 1179656 | tf_op jit(solution)/shard_map/ppermute | solution.py:75
  235.8 3.0 %convolution_convert_fusion.4 = bf16[8,24,1792]{2,1,0:T(8,128)(2,1)S(1)} fusion(bf16[8,24,152]{2,1,0:T(8,128)(2,1)S(1)} %fusion.26, bf16[8,152,1792]{2,1,0:T(8,128)(2,1)} %all-to-all-done.5), kind=kOutput, calls=%fused_computation.5 | convolution fusion | flops 104939520 | bytes 5104640 | tf_op jit(solution)/shard_map/dot_general | solution.py:59
  247.2 6.7 %all-to-all-start.7 = ((bf16[8,24,1024]{2,1,0:T(8,128)(2,1)}), bf16[8,24,1024]{2,1,0:T(8,128)(2,1)S(1)}, u32[]{:S(2)}, u32[]{:S(2)}) async-start(bf16[8,24,1024]{2,1,0:T(8,128)(2,1)} %broadcast_in_dim.49), calls=%async_computation.7 | async-start | bytes 786432 | tf_op jit(solution)/shard_map/all_to_all | solution.py:30
  255.3 3.9 %convolution_convert_fusion.2 = bf16[1792,1024]{1,0:T(8,128)(2,1)} fusion(bf16[192,1792]{1,0:T(8,128)(2,1)S(1)} %get-tuple-element.44, bf16[192,1792]{1,0:T(8,128)(2,1)S(1)} %get-tuple-element.43, bf16[192,1024]{1,0:T(8,128)(2,1)S(1)} %copy-done.8, bf16[192,1024]{1,0:T(8,128)(2,1)S(1)} %copy-done.7), kind=kOutput, calls=%fused_computation.3 | convolution fusion | flops 1415446528 | bytes 5832704 | tf_op jit(solution)/shard_map/dot_general | solution.py:83
  259.3 4.2 %all-to-all-done.7 = bf16[8,24,1024]{2,1,0:T(8,128)(2,1)S(1)} async-done(((bf16[8,24,1024]{2,1,0:T(8,128)(2,1)}), bf16[8,24,1024]{2,1,0:T(8,128)(2,1)S(1)}, u32[]{:S(2)}, u32[]{:S(2)}) %all-to-all-start.7) | async-done | bytes 393248 | tf_op jit(solution)/shard_map/all_to_all | solution.py:30
  265.1 3.7 %all-to-all-start.8 = ((bf16[8,24,1024]{2,1,0:T(8,128)(2,1)}), bf16[8,24,1024]{2,1,0:T(8,128)(2,1)S(1)}, u32[]{:S(2)}, u32[]{:S(2)}) async-start(bf16[8,24,1024]{2,1,0:T(8,128)(2,1)} %bitcast.17), calls=%async_computation.8 | async-start | bytes 786432 | tf_op jit(solution)/shard_map/all_to_all | solution.py:34
  270.3 6.0 %collective-permute-start.5 = (bf16[192,1024]{1,0:T(8,128)(2,1)S(1)}, bf16[192,1024]{1,0:T(8,128)(2,1)}, u32[]{:S(2)}, u32[]{:S(2)}) collective-permute-start(bf16[192,1024]{1,0:T(8,128)(2,1)S(1)} %bitcast.60), channel_id=1, source_target_pairs={{0,64},{64,0},{1,65},{65,1},{2,66},{66,2},{3,67},{67,3},{4,68},{68... | collective-permute-start | bytes 1179656 | tf_op jit(solution)/shard_map/ppermute | solution.py:75
  276.3 3.9 %convolution_convert_fusion.1 = bf16[1024,1792]{1,0:T(8,128)(2,1)} fusion(bf16[192,1792]{1,0:T(8,128)(2,1)S(1)} %get-tuple-element.42, bf16[192,1792]{1,0:T(8,128)(2,1)S(1)} %get-tuple-element.41, bf16[192,1024]{1,0:T(8,128)(2,1)S(1)} %copy-done.6, bf16[192,1024]{1,0:T(8,128)(2,1)S(1)} %copy-done.5), kind=kOutput, calls=%fused_computation.2 | convolution fusion | flops 1415446528 | bytes 5832704 | tf_op jit(solution)/shard_map/dot_general | solution.py:83
  283.1 3.7 %convolution_convert_fusion.7 = bf16[1024,1024]{1,0:T(8,128)(2,1)} fusion(bf16[192,1024]{1,0:T(8,128)(2,1)} %get-tuple-element.50, bf16[192,1024]{1,0:T(8,128)(2,1)} %get-tuple-element.49, bf16[192,1024]{1,0:T(8,128)(2,1)S(1)} %get-tuple-element.48, bf16[192,1024]{1,0:T(8,128)(2,1)S(1)} %get-tuple-element.47), kind=kOutput, calls=%fused_computation.9 | convolution fusion | flops 809500672 | bytes 3670016 | tf_op jit(solution)/shard_map/dot_general | solution.py:83
  (80 shorter events, 38.7 us)
Async XLA Ops:
  0.6 27.5 %copy-start = (bf16[1024,1024]{1,0:T(8,128)(2,1)S(1)}, bf16[1024,1024]{1,0:T(8,128)(2,1)}, u32[]{:S(2)}) copy-start(bf16[1024,1024]{1,0:T(8,128)(2,1)} %param.11) | copy-start | bytes 6291460
  26.0 2.1 collective-permute-start
  33.3 6.8 %copy-start.11 = (s32[1,20]{1,0:T(1,128)S(1)}, s32[1,20]{1,0:T(1,128)}, u32[]{:S(2)}) copy-start(s32[1,20]{1,0:T(1,128)} %param.15) | copy-start | bytes 244
  33.3 8.0 %copy-start.9 = (bf16[128,1024]{1,0:T(8,128)(2,1)S(1)}, bf16[128,1024]{1,0:T(8,128)(2,1)}, u32[]{:S(2)}) copy-start(bf16[128,1024]{1,0:T(8,128)(2,1)} %param.14) | copy-start | bytes 786436
  33.3 28.6 %all-to-all-start.2 = ((bf16[8,128,1024]{2,1,0:T(8,128)(2,1)}), bf16[8,128,1024]{2,1,0:T(8,128)(2,1)}, u32[]{:S(2)}, u32[]{:S(2)}) async-start(bf16[8,128,1024]{2,1,0:T(8,128)(2,1)} %bitcast.63), calls=%async_computation.2 | async-start | bytes 4194304 | tf_op jit(solution)/shard_map/all_to_all | solution.py:34
  64.2 33.3 %copy-start.3 = (bf16[1792,1024]{1,0:T(8,128)(2,1)S(1)}, bf16[1792,1024]{1,0:T(8,128)(2,1)}, u32[]{:S(2)}) copy-start(bf16[1792,1024]{1,0:T(8,128)(2,1)} %param.13) | copy-start | bytes 11010052
  97.5 1.4 copy-start.1
  97.6 2.9 %copy-start.10 = (bf16[1024,1792]{1,0:T(8,128)(2,1)S(1)}, bf16[1024,1792]{1,0:T(8,128)(2,1)}, u32[]{:S(2)}) copy-start(bf16[1024,1792]{1,0:T(8,128)(2,1)} %param.12) | copy-start | bytes 11010052
  107.7 33.9 %all-to-all-start.4 = ((bf16[8,152,1792]{2,1,0:T(8,128)(2,1)}), bf16[8,152,1792]{2,1,0:T(8,128)(2,1)}, u32[]{:S(2)}, u32[]{:S(2)}) async-start(bf16[8,152,1792]{2,1,0:T(8,128)(2,1)} %constant_dynamic-update-slice_fusion.1), calls=%async_computation.4 | async-start | bytes 8716288 | tf_op jit(solution)/shard_map/all_to_all | solution.py:34
  112.3 0.7 collective-permute-start.1
  147.6 43.3 %all-to-all-start.5 = ((bf16[8,152,1792]{2,1,0:T(8,128)(2,1)}), bf16[8,152,1792]{2,1,0:T(8,128)(2,1)}, u32[]{:S(2)}, u32[]{:S(2)}) async-start(bf16[8,152,1792]{2,1,0:T(8,128)(2,1)} %broadcast_in_dim.48), calls=%async_computation.5 | async-start | bytes 8716288 | tf_op jit(solution)/shard_map/all_to_all | solution.py:30
  152.2 3.8 %copy-start.2 = (bf16[8,152,1024]{2,1,0:T(8,128)(2,1)S(1)}, bf16[8,152,1024]{2,1,0:T(8,128)(2,1)}, u32[]{:S(2)}) copy-start(bf16[8,152,1024]{2,1,0:T(8,128)(2,1)} %copy-done.1) | copy-start | bytes 7471108
  192.9 3.7 %copy-start.4 = (bf16[1792,1024]{1,0:T(8,128)(2,1)S(1)}, bf16[1792,1024]{1,0:T(8,128)(2,1)}, u32[]{:S(2)}) copy-start(bf16[1792,1024]{1,0:T(8,128)(2,1)} %param.13) | copy-start | bytes 11010052
  205.6 38.7 %all-to-all-start.6 = ((bf16[8,152,1024]{2,1,0:T(8,128)(2,1)}), bf16[8,152,1024]{2,1,0:T(8,128)(2,1)}, u32[]{:S(2)}, u32[]{:S(2)}) async-start(bf16[8,152,1024]{2,1,0:T(8,128)(2,1)} %constant_dynamic-update-slice_fusion), calls=%async_computation.6 | async-start | bytes 4980736 | tf_op jit(solution)/shard_map/all_to_all | solution.py:34
  210.2 29.2 %collective-permute-start.6 = (bf16[192,1024]{1,0:T(8,128)(2,1)}, bf16[192,1024]{1,0:T(8,128)(2,1)S(1)}, u32[]{:S(2)}, u32[]{:S(2)}) collective-permute-start(bf16[192,1024]{1,0:T(8,128)(2,1)} %bitcast.19), channel_id=1, source_target_pairs={{0,64},{64,0},{1,65},{65,1},{2,66},{66,2},{3,67},{67,3},{4,68},{68... | collective-permute-start | bytes 1179656 | tf_op jit(solution)/shard_map/ppermute | solution.py:75
  235.3 6.0 %collective-permute-start.4 = (bf16[192,1024]{1,0:T(8,128)(2,1)}, bf16[192,1024]{1,0:T(8,128)(2,1)S(1)}, u32[]{:S(2)}, u32[]{:S(2)}) collective-permute-start(bf16[192,1024]{1,0:T(8,128)(2,1)} %bitcast.18), channel_id=1, source_target_pairs={{0,64},{64,0},{1,65},{65,1},{2,66},{66,2},{3,67},{67,3},{4,68},{68... | collective-permute-start | bytes 1179656 | tf_op jit(solution)/shard_map/ppermute | solution.py:75
  235.4 7.9 %collective-permute-start.3 = (bf16[192,1024]{1,0:T(8,128)(2,1)S(1)}, bf16[192,1024]{1,0:T(8,128)(2,1)S(1)}, u32[]{:S(2)}, u32[]{:S(2)}) collective-permute-start(bf16[192,1024]{1,0:T(8,128)(2,1)S(1)} %bitcast.58), channel_id=1, source_target_pairs={{0,64},{64,0},{1,65},{65,1},{2,66},{66,2},{3,67},{67,3},{4,68},{68... | collective-permute-start | bytes 1179656 | tf_op jit(solution)/shard_map/ppermute | solution.py:75
  238.8 15.2 %collective-permute-start.2 = (bf16[192,1792]{1,0:T(8,128)(2,1)S(1)}, bf16[192,1792]{1,0:T(8,128)(2,1)}, u32[]{:S(2)}, u32[]{:S(2)}) collective-permute-start(bf16[192,1792]{1,0:T(8,128)(2,1)S(1)} %bitcast.61), channel_id=1, source_target_pairs={{0,64},{64,0},{1,65},{65,1},{2,66},{66,2},{3,67},{67,3},{4,68},{68... | collective-permute-start | bytes 2064392 | tf_op jit(solution)/shard_map/ppermute | solution.py:75
  239.0 29.8 %collective-permute-start.7 = (bf16[192,1792]{1,0:T(8,128)(2,1)}, bf16[192,1792]{1,0:T(8,128)(2,1)}, u32[]{:S(2)}, u32[]{:S(2)}) collective-permute-start(bf16[192,1792]{1,0:T(8,128)(2,1)} %bitcast.20), channel_id=1, source_target_pairs={{0,64},{64,0},{1,65},{65,1},{2,66},{66,2},{3,67},{67,3},{4,68},{68... | collective-permute-start | bytes 2064392 | tf_op jit(solution)/shard_map/ppermute | solution.py:75
  247.2 16.2 %all-to-all-start.7 = ((bf16[8,24,1024]{2,1,0:T(8,128)(2,1)}), bf16[8,24,1024]{2,1,0:T(8,128)(2,1)S(1)}, u32[]{:S(2)}, u32[]{:S(2)}) async-start(bf16[8,24,1024]{2,1,0:T(8,128)(2,1)} %broadcast_in_dim.49), calls=%async_computation.7 | async-start | bytes 786432 | tf_op jit(solution)/shard_map/all_to_all | solution.py:30
  265.1 15.8 %all-to-all-start.8 = ((bf16[8,24,1024]{2,1,0:T(8,128)(2,1)}), bf16[8,24,1024]{2,1,0:T(8,128)(2,1)S(1)}, u32[]{:S(2)}, u32[]{:S(2)}) async-start(bf16[8,24,1024]{2,1,0:T(8,128)(2,1)} %bitcast.17), calls=%async_computation.8 | async-start | bytes 786432 | tf_op jit(solution)/shard_map/all_to_all | solution.py:34
  268.8 7.5 %copy-start.5 = (bf16[192,1024]{1,0:T(8,128)(2,1)S(1)}, bf16[192,1024]{1,0:T(8,128)(2,1)}, u32[]{:S(2)}) copy-start(bf16[192,1024]{1,0:T(8,128)(2,1)} %get-tuple-element.45) | copy-start | bytes 1179652
  268.8 7.5 %copy-start.6 = (bf16[192,1024]{1,0:T(8,128)(2,1)S(1)}, bf16[192,1024]{1,0:T(8,128)(2,1)}, u32[]{:S(2)}) copy-start(bf16[192,1024]{1,0:T(8,128)(2,1)} %get-tuple-element.46) | copy-start | bytes 1179652
  270.3 11.8 %collective-permute-start.5 = (bf16[192,1024]{1,0:T(8,128)(2,1)S(1)}, bf16[192,1024]{1,0:T(8,128)(2,1)}, u32[]{:S(2)}, u32[]{:S(2)}) collective-permute-start(bf16[192,1024]{1,0:T(8,128)(2,1)S(1)} %bitcast.60), channel_id=1, source_target_pairs={{0,64},{64,0},{1,65},{65,1},{2,66},{66,2},{3,67},{67,3},{4,68},{68... | collective-permute-start | bytes 1179656 | tf_op jit(solution)/shard_map/ppermute | solution.py:75
  (2 other events, 2.6 us)

commit v7 on v6

--- a/solution.py
+++ b/solution.py
@@ -120,9 +120,9 @@
     grad_full = row_full[:, SEQ:]
     positions = grad_full[:, MASKED, :MASKED].astype(jnp.int32)
     up_part = replace_tail(product(row_full, up_weight, 0), product(grad_full, down_weight, 1))
-    hidden_sum = scatter_sum(up_part, "col")
-    pre_act = hidden_sum[:SEQ].astype(jnp.bfloat16)
-    grad_act = hidden_sum[SEQ:]
+    terms = lax.all_to_all(up_part, "col", 0, 0)
+    pre_act = jnp.sum(terms[:, :SEQ].astype(jnp.float32), axis=0).astype(jnp.bfloat16)
+    grad_act = jnp.sum(terms[:, SEQ:].astype(jnp.float32), axis=0)
     act = gelu(pre_act.astype(jnp.float32)).astype(jnp.bfloat16)
     col_heads = heads(col_pos[0], SEQ)
     slope = gelu_slope(select(col_heads, pre_act, 1).astype(jnp.float32))

time: 290 us -> 291 us (level)
    all_to_all x0 -> x1, waiting for transfers between devices: none -> 28.6 us  [body(): terms = lax.all_to_all(up_part, 'col', 0, 0)]
    all_to_all x4 -> x3, waiting for transfers between devices: 49 us -> 20.4 us  [scatter_sum(): lax.all_to_all(blocks, axis, 0, 0).astype(jnp.float32)]
    all_to_all x0 -> x1, starting transfers between devices: none -> 4.58 us  [body(): terms = lax.all_to_all(up_part, 'col', 0, 0)]
    reduce_sum x0 -> x2, other arithmetic: none -> 3.74 us  [the longest x1 2.53 us: body(): jnp.sum(terms[:, :SEQ].astype(jnp.float32), axis=0).astype(jnp.bfloat16)]
    all_to_all x4 -> x3, starting transfers between devices: 19.6 us -> 16 us  [scatter_sum(): lax.all_to_all(blocks, axis, 0, 0).astype(jnp.float32)]
    reduce_sum x4 -> x3, other arithmetic: 7.16 us -> 4.2 us  [scatter_sum(): jnp.sum(lax.all_to_all(blocks, axis, 0, 0).astype(jnp.float32), axis=0)]
where the time goes in v7:
time: 291 us; the launch traced here: 288 us
  waiting for transfers between devices  86.9 us (30%)
  starting transfers between devices  66.7 us (23%)
  blocking collectives  56.6 us (19%)
  matrix products  46.6 us (16%)
  other arithmetic  17.1 us (6%)
  local copies, waits for them, and re-layouts  12.9 us (4%)
    all_to_all x2, blocking collectives, gather(): return lax.all_to_all(copies, axis, 0, 0)  56.6 us
    all_to_all x2, waiting for transfers between devices, gather(): return lax.all_to_all(copies, axis, 0, 0)  37.1 us
    ppermute x6, starting transfers between devices, both_replicas(): other = lax.ppermute(values, 'dp', CORES)  33.1 us
    all_to_all x1, waiting for transfers between devices, body(): terms = lax.all_to_all(up_part, 'col', 0, 0)  28.6 us
    dot_general x6, matrix products, product(): lax.dot_general(flat(blocks), weight, (((1,), (contract,)), ((), ())), pr...  26.4 us
    all_to_all x3, waiting for transfers between devices, scatter_sum(): lax.all_to_all(blocks, axis, 0, 0).astype(jnp.float32)  20.4 us
    all_to_all x3, starting transfers between devices, scatter_sum(): lax.all_to_all(blocks, axis, 0, 0).astype(jnp.float32)  16 us
    dot_general x3, matrix products, token_product(): lax.dot_general(both_replicas(flat(left), core), both_replicas(flat(right...  11.6 us
  transfers between devices with their start and end apart: 14, of which 5 were waited for; matrix products, arithmetic and copies ran while one was open for 11% of the time, Pallas kernels for 0%

profile of v7, /device:TPU:0, one launch (start us, length us, event | category | flops | bytes accessed | tf_op | source)
XLA Modules:
  0.0 288.4 jit_solution(14910118139175776965)
XLA Ops:
  0.7 24.7 %conditional.2 = (bf16[8,128,1024]{2,1,0:T(8,128)(2,1)}) conditional(s32[]{:T(128)} %convert_element_type.87, bf16[128,1024]{1,0:T(8,128)(2,1)} %param.10, bf16[128,1024]{1,0:T(8,128)(2,1)} %param.10), branch_computations={%region_0.0_spmd, %region_1.0_spmd} | conditional | bytes 6553608 | solution.py:97
  2.0 23.3 %all_to_all.43 = bf16[8,128,1024]{2,1,0:T(8,128)(2,1)} all-to-all(bf16[8,128,1024]{2,1,0:T(8,128)(2,1)S(1)} %broadcast_in_dim.29), channel_id=1, replica_groups=mesh['dp'=2,'row'=8,'col'=8] {'col'}, dimensions={0} | all-to-all | bytes 4194304 | tf_op jit(solution)/shard_map/cond/branch_1_fun/all_to_all | solution.py:30
  28.1 5.2 %convolution_convert_fusion.8 = bf16[1024,1024]{1,0:T(8,128)(2,1)} fusion(bf16[1024,1024]{1,0:T(8,128)(2,1)} %bitcast.56, bf16[1024,1024]{1,0:T(8,128)(2,1)S(1)} %copy-done), kind=kOutput, calls=%fused_computation.10 | convolution fusion | flops 2148532224 | bytes 6291456 | tf_op jit(solution)/shard_map/dot_general | solution.py:38
  33.4 6.8 %all-to-all-start.2 = ((bf16[8,128,1024]{2,1,0:T(8,128)(2,1)}), bf16[8,128,1024]{2,1,0:T(8,128)(2,1)}, u32[]{:S(2)}, u32[]{:S(2)}) async-start(bf16[8,128,1024]{2,1,0:T(8,128)(2,1)} %bitcast.64), calls=%async_computation.2 | async-start | bytes 4194304 | tf_op jit(solution)/shard_map/all_to_all | solution.py:34
  41.5 20.4 %all-to-all-done.2 = bf16[8,128,1024]{2,1,0:T(8,128)(2,1)} async-done(((bf16[8,128,1024]{2,1,0:T(8,128)(2,1)}), bf16[8,128,1024]{2,1,0:T(8,128)(2,1)}, u32[]{:S(2)}, u32[]{:S(2)}) %all-to-all-start.2) | async-done | bytes 2097184 | tf_op jit(solution)/shard_map/all_to_all | solution.py:34
  64.3 33.3 %all_to_all.45 = bf16[8,152,1024]{2,1,0:T(8,128)(2,1)S(1)} all-to-all(bf16[8,152,1024]{2,1,0:T(8,128)(2,1)S(1)} %broadcast_in_dim.45), channel_id=1, replica_groups=mesh['dp'=2,'row'=8,'col'=8] {'row'}, dimensions={0} | all-to-all | bytes 4980736 | tf_op jit(solution)/shard_map/all_to_all | solution.py:30
  100.5 6.3 %convolution_convert_fusion = bf16[1216,1792]{1,0:T(8,128)(2,1)} fusion(bf16[1216,1024]{1,0:T(8,128)(2,1)S(1)} %bitcast.57, bf16[1024,1792]{1,0:T(8,128)(2,1)S(1)} %copy-done.10), kind=kOutput, calls=%fused_computation | convolution fusion | flops 4464918528 | bytes 10518528 | tf_op jit(solution)/shard_map/dot_general | solution.py:38
  107.7 4.6 %all-to-all-start.4 = ((bf16[8,152,1792]{2,1,0:T(8,128)(2,1)}), bf16[8,152,1792]{2,1,0:T(8,128)(2,1)}, u32[]{:S(2)}, u32[]{:S(2)}) async-start(bf16[8,152,1792]{2,1,0:T(8,128)(2,1)} %constant_dynamic-update-slice_fusion.1), calls=%async_computation.4 | async-start | bytes 8716288 | tf_op jit(solution)/shard_map/all_to_all | solution.py:123
  113.0 28.6 %all-to-all-done.4 = bf16[8,152,1792]{2,1,0:T(8,128)(2,1)} async-done(((bf16[8,152,1792]{2,1,0:T(8,128)(2,1)}), bf16[8,152,1792]{2,1,0:T(8,128)(2,1)}, u32[]{:S(2)}, u32[]{:S(2)}) %all-to-all-start.4) | async-done | bytes 4358176 | tf_op jit(solution)/shard_map/all_to_all | solution.py:123
  148.4 4.6 %all-to-all-start.5 = ((bf16[8,152,1792]{2,1,0:T(8,128)(2,1)}), bf16[8,152,1792]{2,1,0:T(8,128)(2,1)}, u32[]{:S(2)}, u32[]{:S(2)}) async-start(bf16[8,152,1792]{2,1,0:T(8,128)(2,1)} %broadcast_in_dim.48), calls=%async_computation.5 | async-start | bytes 8716288 | tf_op jit(solution)/shard_map/all_to_all | solution.py:30
  154.0 2.8 convolution_convert_fusion.12
  158.1 32.8 %all-to-all-done.5 = bf16[8,152,1792]{2,1,0:T(8,128)(2,1)} async-done(((bf16[8,152,1792]{2,1,0:T(8,128)(2,1)}), bf16[8,152,1792]{2,1,0:T(8,128)(2,1)}, u32[]{:S(2)}, u32[]{:S(2)}) %all-to-all-start.5) | async-done | bytes 4358176 | tf_op jit(solution)/shard_map/all_to_all | solution.py:30
  192.9 3.7 %convolution_convert_fusion.10 = bf16[192,1024]{1,0:T(8,128)(2,1)S(1)} fusion(bf16[192,1792]{1,0:T(8,128)(2,1)} %bitcast.12, bf16[1024,1792]{1,0:T(8,128)(2,1)} %param.12), kind=kOutput, calls=%fused_computation.24 | convolution fusion | flops 704839680 | bytes 4751360 | tf_op jit(solution)/shard_map/dot_general | solution.py:38
  196.6 8.2 %convolution_convert_fusion.3 = bf16[1216,1024]{1,0:T(8,128)(2,1)} fusion(bf16[1216,1792]{1,0:T(8,128)(2,1)} %bitcast.10, bf16[1792,1024]{1,0:T(8,128)(2,1)S(1)} %copy-done.4), kind=kOutput, calls=%fused_computation.3 | convolution fusion | flops 4463984640 | bytes 10518528 | tf_op jit(solution)/shard_map/dot_general | solution.py:38
  205.6 4.4 %all-to-all-start.6 = ((bf16[8,152,1024]{2,1,0:T(8,128)(2,1)}), bf16[8,152,1024]{2,1,0:T(8,128)(2,1)}, u32[]{:S(2)}, u32[]{:S(2)}) async-start(bf16[8,152,1024]{2,1,0:T(8,128)(2,1)} %constant_dynamic-update-slice_fusion), calls=%async_computation.6 | async-start | bytes 4980736 | tf_op jit(solution)/shard_map/all_to_all | solution.py:34
  210.0 26.1 %collective-permute-start.6 = (bf16[192,1024]{1,0:T(8,128)(2,1)}, bf16[192,1024]{1,0:T(8,128)(2,1)S(1)}, u32[]{:S(2)}, u32[]{:S(2)}) collective-permute-start(bf16[192,1024]{1,0:T(8,128)(2,1)} %bitcast.19), channel_id=1, source_target_pairs={{0,64},{64,0},{1,65},{65,1},{2,66},{66,2},{3,67},{67,3},{4,68},{68... | collective-permute-start | bytes 1179656 | tf_op jit(solution)/shard_map/ppermute | solution.py:75
  236.6 3.0 %convolution_convert_fusion.4 = bf16[8,24,1792]{2,1,0:T(8,128)(2,1)S(1)} fusion(bf16[8,24,152]{2,1,0:T(8,128)(2,1)S(1)} %fusion.26, bf16[8,152,1792]{2,1,0:T(8,128)(2,1)} %all-to-all-done.5), kind=kOutput, calls=%fused_computation.5 | convolution fusion | flops 104939520 | bytes 5104640 | tf_op jit(solution)/shard_map/dot_general | solution.py:59
  248.0 6.6 %all-to-all-start.7 = ((bf16[8,24,1024]{2,1,0:T(8,128)(2,1)}), bf16[8,24,1024]{2,1,0:T(8,128)(2,1)S(1)}, u32[]{:S(2)}, u32[]{:S(2)}) async-start(bf16[8,24,1024]{2,1,0:T(8,128)(2,1)} %broadcast_in_dim.49), calls=%async_computation.7 | async-start | bytes 786432 | tf_op jit(solution)/shard_map/all_to_all | solution.py:30
  255.8 3.9 %convolution_convert_fusion.2 = bf16[1792,1024]{1,0:T(8,128)(2,1)} fusion(bf16[192,1792]{1,0:T(8,128)(2,1)S(1)} %get-tuple-element.44, bf16[192,1792]{1,0:T(8,128)(2,1)S(1)} %get-tuple-element.43, bf16[192,1024]{1,0:T(8,128)(2,1)S(1)} %copy-done.8, bf16[192,1024]{1,0:T(8,128)(2,1)S(1)} %copy-done.7), kind=kOutput, calls=%fused_computation.2 | convolution fusion | flops 1415446528 | bytes 5832704 | tf_op jit(solution)/shard_map/dot_general | solution.py:83
  259.8 4.2 %all-to-all-done.7 = bf16[8,24,1024]{2,1,0:T(8,128)(2,1)S(1)} async-done(((bf16[8,24,1024]{2,1,0:T(8,128)(2,1)}), bf16[8,24,1024]{2,1,0:T(8,128)(2,1)S(1)}, u32[]{:S(2)}, u32[]{:S(2)}) %all-to-all-start.7) | async-done | bytes 393248 | tf_op jit(solution)/shard_map/all_to_all | solution.py:30
  265.6 4.8 %all-to-all-start.8 = ((bf16[8,24,1024]{2,1,0:T(8,128)(2,1)}), bf16[8,24,1024]{2,1,0:T(8,128)(2,1)S(1)}, u32[]{:S(2)}, u32[]{:S(2)}) async-start(bf16[8,24,1024]{2,1,0:T(8,128)(2,1)} %bitcast.17), calls=%async_computation.8 | async-start | bytes 786432 | tf_op jit(solution)/shard_map/all_to_all | solution.py:34
  271.9 5.9 %collective-permute-start.5 = (bf16[192,1024]{1,0:T(8,128)(2,1)S(1)}, bf16[192,1024]{1,0:T(8,128)(2,1)}, u32[]{:S(2)}, u32[]{:S(2)}) collective-permute-start(bf16[192,1024]{1,0:T(8,128)(2,1)S(1)} %bitcast.61), channel_id=1, source_target_pairs={{0,64},{64,0},{1,65},{65,1},{2,66},{66,2},{3,67},{67,3},{4,68},{68... | collective-permute-start | bytes 1179656 | tf_op jit(solution)/shard_map/ppermute | solution.py:75
  277.9 3.9 %convolution_convert_fusion.1 = bf16[1024,1792]{1,0:T(8,128)(2,1)} fusion(bf16[192,1792]{1,0:T(8,128)(2,1)S(1)} %get-tuple-element.42, bf16[192,1792]{1,0:T(8,128)(2,1)S(1)} %get-tuple-element.41, bf16[192,1024]{1,0:T(8,128)(2,1)S(1)} %copy-done.6, bf16[192,1024]{1,0:T(8,128)(2,1)S(1)} %copy-done.5), kind=kOutput, calls=%fused_computation.1 | convolution fusion | flops 1415446528 | bytes 5832704 | tf_op jit(solution)/shard_map/dot_general | solution.py:83
  284.7 3.7 %convolution_convert_fusion.7 = bf16[1024,1024]{1,0:T(8,128)(2,1)} fusion(bf16[192,1024]{1,0:T(8,128)(2,1)} %get-tuple-element.50, bf16[192,1024]{1,0:T(8,128)(2,1)} %get-tuple-element.49, bf16[192,1024]{1,0:T(8,128)(2,1)S(1)} %get-tuple-element.48, bf16[192,1024]{1,0:T(8,128)(2,1)S(1)} %get-tuple-element.47), kind=kOutput, calls=%fused_computation.9 | convolution fusion | flops 809500672 | bytes 3670016 | tf_op jit(solution)/shard_map/dot_general | solution.py:83
  (81 shorter events, 39.7 us)
Async XLA Ops:
  0.6 27.5 %copy-start = (bf16[1024,1024]{1,0:T(8,128)(2,1)S(1)}, bf16[1024,1024]{1,0:T(8,128)(2,1)}, u32[]{:S(2)}) copy-start(bf16[1024,1024]{1,0:T(8,128)(2,1)} %param.11) | copy-start | bytes 6291460
  26.0 2.1 collective-permute-start
  33.4 6.8 %copy-start.11 = (s32[1,20]{1,0:T(1,128)S(1)}, s32[1,20]{1,0:T(1,128)}, u32[]{:S(2)}) copy-start(s32[1,20]{1,0:T(1,128)} %param.15) | copy-start | bytes 244
  33.4 8.0 %copy-start.9 = (bf16[128,1024]{1,0:T(8,128)(2,1)S(1)}, bf16[128,1024]{1,0:T(8,128)(2,1)}, u32[]{:S(2)}) copy-start(bf16[128,1024]{1,0:T(8,128)(2,1)} %param.14) | copy-start | bytes 786436
  33.4 28.6 %all-to-all-start.2 = ((bf16[8,128,1024]{2,1,0:T(8,128)(2,1)}), bf16[8,128,1024]{2,1,0:T(8,128)(2,1)}, u32[]{:S(2)}, u32[]{:S(2)}) async-start(bf16[8,128,1024]{2,1,0:T(8,128)(2,1)} %bitcast.64), calls=%async_computation.2 | async-start | bytes 4194304 | tf_op jit(solution)/shard_map/all_to_all | solution.py:34
  64.3 33.3 %copy-start.3 = (bf16[1792,1024]{1,0:T(8,128)(2,1)S(1)}, bf16[1792,1024]{1,0:T(8,128)(2,1)}, u32[]{:S(2)}) copy-start(bf16[1792,1024]{1,0:T(8,128)(2,1)} %param.13) | copy-start | bytes 11010052
  97.5 1.4 copy-start.1
  97.6 2.9 %copy-start.10 = (bf16[1024,1792]{1,0:T(8,128)(2,1)S(1)}, bf16[1024,1792]{1,0:T(8,128)(2,1)}, u32[]{:S(2)}) copy-start(bf16[1024,1792]{1,0:T(8,128)(2,1)} %param.12) | copy-start | bytes 11010052
  107.7 33.9 %all-to-all-start.4 = ((bf16[8,152,1792]{2,1,0:T(8,128)(2,1)}), bf16[8,152,1792]{2,1,0:T(8,128)(2,1)}, u32[]{:S(2)}, u32[]{:S(2)}) async-start(bf16[8,152,1792]{2,1,0:T(8,128)(2,1)} %constant_dynamic-update-slice_fusion.1), calls=%async_computation.4 | async-start | bytes 8716288 | tf_op jit(solution)/shard_map/all_to_all | solution.py:123
  112.3 0.7 collective-permute-start.1
  148.4 42.5 %all-to-all-start.5 = ((bf16[8,152,1792]{2,1,0:T(8,128)(2,1)}), bf16[8,152,1792]{2,1,0:T(8,128)(2,1)}, u32[]{:S(2)}, u32[]{:S(2)}) async-start(bf16[8,152,1792]{2,1,0:T(8,128)(2,1)} %broadcast_in_dim.48), calls=%async_computation.5 | async-start | bytes 8716288 | tf_op jit(solution)/shard_map/all_to_all | solution.py:30
  153.0 3.8 %copy-start.2 = (bf16[8,152,1024]{2,1,0:T(8,128)(2,1)S(1)}, bf16[8,152,1024]{2,1,0:T(8,128)(2,1)}, u32[]{:S(2)}) copy-start(bf16[8,152,1024]{2,1,0:T(8,128)(2,1)} %copy-done.1) | copy-start | bytes 7471108
  192.9 3.7 %copy-start.4 = (bf16[1792,1024]{1,0:T(8,128)(2,1)S(1)}, bf16[1792,1024]{1,0:T(8,128)(2,1)}, u32[]{:S(2)}) copy-start(bf16[1792,1024]{1,0:T(8,128)(2,1)} %param.13) | copy-start | bytes 11010052
  205.6 39.4 %all-to-all-start.6 = ((bf16[8,152,1024]{2,1,0:T(8,128)(2,1)}), bf16[8,152,1024]{2,1,0:T(8,128)(2,1)}, u32[]{:S(2)}, u32[]{:S(2)}) async-start(bf16[8,152,1024]{2,1,0:T(8,128)(2,1)} %constant_dynamic-update-slice_fusion), calls=%async_computation.6 | async-start | bytes 4980736 | tf_op jit(solution)/shard_map/all_to_all | solution.py:34
  210.0 30.1 %collective-permute-start.6 = (bf16[192,1024]{1,0:T(8,128)(2,1)}, bf16[192,1024]{1,0:T(8,128)(2,1)S(1)}, u32[]{:S(2)}, u32[]{:S(2)}) collective-permute-start(bf16[192,1024]{1,0:T(8,128)(2,1)} %bitcast.19), channel_id=1, source_target_pairs={{0,64},{64,0},{1,65},{65,1},{2,66},{66,2},{3,67},{67,3},{4,68},{68... | collective-permute-start | bytes 1179656 | tf_op jit(solution)/shard_map/ppermute | solution.py:75
  236.1 6.0 %collective-permute-start.4 = (bf16[192,1024]{1,0:T(8,128)(2,1)}, bf16[192,1024]{1,0:T(8,128)(2,1)S(1)}, u32[]{:S(2)}, u32[]{:S(2)}) collective-permute-start(bf16[192,1024]{1,0:T(8,128)(2,1)} %bitcast.18), channel_id=1, source_target_pairs={{0,64},{64,0},{1,65},{65,1},{2,66},{66,2},{3,67},{67,3},{4,68},{68... | collective-permute-start | bytes 1179656 | tf_op jit(solution)/shard_map/ppermute | solution.py:75
  236.2 7.8 %collective-permute-start.3 = (bf16[192,1024]{1,0:T(8,128)(2,1)S(1)}, bf16[192,1024]{1,0:T(8,128)(2,1)S(1)}, u32[]{:S(2)}, u32[]{:S(2)}) collective-permute-start(bf16[192,1024]{1,0:T(8,128)(2,1)S(1)} %bitcast.59), channel_id=1, source_target_pairs={{0,64},{64,0},{1,65},{65,1},{2,66},{66,2},{3,67},{67,3},{4,68},{68... | collective-permute-start | bytes 1179656 | tf_op jit(solution)/shard_map/ppermute | solution.py:75
  239.5 15.0 %collective-permute-start.2 = (bf16[192,1792]{1,0:T(8,128)(2,1)S(1)}, bf16[192,1792]{1,0:T(8,128)(2,1)}, u32[]{:S(2)}, u32[]{:S(2)}) collective-permute-start(bf16[192,1792]{1,0:T(8,128)(2,1)S(1)} %bitcast.62), channel_id=1, source_target_pairs={{0,64},{64,0},{1,65},{65,1},{2,66},{66,2},{3,67},{67,3},{4,68},{68... | collective-permute-start | bytes 2064392 | tf_op jit(solution)/shard_map/ppermute | solution.py:75
  239.7 30.7 %collective-permute-start.7 = (bf16[192,1792]{1,0:T(8,128)(2,1)}, bf16[192,1792]{1,0:T(8,128)(2,1)}, u32[]{:S(2)}, u32[]{:S(2)}) collective-permute-start(bf16[192,1792]{1,0:T(8,128)(2,1)} %bitcast.20), channel_id=1, source_target_pairs={{0,64},{64,0},{1,65},{65,1},{2,66},{66,2},{3,67},{67,3},{4,68},{68... | collective-permute-start | bytes 2064392 | tf_op jit(solution)/shard_map/ppermute | solution.py:75
  248.0 16.1 %all-to-all-start.7 = ((bf16[8,24,1024]{2,1,0:T(8,128)(2,1)}), bf16[8,24,1024]{2,1,0:T(8,128)(2,1)S(1)}, u32[]{:S(2)}, u32[]{:S(2)}) async-start(bf16[8,24,1024]{2,1,0:T(8,128)(2,1)} %broadcast_in_dim.49), calls=%async_computation.7 | async-start | bytes 786432 | tf_op jit(solution)/shard_map/all_to_all | solution.py:30
  265.6 16.9 %all-to-all-start.8 = ((bf16[8,24,1024]{2,1,0:T(8,128)(2,1)}), bf16[8,24,1024]{2,1,0:T(8,128)(2,1)S(1)}, u32[]{:S(2)}, u32[]{:S(2)}) async-start(bf16[8,24,1024]{2,1,0:T(8,128)(2,1)} %bitcast.17), calls=%async_computation.8 | async-start | bytes 786432 | tf_op jit(solution)/shard_map/all_to_all | solution.py:34
  270.4 7.4 %copy-start.5 = (bf16[192,1024]{1,0:T(8,128)(2,1)S(1)}, bf16[192,1024]{1,0:T(8,128)(2,1)}, u32[]{:S(2)}) copy-start(bf16[192,1024]{1,0:T(8,128)(2,1)} %get-tuple-element.45) | copy-start | bytes 1179652
  270.4 7.4 %copy-start.6 = (bf16[192,1024]{1,0:T(8,128)(2,1)S(1)}, bf16[192,1024]{1,0:T(8,128)(2,1)}, u32[]{:S(2)}) copy-start(bf16[192,1024]{1,0:T(8,128)(2,1)} %get-tuple-element.46) | copy-start | bytes 1179652
  271.9 11.7 %collective-permute-start.5 = (bf16[192,1024]{1,0:T(8,128)(2,1)S(1)}, bf16[192,1024]{1,0:T(8,128)(2,1)}, u32[]{:S(2)}, u32[]{:S(2)}) collective-permute-start(bf16[192,1024]{1,0:T(8,128)(2,1)S(1)} %bitcast.61), channel_id=1, source_target_pairs={{0,64},{64,0},{1,65},{65,1},{2,66},{66,2},{3,67},{67,3},{4,68},{68... | collective-permute-start | bytes 1179656 | tf_op jit(solution)/shard_map/ppermute | solution.py:75
  (2 other events, 2.6 us)
